TPU v7x, 512 devices: a whole 4x4x16 slice. The times are simulated.
512 devices in a mesh: rows: 8 (over z_hi, core), feat: 64 (over z_lo, x, y).
Axes of the slice: x: 4, y: 4, z: 16 (z_hi: 4, z_lo: 4; z = z_hi * 4 + z_lo), core: 2. Of those that a mesh axis runs over, the one named last changes fastest.
Arguments:
- genotypes: bfloat16 [4096, 131072], P('rows', 'feat')
- labels: int32 [4096], P('rows'), may hold values from 0 to 63
- base_margin: float32 [4096, 64], P('rows')
- winners: int32 [2, 64], replicated, may hold values from 0 to 131071, as said below
Outputs:
- logits: float32 [4096, 64], P('rows')
- scores: float32 [3, 64, 131072], P(None, 'rows', 'feat')
Inputs may be any that keep to these rules, and one draw needn't show every extreme that they name: `winners`: in every iteration each of the 64 aligned blocks of 2048 columns holds the winning column of exactly one class.
All inputs are finite; a program needn't handle non-finite values.
Results may differ from a plain program's by a relative error of at most 0.012.
Values may be sent and summed in bfloat16 or wider, within the bound.
No kernel may reach another device: no remote copies, remote signals or barrier semaphores. Data moves between devices by JAX's collectives and lax.ppermute only.
A program may use at most 64 MiB of HBM per device.

v0:
```python
import jax
import jax.numpy as jnp
from jax import lax
from jax.sharding import PartitionSpec as P

K = 64
ITERS = 2


shrink_rate = 0.5
ridge_term = 1.0


def softmax_rows(values):
    top = jnp.max(values, axis=1, keepdims=True)
    expo = jnp.exp(values - top)
    return expo / jnp.sum(expo, axis=1, keepdims=True)


def shards(genotypes, labels, base_margin, winners):
    column_count = genotypes.shape[1]
    feat_count = lax.axis_size("feat")
    per_device = K // feat_count
    class_share = K // lax.axis_size("rows")
    feat_pos = lax.axis_index("feat")
    classes = jnp.arange(K, dtype=jnp.int32)
    onehot = (labels[:, None] == classes[None, :]).astype(jnp.float32)
    logits = base_margin
    tables = []
    contract = (((0,), (0,)), ((), ()))
    for step in range(ITERS + 1):
        prob = softmax_rows(logits)
        resid = (onehot - prob).astype(jnp.bfloat16)
        whole = lax.dot_general(resid, genotypes, contract, preferred_element_type=jnp.float32)
        total = lax.psum(whole.astype(jnp.bfloat16), "rows").astype(jnp.float32)
        table = lax.dynamic_slice_in_dim(
            total, lax.axis_index("rows") * class_share, class_share, 0
        )
        tables.append(table)
        if step < ITERS:
            chosen = winners[step]
            owner = chosen // column_count
            order = jnp.argsort(owner, stable=True)
            mine = lax.dynamic_slice_in_dim(order, feat_pos * per_device, per_device)
            local_cols = jnp.take(chosen, mine) - feat_pos * column_count
            picked = jnp.take(genotypes, local_cols, axis=1).astype(jnp.float32)
            select = (mine[:, None] == classes[None, :]).astype(jnp.float32)
            resid_mine = jnp.dot(
                resid.astype(jnp.float32), select.T, precision=lax.Precision.HIGHEST
            )
            prob_mine = jnp.dot(prob, select.T, precision=lax.Precision.HIGHEST)
            grad = jnp.sum(resid_mine * picked, axis=0)
            curv = jnp.sum(prob_mine * (1.0 - prob_mine) * picked * picked, axis=0)
            grad, curv = lax.psum((grad, curv), "rows")
            coef = shrink_rate * grad / (curv + ridge_term)
            contrib = coef[None, :] * picked
            spread_out = jnp.dot(contrib, select, precision=lax.Precision.HIGHEST)
            update = lax.psum(spread_out, "feat")
            logits = logits + update
    return (logits, jnp.stack(tables))


def solution(mesh):
    in_specs = (P("rows", "feat"), P("rows"), P("rows", None), P())
    out_specs = (P("rows", None), P(None, "rows", "feat"))
    return jax.shard_map(shards, mesh=mesh, in_specs=in_specs, out_specs=out_specs, check_vma=False)
```

profile of v0, /device:TPU:1, one launch (start us, length us, event | category | flops | bytes accessed | tf_op | source)
XLA Modules:
  0.0 1470.6 jit_solution(5654889008482441123)
XLA Ops:
  7.2 0.0 copy-start
  7.2 0.0 all-reduce.7.cloned.1.call-start
  7.2 0.8 fusion.44
  8.1 0.8 and_select_fusion
  8.8 2.0 sort.32
  10.9 0.6 dynamic_slice.16
  12.8 2.0 sort.31
  14.8 0.6 dynamic_slice.15
  18.0 0.7 fusion.45
  19.9 0.7 fusion.36
  20.5 0.9 reduce_max.27
  21.4 0.9 fusion.8
  22.4 0.0 copy-start.1
  22.4 1.8 fusion.18
  24.2 1.0 fusion.4
  25.1 1.1 constant_dynamic-slice_fusion
  26.3 0.0 copy-start.3
  26.3 0.1 copy.8
  26.4 0.6 fusion.22
  27.0 1.4 fusion.2
  28.4 24.7 %all-reduce.1 = (f32[1]{0:T(128)}, f32[1]{0:T(128)}) all-reduce(f32[1]{0:T(128)} %bitcast.11, f32[1]{0:T(128)} %bitcast.15), channel_id=1, replica_groups=mesh['rows'=8,'feat'=64] {'rows'}, use_global_device_ids=true, to_apply=%region_4.6 | all-reduce | flops 2 | bytes 16 | tf_op jit(solution)/shard_map/psum | solution.py:54
  54.5 0.7 broadcast_multiply_fusion.1
  55.2 0.0 all-reduce.7.cloned.1.call-update
  55.2 0.0 all-reduce.9.cloned.1.call-start
  55.3 0.0 copy-done
  55.3 1.2 convolution_convert_fusion.2
  56.5 0.1 copy.9
  56.6 0.7 fusion.37
  57.2 617.7 %all-reduce.7.cloned.1.call-done = f32[512,64]{0,1:T(8,128)} async-done(((f32[512,64]{0,1:T(8,128)}), f32[512,64]{0,1:T(8,128)}) %all-reduce.7.cloned.1.call-update) | async-done | bytes 131088 | tf_op jit(solution)/shard_map/psum | solution.py:58
  674.9 0.0 copy-done.1
  674.9 0.9 fusion.43
  675.9 0.8 fusion.16
  676.7 0.0 copy-done.3
  676.8 0.7 fusion.23
  677.5 1.4 fusion.3
  678.8 39.0 %all-reduce = (f32[1]{0:T(128)}, f32[1]{0:T(128)}) all-reduce(f32[1]{0:T(128)} %bitcast.29, f32[1]{0:T(128)} %bitcast.33), channel_id=1, replica_groups=mesh['rows'=8,'feat'=64] {'rows'}, use_global_device_ids=true, to_apply=%region_12.14 | all-reduce | flops 2 | bytes 16 | tf_op jit(solution)/shard_map/psum | solution.py:54
  719.1 0.7 broadcast_multiply_fusion
  719.9 0.0 all-reduce.9.cloned.1.call-update
  719.9 0.0 all-reduce.11.cloned.1.call-start
  720.0 1.2 convolution_convert_fusion.1
  721.1 616.6 %all-reduce.9.cloned.1.call-done = f32[512,64]{0,1:T(8,128)} async-done(((f32[512,64]{0,1:T(8,128)}), f32[512,64]{0,1:T(8,128)}) %all-reduce.9.cloned.1.call-update) | async-done | bytes 131088 | tf_op jit(solution)/shard_map/psum | solution.py:58
  1337.7 0.9 fusion.42
  1338.6 0.0 copy-start.2
  1338.7 1.2 convolution_convert_fusion
  1339.9 0.0 all-reduce.11.cloned.1.call-update
  1339.9 121.2 %all-reduce.11.cloned.1.call-done = (bf16[64,2048]{1,0:T(8,128)(2,1)}, bf16[64,2048]{1,0:T(8,128)(2,1)}, bf16[64,2048]{1,0:T(8,128)(2,1)}) async-done(((bf16[64,2048]{1,0:T(8,128)(2,1)}, bf16[64,2048]{1,0:T(8,128)(2,1)}, bf16[64,2048]{1,0:T(8,128)(2,1)}), (bf16[64,2048]{1,0:T(8,128)(2,1)}, bf16[64,2048]{1,0:T(8,128)(2,1)}, bf16[64,2048]{1,0:T(8,128)(2,1)})) %all-reduce.11.cloned.1.call-update) | async-done | bytes 786448 | tf_op jit(solution)/shard_map/psum | solution.py:35
  1461.1 0.8 convert_bitcast_fusion
  1461.9 0.8 convert_bitcast_fusion.1
  1462.6 0.8 convert_bitcast_fusion.2
  1463.4 0.7 pad_maximum_fusion
  1464.1 0.0 copy-done.2
  (9 shorter events, 0.2 us)
Async XLA Ops:
  7.2 48.1 %copy-start = (bf16[512,2048]{1,0:T(8,128)(2,1)S(1)}, bf16[512,2048]{1,0:T(8,128)(2,1)}, u32[]{:S(2)}) copy-start(bf16[512,2048]{1,0:T(8,128)(2,1)} %param.6) | copy-start | bytes 6291460
  7.2 667.7 %all-reduce.7.cloned.1.call-start = ((), (), s32[]{:S(2)}) async-start(), calls=%async_computation | async-start | bytes 262144 | tf_op jit(solution)/shard_map/psum | solution.py:58
  22.4 652.5 %copy-start.1 = (f32[512,64]{0,1:T(8,128)S(1)}, f32[512,64]{0,1:T(8,128)}, u32[]{:S(2)}) copy-start(f32[512,64]{0,1:T(8,128)} %param.8) | copy-start | bytes 393220
  26.3 650.5 %copy-start.3 = (s32[512]{0:T(512)S(1)}, s32[512]{0:T(512)}, u32[]{:S(2)}) copy-start(s32[512]{0:T(512)} %param.7) | copy-start | bytes 6148
  55.2 1282.5 %all-reduce.9.cloned.1.call-start = ((), (), s32[]{:S(2)}) async-start(), calls=%async_computation.1 | async-start | bytes 262144 | tf_op jit(solution)/shard_map/psum | solution.py:58
  719.9 741.2 %all-reduce.11.cloned.1.call-start = ((), (), s32[]{:S(2)}) async-start(), calls=%async_computation.2 | async-start | bytes 1572864 | tf_op jit(solution)/shard_map/psum | solution.py:35
  1338.6 125.4 %copy-start.2 = (f32[512,64]{0,1:T(8,128)}, f32[512,64]{0,1:T(8,128)S(1)}, u32[]{:S(2)}) copy-start(f32[512,64]{0,1:T(8,128)S(1)} %get-tuple-element.48) | copy-start | bytes 393220
Sparse Core Ops, SparseCore 0:
  55.3 619.5 all-reduce.6
  720.0 617.6 all-reduce.8
  1340.9 120.1 all-reduce.10
where the time goes:
time: 1470 us
  waiting for transfers between devices  1360 us (93%)
  blocking collectives  63.7 us (4%)
  between operations  21.7 us (1%)
  other arithmetic  17.4 us (1%)
    psum x2, waiting for transfers between devices, shards(): update = lax.psum(spread_out, 'feat')  1230 us
    psum x1, waiting for transfers between devices, shards(): total = lax.psum(whole.astype(jnp.bfloat16), 'rows').astype(jnp.float32)  121 us
    psum x2, blocking collectives, shards(): grad, curv = lax.psum((grad, curv), 'rows')  63.7 us
  transfers between devices with their start and end apart: 3, of which 3 were waited for; matrix products, arithmetic and copies ran while one was open for 0% of the time, Pallas kernels for 0%

commit v1 on v0

v1 whole, which is shorter than its diff:
```python
import jax
import jax.numpy as jnp
from jax import lax
from jax.sharding import PartitionSpec as P

K = 64
ITERS = 2


shrink_rate = 0.5
ridge_term = 1.0


def softmax_rows(values):
    top = jnp.max(values, axis=1, keepdims=True)
    expo = jnp.exp(values - top)
    return expo / jnp.sum(expo, axis=1, keepdims=True)


def shards(genotypes, labels, base_margin, winners):
    sample_count, column_count = genotypes.shape
    feat_count = lax.axis_size("feat")
    rows_count = lax.axis_size("rows")
    class_share = K // rows_count
    feat_pos = lax.axis_index("feat")
    classes = jnp.arange(K, dtype=jnp.int32)
    onehot = (labels[:, None] == classes[None, :]).astype(jnp.float32)
    contract = (((0,), (0,)), ((), ()))

    owner = winners // column_count
    local_cols = jnp.sum(
        jnp.where(owner == feat_pos, winners - feat_pos * column_count, 0), axis=1
    )
    pick = (
        jnp.arange(column_count, dtype=jnp.int32)[None, :] == local_cols[:, None]
    ).astype(jnp.bfloat16)
    own = lax.dot_general(
        pick, genotypes, (((1,), (1,)), ((), ())), preferred_element_type=jnp.float32
    ).astype(jnp.bfloat16)
    sent = jnp.broadcast_to(own[None], (feat_count, ITERS, sample_count))
    columns = lax.all_to_all(sent, "feat", 0, 0, tiled=True)

    def partial_table(resid):
        return lax.dot_general(
            resid, genotypes, contract, preferred_element_type=jnp.float32
        ).astype(jnp.bfloat16)

    logits = base_margin
    tables = []
    for step in range(ITERS + 1):
        prob = softmax_rows(logits)
        resid = (onehot - prob).astype(jnp.bfloat16)
        part = partial_table(resid)
        if step < ITERS:
            tables.append(
                lax.psum_scatter(part, "rows", scatter_dimension=0, tiled=True).astype(
                    jnp.float32
                )
            )
            place = (
                jnp.arange(feat_count, dtype=jnp.int32)[:, None] == owner[step][None, :]
            ).astype(jnp.bfloat16)
            picked = lax.dot_general(
                columns[:, step], place, contract, preferred_element_type=jnp.float32
            )
            grad = jnp.sum(resid.astype(jnp.float32) * picked, axis=0)
            curv = jnp.sum(prob * (1.0 - prob) * picked * picked, axis=0)
            sums = jnp.concatenate([grad, curv])
            shared = lax.all_to_all(
                jnp.broadcast_to(sums[None], (rows_count, 2 * K)), "rows", 0, 0, tiled=True
            )
            sums = jnp.sum(shared, axis=0)
            coef = shrink_rate * sums[:K] / (sums[K:] + ridge_term)
            logits = logits + coef[None, :] * picked
        else:
            shared = lax.all_to_all(part, "rows", 0, 0, tiled=True)
            shared = shared.reshape(rows_count, class_share, column_count)
            tables.append(jnp.sum(shared.astype(jnp.float32), axis=0))
    return (logits, jnp.stack(tables))


def solution(mesh):
    in_specs = (P("rows", "feat"), P("rows"), P("rows", None), P())
    out_specs = (P("rows", None), P(None, "rows", "feat"))
    return jax.shard_map(shards, mesh=mesh, in_specs=in_specs, out_specs=out_specs, check_vma=False)
```

time: 1470 us -> 165 us (0.11)
  waiting for transfers between devices: 1360 us -> 104 us
  blocking collectives: 63.7 us -> 0 us
  starting transfers between devices: 0.12 us -> 35 us
    psum x3 -> x0, waiting for transfers between devices: 1360 us -> none  [the longest x2 1230 us: shards(): update = lax.psum(spread_out, 'feat')]
    reduce_scatter x0 -> x2, waiting for transfers between devices: none -> 73 us  [shards(): lax.psum_scatter(part, 'rows', scatter_dimension=0, tiled=True)]
    psum x2 -> x0, blocking collectives: 63.7 us -> none  [shards(): grad, curv = lax.psum((grad, curv), 'rows')]
    all_to_all x0 -> x4, starting transfers between devices: none -> 35 us  [the longest x2 18.4 us: shards(): lax.all_to_all(jnp.broadcast_to(sums[None], (rows_count, 2 * K)), 'rows',...]
    all_to_all x0 -> x4, waiting for transfers between devices: none -> 30.7 us  [the longest x2 21.1 us: shards(): lax.all_to_all(jnp.broadcast_to(sums[None], (rows_count, 2 * K)), 'rows',...]
  transfers between devices with their start and end apart: 3 -> 6, of which waited for: 3 -> 5; matrix products, arithmetic and copies ran while one was open for 0% -> 4% of each run, Pallas kernels for 0% -> 0%
where the time goes in v1:
time: 165 us; the launch traced here: 164 us
  waiting for transfers between devices  104 us (63%)
  starting transfers between devices  35 us (21%)
  between operations  14.1 us (9%)
  matrix products  4.81 us (3%)
  other arithmetic  3.92 us (2%)
  local copies, waits for them, and re-layouts  2.79 us (2%)
    reduce_scatter x2, waiting for transfers between devices, shards(): lax.psum_scatter(part, 'rows', scatter_dimension=0, tiled=True)  73 us
    all_to_all x2, waiting for transfers between devices, shards(): lax.all_to_all(jnp.broadcast_to(sums[None], (rows_count, 2 * K)), 'rows',...  21.1 us
    all_to_all x2, starting transfers between devices, shards(): lax.all_to_all(jnp.broadcast_to(sums[None], (rows_count, 2 * K)), 'rows',...  18.4 us
    all_to_all x1, starting transfers between devices, shards(): columns = lax.all_to_all(sent, 'feat', 0, 0, tiled=True)  12.6 us
    all_to_all x1, waiting for transfers between devices, shards(): columns = lax.all_to_all(sent, 'feat', 0, 0, tiled=True)  9.58 us
    all_to_all x1, starting transfers between devices, shards(): shared = lax.all_to_all(part, 'rows', 0, 0, tiled=True)  4.01 us
    dot_general x3, matrix products, partial_table(): lax.dot_general(resid, genotypes, contract, preferred_element_type=jnp.fl...  3.53 us
  transfers between devices with their start and end apart: 6, of which 5 were waited for; matrix products, arithmetic and copies ran while one was open for 4% of the time, Pallas kernels for 0%

profile of v1, /device:TPU:1, one launch (start us, length us, event | category | flops | bytes accessed | tf_op | source)
XLA Modules:
  0.0 164.3 jit_solution(18184049646233091835)
XLA Ops:
  7.2 0.0 copy-start
  7.2 0.0 copy-start.1
  7.2 0.0 copy-start.3
  7.2 1.0 fusion.22
  8.2 0.6 copy-done
  8.8 0.6 convolution_convert_fusion.3
  9.4 0.7 broadcast_in_dim.8
  10.2 12.6 %all-to-all-start = ((bf16[64,2,512]{2,1,0:T(2,128)(2,1)}), bf16[64,2,512]{2,1,0:T(2,128)(2,1)S(1)}, u32[]{:S(2)}, u32[]{:S(2)}) async-start(bf16[64,2,512]{2,1,0:T(2,128)(2,1)} %broadcast_in_dim.8), calls=%async_computation | async-start | bytes 262144 | tf_op jit(solution)/shard_map/all_to_all | solution.py:41
  22.7 0.0 copy-done.1
  22.8 9.6 %all-to-all-done = bf16[64,2,512]{2,1,0:T(2,128)(2,1)S(1)} async-done(((bf16[64,2,512]{2,1,0:T(2,128)(2,1)}), bf16[64,2,512]{2,1,0:T(2,128)(2,1)S(1)}, u32[]{:S(2)}, u32[]{:S(2)}) %all-to-all-start) | async-done | bytes 131104 | tf_op jit(solution)/shard_map/all_to_all | solution.py:41
  32.4 0.2 fusion.27
  32.6 0.0 copy-done.3
  32.6 0.3 multiply_reduce_fusion.1
  32.9 0.1 pad_maximum_fusion.1
  33.0 0.6 broadcast_in_dim.9
  33.6 14.5 %all-to-all-start.1 = ((f32[8,1,128]{2,1,0:T(1,128)}), f32[8,1,128]{2,1,0:T(1,128)S(1)}, u32[]{:S(2)}, u32[]{:S(2)}) async-start(f32[8,1,128]{2,1,0:T(1,128)} %broadcast_in_dim.9), calls=%async_computation.1 | async-start | bytes 8192 | tf_op jit(solution)/shard_map/all_to_all | solution.py:69
  48.1 0.0 reduce-scatter.3.cloned.1.call-start
  48.1 1.2 convolution_convert_fusion.2
  49.3 0.0 reduce-scatter.3.cloned.1.call-update
  49.3 10.5 %all-to-all-done.1 = f32[8,1,128]{2,1,0:T(1,128)S(1)} async-done(((f32[8,1,128]{2,1,0:T(1,128)}), f32[8,1,128]{2,1,0:T(1,128)S(1)}, u32[]{:S(2)}, u32[]{:S(2)}) %all-to-all-start.1) | async-done | bytes 4128 | tf_op jit(solution)/shard_map/all_to_all | solution.py:69
  59.8 0.1 add_divide_fusion.1
  59.9 0.1 fusion.26
  60.1 0.3 multiply_reduce_fusion
  60.4 0.1 pad_maximum_fusion.2
  60.5 0.6 broadcast_in_dim.10
  61.1 3.9 %all-to-all-start.2 = ((f32[8,1,128]{2,1,0:T(1,128)}), f32[8,1,128]{2,1,0:T(1,128)S(1)}, u32[]{:S(2)}, u32[]{:S(2)}) async-start(f32[8,1,128]{2,1,0:T(1,128)} %broadcast_in_dim.10), calls=%async_computation.2 | async-start | bytes 8192 | tf_op jit(solution)/shard_map/all_to_all | solution.py:69
  65.0 0.0 reduce-scatter.5.cloned.1.call-start
  65.0 1.2 convolution_convert_fusion.1
  66.2 0.0 reduce-scatter.5.cloned.1.call-update
  66.2 10.6 %all-to-all-done.2 = f32[8,1,128]{2,1,0:T(1,128)S(1)} async-done(((f32[8,1,128]{2,1,0:T(1,128)}), f32[8,1,128]{2,1,0:T(1,128)S(1)}, u32[]{:S(2)}, u32[]{:S(2)}) %all-to-all-start.2) | async-done | bytes 4128 | tf_op jit(solution)/shard_map/all_to_all | solution.py:69
  76.8 0.1 add_divide_fusion
  76.8 0.1 fusion.25
  76.9 0.0 copy-start.2
  77.0 1.2 fusion
  78.2 4.0 %all-to-all-start.3 = ((bf16[8,8,2048]{2,1,0:T(8,128)(2,1)}), bf16[8,8,2048]{2,1,0:T(8,128)(2,1)S(1)}, u32[]{:S(2)}, u32[]{:S(2)}) async-start(bf16[8,8,2048]{2,1,0:T(8,128)(2,1)} %fusion), calls=%async_computation.5 | async-start | bytes 524288 | tf_op jit(solution)/shard_map/all_to_all | solution.py:76
  82.2 24.8 %reduce-scatter.3.cloned.1.call-done = bf16[8,2048]{1,0:T(8,128)(2,1)} async-done(((bf16[64,2048]{1,0:T(8,128)(2,1)}), bf16[8,2048]{1,0:T(8,128)(2,1)}) %reduce-scatter.3.cloned.1.call-update) | async-done | bytes 32784 | tf_op jit(solution)/shard_map/reduce_scatter | solution.py:56
  107.0 0.8 bitcast_convert_fusion.1
  107.7 48.2 %reduce-scatter.5.cloned.1.call-done = bf16[8,2048]{1,0:T(8,128)(2,1)} async-done(((bf16[64,2048]{1,0:T(8,128)(2,1)}), bf16[8,2048]{1,0:T(8,128)(2,1)}) %reduce-scatter.5.cloned.1.call-update) | async-done | bytes 32784 | tf_op jit(solution)/shard_map/reduce_scatter | solution.py:56
  155.9 0.8 bitcast_convert_fusion
  156.7 0.0 all-to-all-done.3
  156.7 0.7 pad_maximum_fusion
  157.4 0.0 copy-done.2
  (8 shorter events, 0.2 us)
Async XLA Ops:
  7.2 1.6 copy-start
  7.2 15.5 %copy-start.1 = (f32[512,64]{0,1:T(8,128)S(1)}, f32[512,64]{0,1:T(8,128)}, u32[]{:S(2)}) copy-start(f32[512,64]{0,1:T(8,128)} %param.6) | copy-start | bytes 393220
  7.2 25.4 %copy-start.3 = (s32[512]{0:T(512)S(1)}, s32[512]{0:T(512)}, u32[]{:S(2)}) copy-start(s32[512]{0:T(512)} %param.5) | copy-start | bytes 6148
  10.2 22.2 %all-to-all-start = ((bf16[64,2,512]{2,1,0:T(2,128)(2,1)}), bf16[64,2,512]{2,1,0:T(2,128)(2,1)S(1)}, u32[]{:S(2)}, u32[]{:S(2)}) async-start(bf16[64,2,512]{2,1,0:T(2,128)(2,1)} %broadcast_in_dim.8), calls=%async_computation | async-start | bytes 262144 | tf_op jit(solution)/shard_map/all_to_all | solution.py:41
  33.6 26.2 %all-to-all-start.1 = ((f32[8,1,128]{2,1,0:T(1,128)}), f32[8,1,128]{2,1,0:T(1,128)S(1)}, u32[]{:S(2)}, u32[]{:S(2)}) async-start(f32[8,1,128]{2,1,0:T(1,128)} %broadcast_in_dim.9), calls=%async_computation.1 | async-start | bytes 8192 | tf_op jit(solution)/shard_map/all_to_all | solution.py:69
  48.1 58.9 %reduce-scatter.3.cloned.1.call-start = ((), (), s32[]{:S(2)}) async-start(), calls=%async_computation.6 | async-start | bytes 294912 | tf_op jit(solution)/shard_map/reduce_scatter | solution.py:56
  61.1 15.7 %all-to-all-start.2 = ((f32[8,1,128]{2,1,0:T(1,128)}), f32[8,1,128]{2,1,0:T(1,128)S(1)}, u32[]{:S(2)}, u32[]{:S(2)}) async-start(f32[8,1,128]{2,1,0:T(1,128)} %broadcast_in_dim.10), calls=%async_computation.2 | async-start | bytes 8192 | tf_op jit(solution)/shard_map/all_to_all | solution.py:69
  65.0 91.0 %reduce-scatter.5.cloned.1.call-start = ((), (), s32[]{:S(2)}) async-start(), calls=%async_computation.7 | async-start | bytes 294912 | tf_op jit(solution)/shard_map/reduce_scatter | solution.py:56
  76.9 80.5 %copy-start.2 = (f32[512,64]{0,1:T(8,128)}, f32[512,64]{0,1:T(8,128)S(1)}, u32[]{:S(2)}) copy-start(f32[512,64]{0,1:T(8,128)S(1)} %get-tuple-element.7) | copy-start | bytes 393220
  78.2 78.5 %all-to-all-start.3 = ((bf16[8,8,2048]{2,1,0:T(8,128)(2,1)}), bf16[8,8,2048]{2,1,0:T(8,128)(2,1)S(1)}, u32[]{:S(2)}, u32[]{:S(2)}) async-start(bf16[8,8,2048]{2,1,0:T(8,128)(2,1)} %fusion), calls=%async_computation.5 | async-start | bytes 524288 | tf_op jit(solution)/shard_map/all_to_all | solution.py:76
Sparse Core Ops, SparseCore 0:
  51.7 55.2 reduce-scatter.2
  110.0 45.9 reduce-scatter.4

commit v2 on v1

v2 whole, which is shorter than its diff:
```python
import jax
import jax.numpy as jnp
from jax import lax
from jax.sharding import PartitionSpec as P

K = 64
ITERS = 2


shrink_rate = 0.5
ridge_term = 1.0

bf16 = jnp.bfloat16
f32 = jnp.float32


def softmax_classes(values):
    top = jnp.max(values, axis=0, keepdims=True)
    expo = jnp.exp(values - top)
    return expo / jnp.sum(expo, axis=0, keepdims=True)


def split3(values):
    high = lax.reduce_precision(values, 8, 7)
    rest = values - high
    middle = lax.reduce_precision(rest, 8, 7)
    return high, middle, rest - middle


def shards(genotypes, labels, base_margin, winners):
    sample_count, column_count = genotypes.shape
    feat_count = lax.axis_size("feat")
    rows_count = lax.axis_size("rows")
    class_share = K // rows_count
    half = column_count // 2
    feat_pos = lax.axis_index("feat")
    side = lax.rem(lax.axis_index("rows"), 2)
    partners = [(i, i ^ 1) for i in range(rows_count)]
    classes = jnp.arange(K, dtype=jnp.int32)
    contract = (((0,), (0,)), ((), ()))

    owner = winners // column_count
    local_cols = jnp.sum(
        jnp.where(owner == feat_pos, winners - feat_pos * column_count, 0), axis=1
    )
    pick = (
        jnp.arange(column_count, dtype=jnp.int32)[None, :] == local_cols[:, None]
    ).astype(bf16)
    own = lax.dot_general(
        pick, genotypes, (((1,), (1,)), ((), ())), preferred_element_type=f32
    ).astype(bf16)
    sent = jnp.broadcast_to(own[None], (feat_count, ITERS, sample_count))
    columns = lax.all_to_all(sent, "feat", 0, 0, tiled=True)

    kept = lax.dynamic_slice_in_dim(genotypes, side * half, half, 1)
    given = lax.dynamic_slice_in_dim(genotypes, (1 - side) * half, half, 1)
    taken = lax.ppermute(given, "rows", partners)
    margin = base_margin.T
    state = jnp.concatenate(
        [margin, jnp.broadcast_to(labels.astype(f32)[None, :], (8, sample_count))]
    )
    state_taken = lax.ppermute(state, "rows", partners)
    labels_taken = state_taken[K].astype(jnp.int32)

    onehot = (classes[:, None] == labels[None, :]).astype(f32)
    onehot_taken = (classes[:, None] == labels_taken[None, :]).astype(f32)
    logits, logits_taken = margin, state_taken[:K]
    columns_taken = lax.ppermute(columns, "rows", partners)

    def half_table(resid, resid_taken):
        rows_dim = (((1,), (0,)), ((), ()))
        first = lax.dot_general(resid, kept, rows_dim, preferred_element_type=f32)
        second = lax.dot_general(resid_taken, taken, rows_dim, preferred_element_type=f32)
        return (first + second).astype(bf16).reshape(rows_count, class_share, half)

    def finish_table(shared):
        parts = shared.astype(f32).reshape(rows_count // 2, 2, class_share, half)
        total = jnp.sum(parts, axis=0)
        return jnp.concatenate([total[0], total[1]], axis=1)

    tables = []
    for step in range(ITERS + 1):
        prob = softmax_classes(logits)
        resid = (onehot - prob).astype(bf16)
        resid_taken = (onehot_taken - softmax_classes(logits_taken)).astype(bf16)
        part = half_table(resid, resid_taken)
        if step < ITERS:
            place = (
                jnp.arange(feat_count, dtype=jnp.int32)[:, None] == owner[step][None, :]
            ).astype(bf16)
            picked = lax.dot_general(
                place, columns[:, step], contract, preferred_element_type=f32
            )
            picked_taken = lax.dot_general(
                place, columns_taken[:, step], contract, preferred_element_type=f32
            )
            grad = jnp.sum(resid.astype(f32) * picked, axis=1)
            curv = jnp.sum(prob * (1.0 - prob) * picked * picked, axis=1)
            terms = split3(0.5 * jnp.concatenate([grad, curv]))
            terms = jnp.stack(list(terms) + [jnp.zeros_like(grad, shape=(2 * K,))] * 5)
            terms = jnp.broadcast_to(terms.astype(bf16)[None], (rows_count, 8, 2 * K))
            shared = lax.all_to_all(
                jnp.concatenate([part, terms], axis=2), "rows", 0, 0, tiled=True
            )
            sums = jnp.sum(shared[:, :3, half:].astype(f32), axis=1)
            sums = 2.0 * jnp.sum(sums, axis=0)
            coef = (shrink_rate * sums[:K] / (sums[K:] + ridge_term))[:, None]
            logits = logits + coef * picked
            logits_taken = logits_taken + coef * picked_taken
            tables.append(finish_table(shared[:, :, :half]))
        else:
            shared = lax.all_to_all(part, "rows", 0, 0, tiled=True)
            tables.append(finish_table(shared))
    return (logits.T, jnp.stack(tables))


def solution(mesh):
    in_specs = (P("rows", "feat"), P("rows"), P("rows", None), P())
    out_specs = (P("rows", None), P(None, "rows", "feat"))
    return jax.shard_map(shards, mesh=mesh, in_specs=in_specs, out_specs=out_specs, check_vma=False)
```

time: 165 us -> 128 us (0.78)
  the two profiles are of different devices: /device:TPU:1 before, /device:TPU:32 now
where the time goes in v2:
time: 128 us; the launch traced here: 127 us
  waiting for transfers between devices  48 us (38%)
  starting transfers between devices  38.1 us (30%)
  other arithmetic  14.3 us (11%)
  matrix products  12.7 us (10%)
  local copies, waits for them, and re-layouts  12.4 us (10%)
    all_to_all x2, waiting for transfers between devices, shards(): lax.all_to_all(jnp.concatenate([part, terms], axis=2), 'rows', 0, 0, tile...  29.9 us
    all_to_all x2, starting transfers between devices, shards(): lax.all_to_all(jnp.concatenate([part, terms], axis=2), 'rows', 0, 0, tile...  16.4 us
    all_to_all x1, waiting for transfers between devices, shards(): shared = lax.all_to_all(part, 'rows', 0, 0, tiled=True)  14.7 us
    all_to_all x1, starting transfers between devices, shards(): columns = lax.all_to_all(sent, 'feat', 0, 0, tiled=True)  11.7 us
    dot_general x3, matrix products, half_table(): first = lax.dot_general(resid, kept, rows_dim, preferred_element_type=f32)  3.67 us
    dot_general x3, matrix products, half_table(): lax.dot_general(resid_taken, taken, rows_dim, preferred_element_type=f32)  3.48 us
    all_to_all x1, starting transfers between devices, shards(): shared = lax.all_to_all(part, 'rows', 0, 0, tiled=True)  3.37 us
    all_to_all x1, waiting for transfers between devices, shards(): columns = lax.all_to_all(sent, 'feat', 0, 0, tiled=True)  3.36 us
  transfers between devices with their start and end apart: 7, of which 4 were waited for; matrix products, arithmetic and copies ran while one was open for 18% of the time, Pallas kernels for 0%

profile of v2, /device:TPU:32, one launch (start us, length us, event | category | flops | bytes accessed | tf_op | source)
XLA Modules:
  0.0 126.5 jit_solution(10046347234049783303)
XLA Ops:
  0.6 0.0 copy-start
  0.6 0.0 copy-start.7
  0.7 1.5 %copy-done = bf16[512,2048]{1,0:T(8,128)(2,1)S(1)} copy-done((bf16[512,2048]{1,0:T(8,128)(2,1)S(1)}, bf16[512,2048]{1,0:T(8,128)(2,1)}, u32[]{:S(2)}) %copy-start) | copy-done | bytes 2097176
  2.2 1.1 constant_dynamic-slice_fusion
  3.3 1.9 %collective-permute-start.1 = (bf16[512,1024]{1,0:T(8,128)(2,1)}, bf16[512,1024]{1,0:T(8,128)(2,1)S(1)}, u32[]{:S(2)}, u32[]{:S(2)}) collective-permute-start(bf16[512,1024]{1,0:T(8,128)(2,1)} %constant_dynamic-slice_fusion), channel_id=1, source_target_pairs={{0,64},{64,0},{128,192},{192,128},{256,320},{320,256},{384,448},{4... | collective-permute-start | bytes 3145736 | tf_op jit(solution)/shard_map/ppermute | solution.py:57
  5.3 0.7 pad_maximum_fusion.1
  5.9 2.4 %collective-permute-start = (f32[72,512]{1,0:T(8,128)}, f32[72,512]{1,0:T(8,128)S(1)}, u32[]{:S(2)}, u32[]{:S(2)}) collective-permute-start(f32[72,512]{1,0:T(8,128)} %pad_maximum_fusion.1), channel_id=1, source_target_pairs={{0,64},{64,0},{128,192},{192,128},{256,320},{320,256},{384,448},{4... | collective-permute-start | bytes 442376 | tf_op jit(solution)/shard_map/ppermute | solution.py:62
  8.4 0.7 fusion.55
  9.0 0.6 convolution_convert_fusion
  9.7 0.7 broadcast_in_dim.11
  10.4 11.7 %all-to-all-start = ((bf16[64,2,512]{2,1,0:T(2,128)(2,1)}), bf16[64,2,512]{2,1,0:T(2,128)(2,1)S(1)}, u32[]{:S(2)}, u32[]{:S(2)}) async-start(bf16[64,2,512]{2,1,0:T(2,128)(2,1)} %broadcast_in_dim.11), calls=%async_computation | async-start | bytes 262144 | tf_op jit(solution)/shard_map/all_to_all | solution.py:53
  22.1 0.6 reduce_max.54
  22.7 1.3 %fusion.23 = f32[512]{0:T(512)} fusion(f32[512]{0:T(512)} %reduce_max.54, f32[512,64]{0,1:T(8,128)S(1)} %copy-done.1), kind=kLoop, calls=%fused_computation.60 | loop fusion | flops 65024 | bytes 135168 | tf_op jit(solution)/shard_map/reduce_sum | solution.py:20
  24.0 1.7 %fusion.12 = f32[64,1024]{1,0:T(8,128)} fusion(bf16[512,2048]{1,0:T(8,128)(2,1)S(1)} %copy-done, s32[]{:T(128)S(6)} %select_n.15, s32[512]{0:T(512)} %param.5, f32[512]{0:T(512)} %fusion.23, f32[512]{0:T(512)} %reduce_max.54, f32[512,64]{0,1:T(8,128)S(1)} %copy-done.1), kind=kOutput, calls=%fused_computation.18 | convolution fusion | flops 67305472 | bytes 1447940 | tf_op jit(solution)/shard_map/dot_general | solution.py:72
  25.7 1.3 %slice_bitcast_fusion.15 = (s32[64]{0:T(128)}, s32[64]{0:T(128)}) fusion(s32[2,64]{1,0:T(2,128)} %get-tuple-element.15), kind=kLoop, calls=%fused_computation.128 | loop fusion | bytes 1024 | tf_op jit(solution)/shard_map/eq | solution.py:89
  27.0 0.0 collective-permute-done
  27.0 0.6 fusion.24
  27.6 0.6 slice_convert_fusion
  28.2 3.4 %all-to-all-done = bf16[64,2,512]{2,1,0:T(2,128)(2,1)S(1)} async-done(((bf16[64,2,512]{2,1,0:T(2,128)(2,1)}), bf16[64,2,512]{2,1,0:T(2,128)(2,1)S(1)}, u32[]{:S(2)}, u32[]{:S(2)}) %all-to-all-start) | async-done | bytes 131104 | tf_op jit(solution)/shard_map/all_to_all | solution.py:53
  31.6 0.0 copy-start.6
  31.6 0.6 copy-done.6
  32.3 1.0 multiply_reduce_fusion.1
  33.3 0.6 fusion.56
  33.9 0.6 reduce-precision_convert_fusion.2
  34.5 0.6 stack.29
  35.1 0.6 stack.28
  35.7 1.3 %stack.30 = bf16[8,128]{1,0:T(8,128)(2,1)} concatenate(bf16[1,128]{1,0:T(2,128)(2,1)} %get-tuple-element.27, bf16[1,128]{1,0:T(2,128)(2,1)} %get-tuple-element.26, bf16[1,128]{1,0:T(2,128)(2,1)} %get-tuple-element.12, bf16[1,128]{1,0:T(2,128)(2,1)} %stack.28, bf16[4,128]{1,0:T(4,128)(2,1)} %stack.29), dimensions={0} | concatenate | bytes 4096 | tf_op jit(solution)/shard_map/stack | solution.py:100
  36.9 0.0 collective-permute-done.1
  37.0 1.3 fusion.5
  38.2 0.7 broadcast_in_dim.12
  38.9 0.7 pad_maximum_fusion.2
  39.6 12.4 %all-to-all-start.1 = ((bf16[8,8,1152]{2,1,0:T(8,128)(2,1)}), bf16[8,8,1152]{2,1,0:T(8,128)(2,1)}, u32[]{:S(2)}, u32[]{:S(2)}) async-start(bf16[8,8,1152]{2,1,0:T(8,128)(2,1)} %pad_maximum_fusion.2), calls=%async_computation.1 | async-start | bytes 294912 | tf_op jit(solution)/shard_map/all_to_all | solution.py:102
  52.0 2.4 %collective-permute-start.2 = (bf16[64,2,512]{2,0,1:T(8,128)(2,1)}, bf16[64,2,512]{2,0,1:T(8,128)(2,1)}, u32[]{:S(2)}, u32[]{:S(2)}) collective-permute-start(bf16[64,2,512]{2,0,1:T(8,128)(2,1)} %copy-done.6), channel_id=1, source_target_pairs={{0,64},{64,0},{128,192},{192,128},{256,320},{320,256},{384,448},{4... | collective-permute-start | bytes 393224 | tf_op jit(solution)/shard_map/ppermute | solution.py:68
  54.4 15.3 %all-to-all-done.1 = bf16[8,8,1152]{2,1,0:T(8,128)(2,1)} async-done(((bf16[8,8,1152]{2,1,0:T(8,128)(2,1)}), bf16[8,8,1152]{2,1,0:T(8,128)(2,1)}, u32[]{:S(2)}, u32[]{:S(2)}) %all-to-all-start.1) | async-done | bytes 147488 | tf_op jit(solution)/shard_map/all_to_all | solution.py:102
  69.6 0.7 convert_reduce_fusion.4
  70.4 0.1 add_divide_fusion.1
  70.5 0.1 fusion.64
  70.6 1.7 %fusion.10 = f32[64,1024]{1,0:T(8,128)} fusion(bf16[512,2048]{1,0:T(8,128)(2,1)S(1)} %copy-done, s32[]{:T(128)S(6)} %select_n.15, s32[512]{0:T(512)} %param.5, f32[512]{0:T(512)S(1)} %fusion.26, f32[64,512]{1,0:T(8,128)S(1)} %get-tuple-element.11, f32[512]{0:T(512)S(1)} %get-tuple-element.10), kind=kOutput, calls=%fused_computation.16 | convolution fusion | flops 67305472 | bytes 1447940 | tf_op jit(solution)/shard_map/dot_general | solution.py:72
  72.3 1.8 %multiply_reduce_fusion = (f32[64]{0:T(128)S(1)}, f32[64]{0:T(128)S(1)}, f32[64,512]{1,0:T(8,128)}) fusion(f32[512]{0:T(512)S(1)} %fusion.26, f32[64,512]{1,0:T(8,128)S(1)} %get-tuple-element.11, f32[512]{0:T(512)S(1)} %get-tuple-element.10, s32[512]{0:T(512)} %param.5, bf16[64,2,512]{2,0,1:T(8,128)(2,1)} %copy-done.6, s32[64]{0:T(128)} %get-tuple-element.23), kind=kOutput, calls=%fused_computation.49 | convolution fusion | flops 4657024 | bytes 334848 | tf_op jit(solution)/shard_map/dot_general | solution.py:91
  74.1 0.6 fusion.57
  74.7 0.6 reduce-precision_convert_fusion
  75.3 0.0 collective-permute-done.2
  75.3 1.1 fusion.65
  76.4 0.0 copy-start.8
  76.4 0.7 stack.31
  77.2 1.3 fusion.4
  78.4 0.7 pad_maximum_fusion.3
  79.1 4.0 %all-to-all-start.2 = ((bf16[8,8,1152]{2,1,0:T(8,128)(2,1)}), bf16[8,8,1152]{2,1,0:T(8,128)(2,1)}, u32[]{:S(2)}, u32[]{:S(2)}) async-start(bf16[8,8,1152]{2,1,0:T(8,128)(2,1)} %pad_maximum_fusion.3), calls=%async_computation.2 | async-start | bytes 294912 | tf_op jit(solution)/shard_map/all_to_all | solution.py:102
  83.1 0.9 slice.95
  84.1 0.6 slice_bitcast_fusion.13
  84.7 14.6 %all-to-all-done.2 = bf16[8,8,1152]{2,1,0:T(8,128)(2,1)} async-done(((bf16[8,8,1152]{2,1,0:T(8,128)(2,1)}), bf16[8,8,1152]{2,1,0:T(8,128)(2,1)}, u32[]{:S(2)}, u32[]{:S(2)}) %all-to-all-start.2) | async-done | bytes 147488 | tf_op jit(solution)/shard_map/all_to_all | solution.py:102
  99.3 0.9 slice.98
  100.2 0.6 slice_bitcast_fusion.11
  100.9 0.7 convert_reduce_fusion.3
  101.6 0.1 add_divide_fusion
  101.7 1.0 fusion.63
  102.8 0.3 fusion.8
  103.1 1.1 fusion.66
  104.2 1.0 fusion.3
  105.2 3.4 %all-to-all-start.3 = ((bf16[8,8,1024]{2,1,0:T(8,128)(2,1)}), bf16[8,8,1024]{2,1,0:T(8,128)(2,1)S(1)}, u32[]{:S(2)}, u32[]{:S(2)}) async-start(bf16[8,8,1024]{2,1,0:T(8,128)(2,1)} %fusion.3), calls=%async_computation.3 | async-start | bytes 262144 | tf_op jit(solution)/shard_map/all_to_all | solution.py:112
  108.5 0.8 maximum_bitcast_fusion
  109.4 1.6 %bitcast_add_fusion = f32[512,64]{0,1:T(8,128)} fusion(f32[512,64]{0,1:T(8,128)S(1)} %copy-done.1, f32[64,512]{1,0:T(8,128)} %get-tuple-element.29, f32[64,512]{1,0:T(8,128)S(1)} %copy-done.5, f32[64]{0:T(128)S(1)} %add_divide_fusion, f32[64]{0:T(128)S(1)} %copy-done.12), kind=kLoop, calls=%fused_computation.45 | loop fusion | flops 131072 | bytes 524800 | tf_op jit(solution)/shard_map/add | solution.py:108
  111.0 14.7 %all-to-all-done.3 = bf16[8,8,1024]{2,1,0:T(8,128)(2,1)S(1)} async-done(((bf16[8,8,1024]{2,1,0:T(8,128)(2,1)}), bf16[8,8,1024]{2,1,0:T(8,128)(2,1)S(1)}, u32[]{:S(2)}, u32[]{:S(2)}) %all-to-all-start.3) | async-done | bytes 131104 | tf_op jit(solution)/shard_map/all_to_all | solution.py:112
  125.8 0.7 pad_maximum_fusion
  (40 shorter events, 0.4 us)
Async XLA Ops:
  0.6 1.6 %copy-start = (bf16[512,2048]{1,0:T(8,128)(2,1)S(1)}, bf16[512,2048]{1,0:T(8,128)(2,1)}, u32[]{:S(2)}) copy-start(bf16[512,2048]{1,0:T(8,128)(2,1)} %param.4) | copy-start | bytes 6291460
  0.6 4.6 %copy-start.7 = (s32[512]{0:T(512)S(1)}, s32[512]{0:T(512)}, u32[]{:S(2)}) copy-start(s32[512]{0:T(512)} %param.5) | copy-start | bytes 6148
  0.7 4.6 %copy-start.1 = (f32[512,64]{0,1:T(8,128)S(1)}, f32[512,64]{0,1:T(8,128)}, u32[]{:S(2)}) copy-start(f32[512,64]{0,1:T(8,128)} %param.6) | copy-start | bytes 393220
  0.7 7.7 %copy-start.14 = (s32[2,64]{1,0:T(2,128)S(1)}, s32[2,64]{1,0:T(2,128)}, u32[]{:S(2)}) copy-start(s32[2,64]{1,0:T(2,128)} %param.7) | copy-start | bytes 1540
  3.3 33.6 %collective-permute-start.1 = (bf16[512,1024]{1,0:T(8,128)(2,1)}, bf16[512,1024]{1,0:T(8,128)(2,1)S(1)}, u32[]{:S(2)}, u32[]{:S(2)}) collective-permute-start(bf16[512,1024]{1,0:T(8,128)(2,1)} %constant_dynamic-slice_fusion), channel_id=1, source_target_pairs={{0,64},{64,0},{128,192},{192,128},{256,320},{320,256},{384,448},{4... | collective-permute-start | bytes 3145736 | tf_op jit(solution)/shard_map/ppermute | solution.py:57
  5.9 21.1 %collective-permute-start = (f32[72,512]{1,0:T(8,128)}, f32[72,512]{1,0:T(8,128)S(1)}, u32[]{:S(2)}, u32[]{:S(2)}) collective-permute-start(f32[72,512]{1,0:T(8,128)} %pad_maximum_fusion.1), channel_id=1, source_target_pairs={{0,64},{64,0},{128,192},{192,128},{256,320},{320,256},{384,448},{4... | collective-permute-start | bytes 442376 | tf_op jit(solution)/shard_map/ppermute | solution.py:62
  10.4 21.2 %all-to-all-start = ((bf16[64,2,512]{2,1,0:T(2,128)(2,1)}), bf16[64,2,512]{2,1,0:T(2,128)(2,1)S(1)}, u32[]{:S(2)}, u32[]{:S(2)}) async-start(bf16[64,2,512]{2,1,0:T(2,128)(2,1)} %broadcast_in_dim.11), calls=%async_computation | async-start | bytes 262144 | tf_op jit(solution)/shard_map/all_to_all | solution.py:53
  27.0 43.5 %copy-start.2 = (f32[72,512]{1,0:T(8,128)}, f32[72,512]{1,0:T(8,128)S(1)}, u32[]{:S(2)}) copy-start(f32[72,512]{1,0:T(8,128)S(1)} %collective-permute-done) | copy-start | bytes 442372
  27.0 0.6 copy-start.10
  31.6 0.7 copy-start.6
  33.3 39.0 %copy-start.4 = (f32[64,512]{1,0:T(8,128)}, f32[64,512]{1,0:T(8,128)S(1)}, u32[]{:S(2)}) copy-start(f32[64,512]{1,0:T(8,128)S(1)} %get-tuple-element.28) | copy-start | bytes 393220
  39.6 30.1 %all-to-all-start.1 = ((bf16[8,8,1152]{2,1,0:T(8,128)(2,1)}), bf16[8,8,1152]{2,1,0:T(8,128)(2,1)}, u32[]{:S(2)}, u32[]{:S(2)}) async-start(bf16[8,8,1152]{2,1,0:T(8,128)(2,1)} %pad_maximum_fusion.2), calls=%async_computation.1 | async-start | bytes 294912 | tf_op jit(solution)/shard_map/all_to_all | solution.py:102
  52.0 23.3 %collective-permute-start.2 = (bf16[64,2,512]{2,0,1:T(8,128)(2,1)}, bf16[64,2,512]{2,0,1:T(8,128)(2,1)}, u32[]{:S(2)}, u32[]{:S(2)}) collective-permute-start(bf16[64,2,512]{2,0,1:T(8,128)(2,1)} %copy-done.6), channel_id=1, source_target_pairs={{0,64},{64,0},{128,192},{192,128},{256,320},{320,256},{384,448},{4... | collective-permute-start | bytes 393224 | tf_op jit(solution)/shard_map/ppermute | solution.py:68
  69.6 5.6 %copy-start.13 = (s32[64]{0:T(128)S(1)}, s32[64]{0:T(128)}, u32[]{:S(2)}) copy-start(s32[64]{0:T(128)} %get-tuple-element.22) | copy-start | bytes 772
  70.5 6.0 %copy-start.11 = (f32[64]{0:T(128)}, f32[64]{0:T(128)S(1)}, u32[]{:S(2)}) copy-start(f32[64]{0:T(128)S(1)} %add_divide_fusion.1) | copy-start | bytes 772
  70.5 4.8 %copy-start.3 = (f32[72,512]{1,0:T(8,128)S(1)}, f32[72,512]{1,0:T(8,128)}, u32[]{:S(2)}) copy-start(f32[72,512]{1,0:T(8,128)} %copy-done.2) | copy-start | bytes 442372
  76.4 26.4 %copy-start.8 = (s32[512]{0:T(512)S(1)}, s32[512]{0:T(512)}, u32[]{:S(2)}) copy-start(s32[512]{0:T(512)} %param.5) | copy-start | bytes 6148
  78.4 25.8 %copy-start.9 = (s32[1,512]{1,0:T(1,128)S(1)}, s32[1,512]{1,0:T(1,128)}, u32[]{:S(2)}) copy-start(s32[1,512]{1,0:T(1,128)} %slice_convert_fusion) | copy-start | bytes 6148
  79.1 20.2 %all-to-all-start.2 = ((bf16[8,8,1152]{2,1,0:T(8,128)(2,1)}), bf16[8,8,1152]{2,1,0:T(8,128)(2,1)}, u32[]{:S(2)}, u32[]{:S(2)}) async-start(bf16[8,8,1152]{2,1,0:T(8,128)(2,1)} %pad_maximum_fusion.3), calls=%async_computation.2 | async-start | bytes 294912 | tf_op jit(solution)/shard_map/all_to_all | solution.py:102
  102.7 6.7 %copy-start.5 = (f32[64,512]{1,0:T(8,128)S(1)}, f32[64,512]{1,0:T(8,128)}, u32[]{:S(2)}) copy-start(f32[64,512]{1,0:T(8,128)} %copy-done.4) | copy-start | bytes 393220
  102.7 6.7 %copy-start.12 = (f32[64]{0:T(128)S(1)}, f32[64]{0:T(128)}, u32[]{:S(2)}) copy-start(f32[64]{0:T(128)} %copy-done.11) | copy-start | bytes 772
  105.2 20.6 %all-to-all-start.3 = ((bf16[8,8,1024]{2,1,0:T(8,128)(2,1)}), bf16[8,8,1024]{2,1,0:T(8,128)(2,1)S(1)}, u32[]{:S(2)}, u32[]{:S(2)}) async-start(bf16[8,8,1024]{2,1,0:T(8,128)(2,1)} %fusion.3), calls=%async_computation.3 | async-start | bytes 262144 | tf_op jit(solution)/shard_map/all_to_all | solution.py:112

commit v3 on v0

v3 whole, which is shorter than its diff:
```python
import jax
import jax.numpy as jnp
from jax import lax
from jax.experimental import pallas as pl
from jax.experimental.pallas import tpu as pltpu
from jax.sharding import PartitionSpec as P

K = 64
ITERS = 2
LANES = 128


shrink_rate = 0.5
ridge_term = 1.0

bf16 = jnp.bfloat16
f32 = jnp.float32
i32 = jnp.int32
VMEM = pl.BlockSpec(memory_space=pltpu.VMEM)
HBM = pl.BlockSpec(memory_space=pltpu.HBM)


def call(body, out_shape, in_specs, scratch=(), flops=0, moved=0, room=16 << 20):
    out_specs = jax.tree.map(lambda _: VMEM, out_shape)
    return pl.pallas_call(
        body,
        out_shape=out_shape,
        in_specs=in_specs,
        out_specs=out_specs,
        scratch_shapes=list(scratch),
        cost_estimate=pl.CostEstimate(flops=flops, bytes_accessed=moved, transcendentals=0),
        compiler_params=pltpu.CompilerParams(vmem_limit_bytes=room),
    )


def rounded(values):
    return values.astype(bf16).astype(f32)


def split3(values):
    high = rounded(values)
    rest = values - high
    middle = rounded(rest)
    return high, middle, rest - middle


def softmax_classes(values):
    top = jnp.max(values, axis=0, keepdims=True)
    expo = jnp.exp(values - top)
    return expo / jnp.sum(expo, axis=0, keepdims=True)


def residuals(logits, label_row):
    prob = softmax_classes(logits)
    classes = lax.broadcasted_iota(i32, logits.shape, 0).astype(f32)
    onehot = jnp.where(classes == label_row, 1.0, 0.0)
    return (onehot - prob).astype(bf16), prob


def pick_body(win_ref, geno_ref, out_ref, block_ref, sem_ref):
    samples, columns = geno_ref.shape
    local = win_ref[...] - lax.axis_index("feat") * columns
    mine = jnp.where((local >= 0) & (local < columns), local, 0).astype(f32)
    copies, lanes = [], []
    for step in range(ITERS):
        col = jnp.sum(mine[step : step + 1]).astype(i32)
        start = pl.multiple_of((col // LANES) * LANES, LANES)
        copy = pltpu.make_async_copy(
            geno_ref.at[:, pl.ds(start, LANES)], block_ref.at[step], sem_ref.at[step]
        )
        copy.start()
        copies.append(copy)
        lanes.append(col - start)
    rows = lax.broadcasted_iota(i32, (8, LANES), 0)
    lane = lax.broadcasted_iota(i32, (8, LANES), 1)
    tile = jnp.zeros((8, LANES), f32)
    for step in range(ITERS):
        copies[step].wait()
        pick = jnp.where(lane == lanes[step], 1.0, 0.0).astype(bf16)
        x = lax.dot_general(
            pick, block_ref[step], (((1,), (1,)), ((), ())), preferred_element_type=f32
        )
        for j in range(samples // LANES):
            here = rows == step * (samples // LANES) + j
            tile = tile + jnp.where(here, x[:, j * LANES : (j + 1) * LANES], 0.0)
    out_ref[...] = jnp.broadcast_to(tile.astype(bf16)[None], out_ref.shape)


def load_halves(geno_ref, taken_ref, both_ref, sem_ref):
    samples, half = taken_ref.shape
    side = lax.rem(lax.axis_index("rows"), 2)
    start = pl.multiple_of(side * half, LANES)
    first = pltpu.make_async_copy(
        geno_ref.at[:, pl.ds(start, half)], both_ref.at[pl.ds(0, samples)], sem_ref.at[0]
    )
    second = pltpu.make_async_copy(taken_ref, both_ref.at[pl.ds(samples, samples)], sem_ref.at[1])
    first.start()
    second.start()
    return first, second


def half_table(resid, resid_taken, both_ref):
    whole = jnp.concatenate([resid, resid_taken], axis=1)
    return jnp.dot(whole, both_ref[...], preferred_element_type=f32)


def sums_tile(resid, prob, picked):
    grad = resid.astype(f32) * picked
    curv = prob * (1.0 - prob) * picked * picked
    both = 0.5 * jnp.concatenate([grad, curv], axis=0)
    folded = both[:, :LANES]
    for j in range(1, both.shape[1] // LANES):
        folded = folded + both[:, j * LANES : (j + 1) * LANES]
    ones = jnp.ones((8, LANES), bf16)
    total = jnp.zeros((8, 2 * K), f32)
    for term in split3(folded):
        total = total + lax.dot_general(
            ones, term.astype(bf16), (((1,), (1,)), ((), ())), preferred_element_type=f32
        )
    high, middle, low = split3(total)
    row = lax.broadcasted_iota(i32, total.shape, 0)
    tile = jnp.where(row == 0, high, jnp.where(row == 1, middle, jnp.where(row == 2, low, 0.0)))
    return tile.astype(bf16)


def coefficients(shared_ref, half):
    tiles = shared_ref[:, :, half:].astype(f32)
    row = jnp.sum(jnp.sum(tiles, axis=0), axis=0, keepdims=True)
    column = jnp.transpose(jnp.broadcast_to(row, (2 * K, LANES)))
    return shrink_rate * (2.0 * column[:K]) / (2.0 * column[K:] + ridge_term)


def lane_tile(values, count):
    return jnp.concatenate([values] * count, axis=1)


def first_table_body(state_ref, state_taken_ref, geno_ref, taken_ref, out_ref, both_ref, sem_ref):
    copies = load_halves(geno_ref, taken_ref, both_ref, sem_ref)
    resid, _ = residuals(state_ref[:K], state_ref[K : K + 1])
    resid_taken, _ = residuals(state_taken_ref[:K], state_taken_ref[K : K + 1])
    for copy in copies:
        copy.wait()
    table = half_table(resid, resid_taken, both_ref)
    out_ref[...] = table.reshape(out_ref.shape).astype(bf16)


def first_sums_body(cols_ref, win_ref, state_ref, table_ref, out_ref, picked_ref, *, columns):
    half = table_ref.shape[2]
    feats = cols_ref.shape[0]
    blocks = state_ref.shape[1] // LANES
    cols = cols_ref[...].astype(f32)
    feat = lax.broadcasted_iota(i32, (feats, K), 0)
    for step in range(ITERS):
        owner = win_ref[step : step + 1] // columns
        place = jnp.where(feat == owner, 1.0, 0.0).astype(bf16)
        for j in range(blocks):
            piece = cols[:, step * blocks + j, :].astype(bf16)
            picked = lax.dot_general(
                place, piece, (((0,), (0,)), ((), ())), preferred_element_type=f32
            )
            picked_ref[step, :, j * LANES : (j + 1) * LANES] = picked.astype(bf16)
    resid, prob = residuals(state_ref[:K], state_ref[K : K + 1])
    tile = sums_tile(resid, prob, picked_ref[0].astype(f32))
    out_ref[:, :, :half] = table_ref[...]
    out_ref[:, :, half:] = jnp.broadcast_to(tile[None], (out_ref.shape[0], 8, 2 * K))


def next_table_body(
    shared_ref, logits_ref, logits_taken_ref, state_ref, state_taken_ref, picked_ref,
    picked_taken_ref, geno_ref, taken_ref, out_ref, new_ref, *rest, step,
):
    half = taken_ref.shape[1]
    last = step == ITERS - 1
    new_taken_ref = None if last else rest[0]
    both_ref, sem_ref = rest[-2:]
    copies = load_halves(geno_ref, taken_ref, both_ref, sem_ref)
    coef = coefficients(shared_ref, half)
    coef = lane_tile(coef, new_ref.shape[1] // LANES)
    logits = logits_ref[:K] + coef * picked_ref[step].astype(f32)
    new_ref[...] = logits
    resid, prob = residuals(logits, state_ref[K : K + 1])
    if not last:
        tile = sums_tile(resid, prob, picked_ref[step + 1].astype(f32))
        out_ref[:, :, half:] = jnp.broadcast_to(tile[None], (out_ref.shape[0], 8, 2 * K))
    logits_taken = logits_taken_ref[:K] + coef * picked_taken_ref[step].astype(f32)
    if not last:
        new_taken_ref[...] = logits_taken
    resid_taken, _ = residuals(logits_taken, state_taken_ref[K : K + 1])
    for copy in copies:
        copy.wait()
    table = half_table(resid, resid_taken, both_ref)
    out_ref[:, :, :half] = table.reshape(out_ref.shape[0], -1, half).astype(bf16)


def shards(genotypes, labels, base_margin, winners):
    samples, columns = genotypes.shape
    feat_count = lax.axis_size("feat")
    rows_count = lax.axis_size("rows")
    class_share = K // rows_count
    half = columns // 2
    side = lax.rem(lax.axis_index("rows"), 2)
    partners = [(i, i ^ 1) for i in range(rows_count)]
    shape = jax.ShapeDtypeStruct
    work = 2 * K * 2 * samples * half
    halves = [pltpu.VMEM((2 * samples, half), bf16), pltpu.SemaphoreType.DMA((2,))]

    sent = call(
        pick_body,
        shape((feat_count, ITERS * samples // LANES, LANES), bf16),
        [VMEM, HBM],
        [pltpu.VMEM((ITERS, samples, LANES), bf16), pltpu.SemaphoreType.DMA((ITERS,))],
        moved=samples * LANES * 4,
        room=None,
    )(winners, genotypes)
    cols = lax.all_to_all(sent, "feat", 0, 0, tiled=True)

    sent, geno, margin, marks = lax.optimization_barrier(
        (sent, genotypes, base_margin, labels)
    )
    given = lax.dynamic_slice_in_dim(geno, (1 - side) * half, half, 1)
    taken = lax.ppermute(given, "rows", partners)
    state = jnp.concatenate(
        [margin.T, jnp.broadcast_to(marks.astype(f32)[None, :], (8, samples))]
    )
    state_taken = lax.ppermute(state, "rows", partners)

    table = call(
        first_table_body,
        shape((rows_count, class_share, half), bf16),
        [VMEM, VMEM, HBM, HBM],
        halves,
        flops=work,
        moved=4 * samples * half,
    )(state, state_taken, genotypes, taken)

    def first_sums(*refs):
        first_sums_body(*refs, columns=columns)

    payload, picked = call(
        first_sums,
        (
            shape((rows_count, class_share, half + 2 * K), bf16),
            shape((ITERS, K, samples), bf16),
        ),
        [VMEM] * 4,
        moved=4 * samples * half,
    )(cols, winners, state, table)
    shared0 = lax.all_to_all(payload, "rows", 0, 0, tiled=True)
    picked_taken = lax.ppermute(picked, "rows", partners)

    def second(*refs):
        next_table_body(*refs, step=0)

    payload, logits, logits_taken = call(
        second,
        (
            shape((rows_count, class_share, half + 2 * K), bf16),
            shape((K, samples), f32),
            shape((K, samples), f32),
        ),
        [VMEM] * 7 + [HBM] * 2,
        halves,
        flops=work,
        moved=4 * samples * half,
    )(shared0, state, state_taken, state, state_taken, picked, picked_taken, genotypes, taken)
    shared1 = lax.all_to_all(payload, "rows", 0, 0, tiled=True)

    def third(*refs):
        next_table_body(*refs, step=1)

    payload, logits = call(
        third,
        (shape((rows_count, class_share, half), bf16), shape((K, samples), f32)),
        [VMEM] * 7 + [HBM] * 2,
        halves,
        flops=work,
        moved=4 * samples * half,
    )(shared1, logits, logits_taken, state, state_taken, picked, picked_taken, genotypes, taken)
    shared2 = lax.all_to_all(payload, "rows", 0, 0, tiled=True)

    tables = []
    for shared in (shared0, shared1, shared2):
        parts = shared[:, :, :half].astype(f32).reshape(rows_count // 2, 2, class_share, half)
        total = jnp.sum(parts, axis=0)
        tables.append(jnp.concatenate([total[0], total[1]], axis=1))
    return (logits.T, jnp.stack(tables))


def solution(mesh):
    in_specs = (P("rows", "feat"), P("rows"), P("rows", None), P())
    out_specs = (P("rows", None), P(None, "rows", "feat"))
    return jax.shard_map(shards, mesh=mesh, in_specs=in_specs, out_specs=out_specs, check_vma=False)
```

time: 1470 us -> 117 us (0.08)
  the two profiles are of different devices: /device:TPU:1 before, /device:TPU:32 now
where the time goes in v3:
time: 117 us; the launch traced here: 116 us
  waiting for transfers between devices  52.7 us (45%)
  starting transfers between devices  38 us (32%)
  local copies, waits for them, and re-layouts  14.5 us (12%)
  Pallas kernels  9.32 us (8%)
    all_to_all x1, waiting for transfers between devices, shards(): shared1 = lax.all_to_all(payload, 'rows', 0, 0, tiled=True)  16 us
    all_to_all x1, waiting for transfers between devices, shards(): shared2 = lax.all_to_all(payload, 'rows', 0, 0, tiled=True)  15.8 us
    all_to_all x1, waiting for transfers between devices, shards(): shared0 = lax.all_to_all(payload, 'rows', 0, 0, tiled=True)  13.5 us
    all_to_all x1, starting transfers between devices, shards(): shared0 = lax.all_to_all(payload, 'rows', 0, 0, tiled=True)  12.4 us
    all_to_all x1, starting transfers between devices, shards(): cols = lax.all_to_all(sent, 'feat', 0, 0, tiled=True)  11.9 us
    unnamed x38, local copies, waits for them, and re-layouts  11.6 us
    all_to_all x1, waiting for transfers between devices, shards(): cols = lax.all_to_all(sent, 'feat', 0, 0, tiled=True)  4.83 us
    all_to_all x1, starting transfers between devices, shards(): shared1 = lax.all_to_all(payload, 'rows', 0, 0, tiled=True)  4 us
  transfers between devices with their start and end apart: 7, of which 6 were waited for; matrix products, arithmetic and copies ran while one was open for 2% of the time, Pallas kernels for 1%

profile of v3, /device:TPU:32, one launch (start us, length us, event | category | flops | bytes accessed | tf_op | source)
XLA Modules:
  0.0 116.2 jit_solution(10399196970153232611)
XLA Ops:
  0.6 0.0 copy-start
  0.6 0.0 copy-start.18
  0.7 0.0 copy-start.17
  0.7 2.9 %shard_map.59 = bf16[64,8,128]{2,1,0:T(8,128)(2,1)} custom-call(s32[2,64]{1,0:T(2,128)} %refs_1_.1, bf16[512,2048]{1,0:T(8,128)(2,1)} %refs_7_.3), custom_call_target="tpu_custom_call" | custom-call | bytes 262144 | tf_op jit(solution)/shard_map/pallas_call | solution.py:207
  3.5 0.0 copy-done
  3.5 1.1 constant_dynamic-slice_fusion
  4.7 0.0 copy-start.16
  4.7 2.0 %collective-permute-start.1 = (bf16[512,1024]{1,0:T(8,128)(2,1)}, bf16[512,1024]{1,0:T(8,128)(2,1)S(1)}, u32[]{:S(2)}, u32[]{:S(2)}) collective-permute-start(bf16[512,1024]{1,0:T(8,128)(2,1)} %constant_dynamic-slice_fusion), channel_id=1, source_target_pairs={{0,64},{64,0},{128,192},{192,128},{256,320},{320,256},{384,448},{4... | collective-permute-start | bytes 3145736 | tf_op jit(solution)/shard_map/ppermute | solution.py:221
  6.7 11.9 %all-to-all-start = ((bf16[64,8,128]{2,1,0:T(8,128)(2,1)}), bf16[64,8,128]{2,1,0:T(8,128)(2,1)}, u32[]{:S(2)}, u32[]{:S(2)}) async-start(bf16[64,8,128]{2,1,0:T(8,128)(2,1)} %shard_map.59), calls=%async_computation | async-start | bytes 262144 | tf_op jit(solution)/shard_map/all_to_all | solution.py:215
  18.6 0.0 copy-done.18
  18.6 0.0 copy-done.17
  18.6 1.9 %collective-permute-start = (f32[72,512]{1,0:T(8,128)S(1)}, f32[72,512]{1,0:T(8,128)S(1)}, u32[]{:S(2)}, u32[]{:S(2)}) collective-permute-start(f32[72,512]{1,0:T(8,128)S(1)} %pad_maximum_fusion.1.state_ref.refs_2_.refs_1_.refs_3_), channel_id=1, source_target_pairs={{0,64},{64,0},{128,192},{192,128},{256,320},{320,256},{384,448},{4... | collective-permute-start | bytes 442376 | tf_op jit(solution)/shard_map/ppermute | solution.py:225
  20.6 1.3 %collective-permute-done.state_taken_ref.refs_2_.refs_4_ = f32[72,512]{1,0:T(8,128)S(1)} collective-permute-done((f32[72,512]{1,0:T(8,128)S(1)}, f32[72,512]{1,0:T(8,128)S(1)}, u32[]{:S(2)}, u32[]{:S(2)}) %collective-permute-start) | collective-permute-done | bytes 147488 | tf_op jit(solution)/shard_map/ppermute | solution.py:225
  21.9 0.0 collective-permute-done.1.taken_ref.refs_8_
  21.9 0.9 shard_map.60.refs_3_
  22.8 0.0 copy-start.1
  22.8 0.6 copy-done.1
  23.5 4.8 %all-to-all-done.refs_0_ = bf16[64,8,128]{2,1,0:T(8,128)(2,1)} async-done(((bf16[64,8,128]{2,1,0:T(8,128)(2,1)}), bf16[64,8,128]{2,1,0:T(8,128)(2,1)}, u32[]{:S(2)}, u32[]{:S(2)}) %all-to-all-start) | async-done | bytes 131104 | tf_op jit(solution)/shard_map/all_to_all | solution.py:215
  28.3 0.0 copy-done.16
  28.3 0.0 copy-start.2
  28.3 0.9 copy-done.2
  29.2 1.3 %shard_map.61 = (bf16[8,8,1152]{2,1,0:T(8,128)(2,1)S(1)}, bf16[2,64,512]{2,1,0:T(8,128)(2,1)S(1)}) custom-call(bf16[64,8,128]{2,1,0:T(8,128)(2,1)} %all-to-all-done.refs_0_, s32[2,64]{1,0:T(2,128)S(1)} %copy-done.16, f32[72,512]{1,0:T(8,128)S(1)} %pad_maximum_fusion.1.state_ref.refs_2_.refs_1_.refs_3_, bf16[8,8,1024]{2,1,0:T(8,128)(2,1)S(1)} %copy-done.2), custom_call_target="tpu_custom_call" | custom-call | bytes 2097152 | tf_op jit(solution)/shard_map/pallas_call | solution.py:239
  30.5 0.0 copy-start.3
  30.6 0.7 copy-done.3
  31.2 0.0 copy-start.9
  31.2 0.7 copy-done.9
  31.9 12.4 %all-to-all-start.1 = ((bf16[8,8,1152]{2,1,0:T(8,128)(2,1)}), bf16[8,8,1152]{2,1,0:T(8,128)(2,1)}, u32[]{:S(2)}, u32[]{:S(2)}) async-start(bf16[8,8,1152]{2,1,0:T(8,128)(2,1)} %copy-done.9), calls=%async_computation.1 | async-start | bytes 294912 | tf_op jit(solution)/shard_map/all_to_all | solution.py:248
  44.3 2.4 %collective-permute-start.2 = (bf16[2,64,512]{2,1,0:T(8,128)(2,1)}, bf16[2,64,512]{2,1,0:T(8,128)(2,1)S(1)}, u32[]{:S(2)}, u32[]{:S(2)}) collective-permute-start(bf16[2,64,512]{2,1,0:T(8,128)(2,1)} %copy-done.3), channel_id=1, source_target_pairs={{0,64},{64,0},{128,192},{192,128},{256,320},{320,256},{384,448},{4... | collective-permute-start | bytes 393224 | tf_op jit(solution)/shard_map/ppermute | solution.py:249
  46.7 1.2 %collective-permute-done.2.refs_6_ = bf16[2,64,512]{2,1,0:T(8,128)(2,1)S(1)} collective-permute-done((bf16[2,64,512]{2,1,0:T(8,128)(2,1)}, bf16[2,64,512]{2,1,0:T(8,128)(2,1)S(1)}, u32[]{:S(2)}, u32[]{:S(2)}) %collective-permute-start.2) | collective-permute-done | bytes 131104 | tf_op jit(solution)/shard_map/ppermute | solution.py:249
  47.9 0.0 copy-start.6
  47.9 0.6 copy-done.6
  48.5 13.5 %all-to-all-done.1.refs_0_ = bf16[8,8,1152]{2,1,0:T(8,128)(2,1)} async-done(((bf16[8,8,1152]{2,1,0:T(8,128)(2,1)}), bf16[8,8,1152]{2,1,0:T(8,128)(2,1)}, u32[]{:S(2)}, u32[]{:S(2)}) %all-to-all-start.1) | async-done | bytes 147488 | tf_op jit(solution)/shard_map/all_to_all | solution.py:248
  62.0 0.0 copy-start.4
  62.0 0.9 copy-done.4
  62.9 0.0 copy-start.7
  62.9 0.9 copy-done.7
  63.8 2.2 %shard_map.62 = (bf16[8,8,1152]{2,1,0:T(8,128)(2,1)S(1)}, f32[64,512]{1,0:T(8,128)S(1)}, f32[64,512]{1,0:T(8,128)S(1)}) custom-call(bf16[8,8,1152]{2,1,0:T(8,128)(2,1)} %all-to-all-done.1.refs_0_, f32[72,512]{1,0:T(8,128)S(1)} %pad_maximum_fusion.1.state_ref.refs_2_.refs_1_.refs_3_, f32[72,512]{1,0:T(8,128)S(1)} %collective-permute-done.state_taken_ref.refs_2_.refs_4_, ...), custom_call_target="tpu_custom_call" | custom-call | flops 134217728 | bytes 2097152 | tf_op jit(solution)/shard_map/pallas_call | solution.py:254
  65.9 0.0 copy-start.10
  66.0 0.7 copy-done.10
  66.6 0.0 copy-start.11
  66.6 0.7 copy-done.11
  67.3 0.0 copy-start.13
  67.3 0.6 copy-done.13
  67.9 4.0 %all-to-all-start.2 = ((bf16[8,8,1152]{2,1,0:T(8,128)(2,1)}), bf16[8,8,1152]{2,1,0:T(8,128)(2,1)}, u32[]{:S(2)}, u32[]{:S(2)}) async-start(bf16[8,8,1152]{2,1,0:T(8,128)(2,1)} %copy-done.10), calls=%async_computation.2 | async-start | bytes 294912 | tf_op jit(solution)/shard_map/all_to_all | solution.py:266
  71.9 0.9 slice.32
  72.9 16.0 %all-to-all-done.2.refs_0_ = bf16[8,8,1152]{2,1,0:T(8,128)(2,1)} async-done(((bf16[8,8,1152]{2,1,0:T(8,128)(2,1)}), bf16[8,8,1152]{2,1,0:T(8,128)(2,1)}, u32[]{:S(2)}, u32[]{:S(2)}) %all-to-all-start.2) | async-done | bytes 147488 | tf_op jit(solution)/shard_map/all_to_all | solution.py:266
  88.9 0.0 copy-start.5
  88.9 0.9 copy-done.5
  89.8 0.0 copy-start.8
  89.8 0.9 copy-done.8
  90.7 0.0 copy-start.12
  90.7 0.9 copy-done.12
  91.6 0.0 copy-start.14
  91.6 0.9 copy-done.14
  92.5 2.1 %shard_map.63 = (bf16[8,8,1024]{2,1,0:T(8,128)(2,1)S(1)}, f32[64,512]{1,0:T(8,128)}) custom-call(bf16[8,8,1152]{2,1,0:T(8,128)(2,1)} %all-to-all-done.2.refs_0_, f32[64,512]{1,0:T(8,128)S(1)} %copy-done.12, f32[64,512]{1,0:T(8,128)S(1)} %copy-done.14, f32[72,512]{1,0:T(8,128)S(1)} %pad_maximum_fusion.1.state_ref.refs_2_.refs_1_.refs_3_, ...), custom_call_target="tpu_custom_call" | custom-call | flops 134217728 | bytes 2097152 | tf_op jit(solution)/shard_map/pallas_call | solution.py:271
  94.6 0.0 copy-start.15
  94.7 0.6 copy-done.15
  95.3 3.4 %all-to-all-start.3 = ((bf16[8,8,1024]{2,1,0:T(8,128)(2,1)}), bf16[8,8,1024]{2,1,0:T(8,128)(2,1)S(1)}, u32[]{:S(2)}, u32[]{:S(2)}) async-start(bf16[8,8,1024]{2,1,0:T(8,128)(2,1)} %copy-done.15), calls=%async_computation.3 | async-start | bytes 262144 | tf_op jit(solution)/shard_map/all_to_all | solution.py:279
  98.7 0.9 slice.35
  99.7 15.8 %all-to-all-done.3 = bf16[8,8,1024]{2,1,0:T(8,128)(2,1)S(1)} async-done(((bf16[8,8,1024]{2,1,0:T(8,128)(2,1)}), bf16[8,8,1024]{2,1,0:T(8,128)(2,1)S(1)}, u32[]{:S(2)}, u32[]{:S(2)}) %all-to-all-start.3) | async-done | bytes 131104 | tf_op jit(solution)/shard_map/all_to_all | solution.py:279
  115.5 0.7 pad_maximum_fusion
  (11 shorter events, 0.1 us)
Async XLA Ops:
  0.6 2.9 %copy-start = (bf16[512,2048]{1,0:T(8,128)(2,1)S(1)}, bf16[512,2048]{1,0:T(8,128)(2,1)}, u32[]{:S(2)}) copy-start(bf16[512,2048]{1,0:T(8,128)(2,1)} %refs_7_.3) | copy-start | bytes 6291460
  0.6 17.9 %copy-start.18 = (s32[512]{0:T(512)S(1)}, s32[512]{0:T(512)}, u32[]{:S(2)}) copy-start(s32[512]{0:T(512)} %param.5) | copy-start | bytes 6148
  0.7 18.0 %copy-start.17 = (f32[512,64]{0,1:T(8,128)S(1)}, f32[512,64]{0,1:T(8,128)}, u32[]{:S(2)}) copy-start(f32[512,64]{0,1:T(8,128)} %param.6) | copy-start | bytes 393220
  4.7 23.6 %copy-start.16 = (s32[2,64]{1,0:T(2,128)S(1)}, s32[2,64]{1,0:T(2,128)}, u32[]{:S(2)}) copy-start(s32[2,64]{1,0:T(2,128)} %refs_1_.1) | copy-start | bytes 1540
  4.7 17.2 %collective-permute-start.1 = (bf16[512,1024]{1,0:T(8,128)(2,1)}, bf16[512,1024]{1,0:T(8,128)(2,1)S(1)}, u32[]{:S(2)}, u32[]{:S(2)}) collective-permute-start(bf16[512,1024]{1,0:T(8,128)(2,1)} %constant_dynamic-slice_fusion), channel_id=1, source_target_pairs={{0,64},{64,0},{128,192},{192,128},{256,320},{320,256},{384,448},{4... | collective-permute-start | bytes 3145736 | tf_op jit(solution)/shard_map/ppermute | solution.py:221
  6.7 21.6 %all-to-all-start = ((bf16[64,8,128]{2,1,0:T(8,128)(2,1)}), bf16[64,8,128]{2,1,0:T(8,128)(2,1)}, u32[]{:S(2)}, u32[]{:S(2)}) async-start(bf16[64,8,128]{2,1,0:T(8,128)(2,1)} %shard_map.59), calls=%async_computation | async-start | bytes 262144 | tf_op jit(solution)/shard_map/all_to_all | solution.py:215
  18.6 3.3 %collective-permute-start = (f32[72,512]{1,0:T(8,128)S(1)}, f32[72,512]{1,0:T(8,128)S(1)}, u32[]{:S(2)}, u32[]{:S(2)}) collective-permute-start(f32[72,512]{1,0:T(8,128)S(1)} %pad_maximum_fusion.1.state_ref.refs_2_.refs_1_.refs_3_), channel_id=1, source_target_pairs={{0,64},{64,0},{128,192},{192,128},{256,320},{320,256},{384,448},{4... | collective-permute-start | bytes 442376 | tf_op jit(solution)/shard_map/ppermute | solution.py:225
  22.8 0.7 copy-start.1
  28.3 0.9 copy-start.2
  30.5 0.7 copy-start.3
  31.2 0.7 copy-start.9
  31.9 30.1 %all-to-all-start.1 = ((bf16[8,8,1152]{2,1,0:T(8,128)(2,1)}), bf16[8,8,1152]{2,1,0:T(8,128)(2,1)}, u32[]{:S(2)}, u32[]{:S(2)}) async-start(bf16[8,8,1152]{2,1,0:T(8,128)(2,1)} %copy-done.9), calls=%async_computation.1 | async-start | bytes 294912 | tf_op jit(solution)/shard_map/all_to_all | solution.py:248
  44.3 3.6 %collective-permute-start.2 = (bf16[2,64,512]{2,1,0:T(8,128)(2,1)}, bf16[2,64,512]{2,1,0:T(8,128)(2,1)S(1)}, u32[]{:S(2)}, u32[]{:S(2)}) collective-permute-start(bf16[2,64,512]{2,1,0:T(8,128)(2,1)} %copy-done.3), channel_id=1, source_target_pairs={{0,64},{64,0},{128,192},{192,128},{256,320},{320,256},{384,448},{4... | collective-permute-start | bytes 393224 | tf_op jit(solution)/shard_map/ppermute | solution.py:249
  47.9 0.6 copy-start.6
  62.0 0.9 copy-start.4
  62.9 0.9 copy-start.7
  65.9 0.7 copy-start.10
  66.6 0.7 copy-start.11
  67.3 0.6 copy-start.13
  67.9 21.0 %all-to-all-start.2 = ((bf16[8,8,1152]{2,1,0:T(8,128)(2,1)}), bf16[8,8,1152]{2,1,0:T(8,128)(2,1)}, u32[]{:S(2)}, u32[]{:S(2)}) async-start(bf16[8,8,1152]{2,1,0:T(8,128)(2,1)} %copy-done.10), calls=%async_computation.2 | async-start | bytes 294912 | tf_op jit(solution)/shard_map/all_to_all | solution.py:266
  88.9 0.9 copy-start.5
  89.8 0.9 copy-start.8
  90.7 0.9 copy-start.12
  91.6 0.9 copy-start.14
  94.6 0.7 copy-start.15
  95.3 20.2 %all-to-all-start.3 = ((bf16[8,8,1024]{2,1,0:T(8,128)(2,1)}), bf16[8,8,1024]{2,1,0:T(8,128)(2,1)S(1)}, u32[]{:S(2)}, u32[]{:S(2)}) async-start(bf16[8,8,1024]{2,1,0:T(8,128)(2,1)} %copy-done.15), calls=%async_computation.3 | async-start | bytes 262144 | tf_op jit(solution)/shard_map/all_to_all | solution.py:279

commit v4 on v3

--- a/solution.py
+++ b/solution.py
@@ -16,12 +16,15 @@
 bf16 = jnp.bfloat16
 f32 = jnp.float32
 i32 = jnp.int32
+BlockSpec = pl.BlockSpec
 VMEM = pl.BlockSpec(memory_space=pltpu.VMEM)
 HBM = pl.BlockSpec(memory_space=pltpu.HBM)
 
 
 def call(body, out_shape, in_specs, scratch=(), flops=0, moved=0, room=16 << 20):
-    out_specs = jax.tree.map(lambda _: VMEM, out_shape)
+    out_specs = jax.tree.map(
+        lambda out: BlockSpec(memory_space=out.memory_space), out_shape, is_leaf=is_out
+    )
     return pl.pallas_call(
         body,
         out_shape=out_shape,
@@ -33,6 +36,33 @@
     )
 
 
+def is_out(value):
+    return hasattr(value, "memory_space")
+
+
+def far(values):
+    return pltpu.with_memory_space_constraint(values, pltpu.HBM)
+
+
+def load(pairs, sem_ref):
+    copies = [
+        pltpu.make_async_copy(source, target, sem_ref.at[i])
+        for i, (source, target) in enumerate(pairs)
+    ]
+    for copy in copies:
+        copy.start()
+    return copies
+
+
+def wait_all(copies):
+    for copy in copies:
+        copy.wait()
+
+
+def near(values):
+    return pltpu.with_memory_space_constraint(values, pltpu.VMEM)
+
+
 def rounded(values):
     return values.astype(bf16).astype(f32)
 
@@ -57,8 +87,13 @@
     return (onehot - prob).astype(bf16), prob
 
 
-def pick_body(win_ref, geno_ref, out_ref, block_ref, sem_ref):
+def pick_body(win_ref, geno_ref, out_ref, given_ref, block_ref, sem_ref):
     samples, columns = geno_ref.shape
+    half = given_ref.shape[1]
+    side = lax.rem(lax.axis_index("rows"), 2)
+    other = pl.multiple_of((1 - side) * half, LANES)
+    give = pltpu.make_async_copy(geno_ref.at[:, pl.ds(other, half)], given_ref, sem_ref.at[ITERS])
+    give.start()
     local = win_ref[...] - lax.axis_index("feat") * columns
     mine = jnp.where((local >= 0) & (local < columns), local, 0).astype(f32)
     copies, lanes = [], []
@@ -84,6 +119,7 @@
             here = rows == step * (samples // LANES) + j
             tile = tile + jnp.where(here, x[:, j * LANES : (j + 1) * LANES], 0.0)
     out_ref[...] = jnp.broadcast_to(tile.astype(bf16)[None], out_ref.shape)
+    give.wait()
 
 
 def load_halves(geno_ref, taken_ref, both_ref, sem_ref):
@@ -123,8 +159,8 @@
     return tile.astype(bf16)
 
 
-def coefficients(shared_ref, half):
-    tiles = shared_ref[:, :, half:].astype(f32)
+def coefficients(tiles):
+    tiles = tiles.astype(f32)
     row = jnp.sum(jnp.sum(tiles, axis=0), axis=0, keepdims=True)
     column = jnp.transpose(jnp.broadcast_to(row, (2 * K, LANES)))
     return shrink_rate * (2.0 * column[:K]) / (2.0 * column[K:] + ridge_term)
@@ -134,7 +170,33 @@
     return jnp.concatenate([values] * count, axis=1)
 
 
-def first_table_body(state_ref, state_taken_ref, geno_ref, taken_ref, out_ref, both_ref, sem_ref):
+def send_tile(tile, both_ref, out_ref, sem_ref):
+    half = out_ref.shape[2] - 2 * K
+    both_ref[...] = jnp.broadcast_to(tile[None], both_ref.shape)
+    copy = pltpu.make_async_copy(both_ref, out_ref.at[:, :, pl.ds(half, 2 * K)], sem_ref)
+    copy.start()
+    return copy
+
+
+def send_table(resid, resid_taken, both_ref, table_ref, out_ref, sem_ref, pieces=2):
+    whole = jnp.concatenate([resid, resid_taken], axis=1)
+    width = table_ref.shape[2] // pieces
+    copies = []
+    for piece in range(pieces):
+        span = pl.ds(piece * width, width)
+        table = jnp.dot(whole, both_ref[:, span], preferred_element_type=f32)
+        table_ref[:, :, span] = table.reshape(table_ref.shape[0], -1, width).astype(bf16)
+        copy = pltpu.make_async_copy(
+            table_ref.at[:, :, span], out_ref.at[:, :, span], sem_ref.at[piece]
+        )
+        copy.start()
+        copies.append(copy)
+    return copies
+
+
+def first_table_body(
+    state_ref, state_taken_ref, geno_ref, taken_ref, out_ref, both_ref, sem_ref
+):
     copies = load_halves(geno_ref, taken_ref, both_ref, sem_ref)
     resid, _ = residuals(state_ref[:K], state_ref[K : K + 1])
     resid_taken, _ = residuals(state_taken_ref[:K], state_taken_ref[K : K + 1])
@@ -144,12 +206,22 @@
     out_ref[...] = table.reshape(out_ref.shape).astype(bf16)
 
 
-def first_sums_body(cols_ref, win_ref, state_ref, table_ref, out_ref, picked_ref, *, columns):
+def first_sums_body(
+    cols_ref, far_win_ref, state_ref, table_ref, out_ref, far_picked_ref, tiles_ref, picked_ref,
+    win_ref, sem_ref, *, columns,
+):
     half = table_ref.shape[2]
-    feats = cols_ref.shape[0]
     blocks = state_ref.shape[1] // LANES
+    first = pltpu.make_async_copy(
+        table_ref, out_ref.at[:, :, pl.ds(0, half)], sem_ref.at[0]
+    )
+    wins = pltpu.make_async_copy(far_win_ref, win_ref, sem_ref.at[3])
+    wins.start()
+    first.start()
+    resid, prob = residuals(state_ref[:K], state_ref[K : K + 1])
     cols = cols_ref[...].astype(f32)
-    feat = lax.broadcasted_iota(i32, (feats, K), 0)
+    feat = lax.broadcasted_iota(i32, (cols.shape[0], K), 0)
+    wins.wait()
     for step in range(ITERS):
         owner = win_ref[step : step + 1] // columns
         place = jnp.where(feat == owner, 1.0, 0.0).astype(bf16)
@@ -159,37 +231,91 @@
                 place, piece, (((0,), (0,)), ((), ())), preferred_element_type=f32
             )
             picked_ref[step, :, j * LANES : (j + 1) * LANES] = picked.astype(bf16)
-    resid, prob = residuals(state_ref[:K], state_ref[K : K + 1])
+    third = pltpu.make_async_copy(picked_ref, far_picked_ref, sem_ref.at[2])
+    third.start()
     tile = sums_tile(resid, prob, picked_ref[0].astype(f32))
-    out_ref[:, :, :half] = table_ref[...]
-    out_ref[:, :, half:] = jnp.broadcast_to(tile[None], (out_ref.shape[0], 8, 2 * K))
-
-
-def next_table_body(
-    shared_ref, logits_ref, logits_taken_ref, state_ref, state_taken_ref, picked_ref,
-    picked_taken_ref, geno_ref, taken_ref, out_ref, new_ref, *rest, step,
+    second = send_tile(tile, tiles_ref, out_ref, sem_ref.at[1])
+    wait_all([first, second, third])
+
+
+def second_table_body(
+    shared_ref, state_ref, far_state_ref, far_picked_ref, far_picked_taken_ref, geno_ref,
+    taken_ref, out_ref, far_coef_ref, both_ref, table_ref, tiles_ref, got_ref, state_taken_ref,
+    picked_ref, picked_taken_ref, coef_ref, sem_ref, load_ref,
 ):
     half = taken_ref.shape[1]
-    last = step == ITERS - 1
-    new_taken_ref = None if last else rest[0]
-    both_ref, sem_ref = rest[-2:]
+    loads = load(
+        [
+            (shared_ref.at[:, :, pl.ds(half, 2 * K)], got_ref),
+            (far_picked_ref, picked_ref),
+            (far_state_ref, state_taken_ref),
+            (far_picked_taken_ref, picked_taken_ref),
+        ],
+        load_ref,
+    )
     copies = load_halves(geno_ref, taken_ref, both_ref, sem_ref)
-    coef = coefficients(shared_ref, half)
-    coef = lane_tile(coef, new_ref.shape[1] // LANES)
-    logits = logits_ref[:K] + coef * picked_ref[step].astype(f32)
+    loads[0].wait()
+    coef = coefficients(got_ref[...])
+    coef_ref[...] = coef
+    coef_copy = pltpu.make_async_copy(coef_ref, far_coef_ref, sem_ref.at[5])
+    coef_copy.start()
+    coef = lane_tile(coef, state_ref.shape[1] // LANES)
+    loads[1].wait()
+    logits = state_ref[:K] + coef * picked_ref[0].astype(f32)
+    resid, prob = residuals(logits, state_ref[K : K + 1])
+    tile = sums_tile(resid, prob, picked_ref[1].astype(f32))
+    sums_copy = send_tile(tile, tiles_ref, out_ref, sem_ref.at[2])
+    wait_all(loads[2:])
+    logits_taken = state_taken_ref[:K] + coef * picked_taken_ref[0].astype(f32)
+    resid_taken, _ = residuals(logits_taken, state_taken_ref[K : K + 1])
+    wait_all(copies)
+    table_copies = send_table(
+        resid, resid_taken, both_ref, table_ref, out_ref, sem_ref.at[pl.ds(3, 2)]
+    )
+    wait_all([coef_copy, sums_copy] + table_copies)
+
+
+def third_table_body(
+    shared_ref, far_coef_ref, state_ref, far_state_ref, far_picked_ref, far_picked_taken_ref,
+    geno_ref, taken_ref, out_ref, logits_ref, both_ref, table_ref, new_ref, got_ref,
+    state_taken_ref, picked_ref, picked_taken_ref, coef_ref, sem_ref, load_ref,
+):
+    half = taken_ref.shape[1]
+    loads = load(
+        [
+            (shared_ref.at[:, :, pl.ds(half, 2 * K)], got_ref),
+            (far_coef_ref, coef_ref),
+            (far_picked_ref, picked_ref),
+            (far_state_ref, state_taken_ref),
+            (far_picked_taken_ref, picked_taken_ref),
+        ],
+        load_ref,
+    )
+    copies = load_halves(geno_ref, taken_ref, both_ref, sem_ref)
+    blocks = state_ref.shape[1] // LANES
+    wait_all(loads[:2])
+    coefs = [lane_tile(coef, blocks) for coef in (coef_ref[...], coefficients(got_ref[...]))]
+
+    def updated(start, columns_ref):
+        for step in range(ITERS):
+            start = start + coefs[step] * columns_ref[step].astype(f32)
+        return start
+
+    loads[2].wait()
+    logits = updated(state_ref[:K], picked_ref)
     new_ref[...] = logits
-    resid, prob = residuals(logits, state_ref[K : K + 1])
-    if not last:
-        tile = sums_tile(resid, prob, picked_ref[step + 1].astype(f32))
-        out_ref[:, :, half:] = jnp.broadcast_to(tile[None], (out_ref.shape[0], 8, 2 * K))
-    logits_taken = logits_taken_ref[:K] + coef * picked_taken_ref[step].astype(f32)
-    if not last:
-        new_taken_ref[...] = logits_taken
-    resid_taken, _ = residuals(logits_taken, state_taken_ref[K : K + 1])
-    for copy in copies:
-        copy.wait()
-    table = half_table(resid, resid_taken, both_ref)
-    out_ref[:, :, :half] = table.reshape(out_ref.shape[0], -1, half).astype(bf16)
+    logits_copy = pltpu.make_async_copy(new_ref, logits_ref, sem_ref.at[2])
+    logits_copy.start()
+    resid, _ = residuals(logits, state_ref[K : K + 1])
+    wait_all(loads[3:])
+    resid_taken, _ = residuals(
+        updated(state_taken_ref[:K], picked_taken_ref), state_taken_ref[K : K + 1]
+    )
+    wait_all(copies)
+    table_copies = send_table(
+        resid, resid_taken, both_ref, table_ref, out_ref, sem_ref.at[pl.ds(3, 2)]
+    )
+    wait_all([logits_copy] + table_copies)
 
 
 def shards(genotypes, labels, base_margin, winners):
@@ -198,37 +324,48 @@
     rows_count = lax.axis_size("rows")
     class_share = K // rows_count
     half = columns // 2
-    side = lax.rem(lax.axis_index("rows"), 2)
     partners = [(i, i ^ 1) for i in range(rows_count)]
-    shape = jax.ShapeDtypeStruct
     work = 2 * K * 2 * samples * half
-    halves = [pltpu.VMEM((2 * samples, half), bf16), pltpu.SemaphoreType.DMA((2,))]
-
-    sent = call(
+    payload_shape = (rows_count, class_share, half + 2 * K)
+    table_shape = (rows_count, class_share, half)
+    tiles = pltpu.VMEM((rows_count, 8, 2 * K), bf16)
+    both = pltpu.VMEM((2 * samples, half), bf16)
+    sems = pltpu.SemaphoreType.DMA
+    loaded = [
+        tiles,
+        pltpu.VMEM((K + 8, samples), f32),
+        pltpu.VMEM((ITERS, K, samples), bf16),
+        pltpu.VMEM((ITERS, K, samples), bf16),
+        pltpu.VMEM((K, LANES), f32),
+    ]
+
+    sent, given = call(
         pick_body,
-        shape((feat_count, ITERS * samples // LANES, LANES), bf16),
+        (
+            pltpu.VMEM((feat_count, ITERS * samples // LANES, LANES), bf16),
+            pltpu.HBM((samples, half), bf16),
+        ),
         [VMEM, HBM],
-        [pltpu.VMEM((ITERS, samples, LANES), bf16), pltpu.SemaphoreType.DMA((ITERS,))],
+        [pltpu.VMEM((ITERS, samples, LANES), bf16), sems((ITERS + 1,))],
         moved=samples * LANES * 4,
         room=None,
     )(winners, genotypes)
     cols = lax.all_to_all(sent, "feat", 0, 0, tiled=True)
 
-    sent, geno, margin, marks = lax.optimization_barrier(
-        (sent, genotypes, base_margin, labels)
-    )
-    given = lax.dynamic_slice_in_dim(geno, (1 - side) * half, half, 1)
-    taken = lax.ppermute(given, "rows", partners)
+    sent, margin, marks = lax.optimization_barrier((sent, base_margin, labels))
     state = jnp.concatenate(
         [margin.T, jnp.broadcast_to(marks.astype(f32)[None, :], (8, samples))]
     )
-    state_taken = lax.ppermute(state, "rows", partners)
+    state, given = lax.optimization_barrier((state, given))
+    taken = lax.ppermute(given, "rows", partners)
+    state_taken = far(lax.ppermute(state, "rows", partners))
+    state = near(state)
 
     table = call(
         first_table_body,
-        shape((rows_count, class_share, half), bf16),
+        pltpu.VMEM(table_shape, bf16),
         [VMEM, VMEM, HBM, HBM],
-        halves,
+        [both, sems((2,))],
         flops=work,
         moved=4 * samples * half,
     )(state, state_taken, genotypes, taken)
@@ -238,44 +375,34 @@
 
     payload, picked = call(
         first_sums,
-        (
-            shape((rows_count, class_share, half + 2 * K), bf16),
-            shape((ITERS, K, samples), bf16),
-        ),
-        [VMEM] * 4,
+        (pltpu.HBM(payload_shape, bf16), pltpu.HBM((ITERS, K, samples), bf16)),
+        [VMEM, HBM, VMEM, VMEM],
+        [tiles, pltpu.VMEM((ITERS, K, samples), bf16), pltpu.VMEM((ITERS, K), i32), sems((4,))],
         moved=4 * samples * half,
-    )(cols, winners, state, table)
+    )(near(cols), far(winners), state, table)
     shared0 = lax.all_to_all(payload, "rows", 0, 0, tiled=True)
-    picked_taken = lax.ppermute(picked, "rows", partners)
-
-    def second(*refs):
-        next_table_body(*refs, step=0)
-
-    payload, logits, logits_taken = call(
-        second,
-        (
-            shape((rows_count, class_share, half + 2 * K), bf16),
-            shape((K, samples), f32),
-            shape((K, samples), f32),
-        ),
-        [VMEM] * 7 + [HBM] * 2,
-        halves,
+    picked_taken = far(lax.ppermute(picked, "rows", partners))
+
+    payload, coef = call(
+        second_table_body,
+        (pltpu.HBM(payload_shape, bf16), pltpu.HBM((K, LANES), f32)),
+        [HBM, VMEM] + [HBM] * 5,
+        [both, pltpu.VMEM(table_shape, bf16), tiles] + loaded + [sems((6,)), sems((4,))],
         flops=work,
         moved=4 * samples * half,
-    )(shared0, state, state_taken, state, state_taken, picked, picked_taken, genotypes, taken)
+    )(far(shared0), state, state_taken, picked, picked_taken, genotypes, taken)
     shared1 = lax.all_to_all(payload, "rows", 0, 0, tiled=True)
 
-    def third(*refs):
-        next_table_body(*refs, step=1)
-
     payload, logits = call(
-        third,
-        (shape((rows_count, class_share, half), bf16), shape((K, samples), f32)),
-        [VMEM] * 7 + [HBM] * 2,
-        halves,
+        third_table_body,
+        (pltpu.HBM(table_shape, bf16), pltpu.HBM((K, samples), f32)),
+        [HBM, HBM, VMEM] + [HBM] * 5,
+        [both, pltpu.VMEM(table_shape, bf16), pltpu.VMEM((K, samples), f32)]
+        + loaded
+        + [sems((5,)), sems((5,))],
         flops=work,
         moved=4 * samples * half,
-    )(shared1, logits, logits_taken, state, state_taken, picked, picked_taken, genotypes, taken)
+    )(far(shared1), far(coef), state, state_taken, picked, picked_taken, genotypes, taken)
     shared2 = lax.all_to_all(payload, "rows", 0, 0, tiled=True)
 
     tables = []

time: 117 us -> 140 us (1.20)
  Pallas kernels: 9.32 us -> 42.8 us
  local copies, waits for them, and re-layouts: 14.5 us -> 3.43 us
    pallas_call x5, Pallas kernels: 9.32 us -> 42.8 us  [the longest x1 34.4 us: shards(): call(pick_body, (pltpu.VMEM((feat_count, ITERS * samples // LANES, LANES)...]
    unnamed x38 -> x12, local copies, waits for them, and re-layouts: 11.6 us -> 1.58 us
  transfers between devices with their start and end apart: 7 -> 7, of which waited for: 6 -> 6; matrix products, arithmetic and copies ran while one was open for 2% -> 1% of each run, Pallas kernels for 1% -> 1%
where the time goes in v4:
time: 140 us; the launch traced here: 139 us
  waiting for transfers between devices  52.6 us (38%)
  Pallas kernels  42.8 us (31%)
  starting transfers between devices  37.8 us (27%)
  local copies, waits for them, and re-layouts  3.43 us (2%)
  other arithmetic  1.69 us (1%)
    pallas_call x1, Pallas kernels, shards(): call(pick_body, (pltpu.VMEM((feat_count, ITERS * samples // LANES, LANES)...  34.4 us
    all_to_all x1, waiting for transfers between devices, shards(): shared1 = lax.all_to_all(payload, 'rows', 0, 0, tiled=True)  16 us
    all_to_all x1, waiting for transfers between devices, shards(): shared2 = lax.all_to_all(payload, 'rows', 0, 0, tiled=True)  15.8 us
    all_to_all x1, waiting for transfers between devices, shards(): shared0 = lax.all_to_all(payload, 'rows', 0, 0, tiled=True)  14.1 us
    all_to_all x1, starting transfers between devices, shards(): shared0 = lax.all_to_all(payload, 'rows', 0, 0, tiled=True)  12.5 us
    all_to_all x1, starting transfers between devices, shards(): cols = lax.all_to_all(sent, 'feat', 0, 0, tiled=True)  11.7 us
    all_to_all x1, waiting for transfers between devices, shards(): cols = lax.all_to_all(sent, 'feat', 0, 0, tiled=True)  4.07 us
    all_to_all x1, starting transfers between devices, shards(): shared1 = lax.all_to_all(payload, 'rows', 0, 0, tiled=True)  4.01 us
  transfers between devices with their start and end apart: 7, of which 6 were waited for; matrix products, arithmetic and copies ran while one was open for 1% of the time, Pallas kernels for 1%

profile of v4, /device:TPU:32, one launch (start us, length us, event | category | flops | bytes accessed | tf_op | source)
XLA Modules:
  0.0 139.1 jit_solution(8490324452311026044)
XLA Ops:
  0.6 0.0 copy-start
  0.6 0.0 copy-start.5
  0.6 34.4 %shard_map.59 = (bf16[64,8,128]{2,1,0:T(8,128)(2,1)}, bf16[512,1024]{1,0:T(8,128)(2,1)}) custom-call(s32[2,64]{1,0:T(2,128)} %refs_1_.1, bf16[512,2048]{1,0:T(8,128)(2,1)} %geno_ref.7), custom_call_target="tpu_custom_call" | custom-call | bytes 262144 | tf_op jit(solution)/shard_map/pallas_call | solution.py:342
  35.0 0.0 copy-done.5
  35.1 0.9 pad_maximum_fusion.1.state_ref.refs_2_
  36.0 1.9 %collective-permute-start.1 = (bf16[512,1024]{1,0:T(8,128)(2,1)}, bf16[512,1024]{1,0:T(8,128)(2,1)S(1)}, u32[]{:S(2)}, u32[]{:S(2)}) collective-permute-start(bf16[512,1024]{1,0:T(8,128)(2,1)} %get-tuple-element.19), channel_id=1, source_target_pairs={{0,64},{64,0},{128,192},{192,128},{256,320},{320,256},{384,448},{4... | collective-permute-start | bytes 3145736 | tf_op jit(solution)/shard_map/ppermute | solution.py:360
  37.9 11.7 %all-to-all-start = ((bf16[64,8,128]{2,1,0:T(8,128)(2,1)}), bf16[64,8,128]{2,1,0:T(8,128)(2,1)S(1)}, u32[]{:S(2)}, u32[]{:S(2)}) async-start(bf16[64,8,128]{2,1,0:T(8,128)(2,1)} %get-tuple-element.14), calls=%async_computation | async-start | bytes 262144 | tf_op jit(solution)/shard_map/all_to_all | solution.py:353
  49.6 1.9 %collective-permute-start = (f32[72,512]{1,0:T(8,128)S(1)}, f32[72,512]{1,0:T(8,128)S(1)}, u32[]{:S(2)}, u32[]{:S(2)}) collective-permute-start(f32[72,512]{1,0:T(8,128)S(1)} %pad_maximum_fusion.1.state_ref.refs_2_), channel_id=1, source_target_pairs={{0,64},{64,0},{128,192},{192,128},{256,320},{320,256},{384,448},{4... | collective-permute-start | bytes 442376 | tf_op jit(solution)/shard_map/ppermute | solution.py:361
  51.5 1.3 collective-permute-done.state_taken_ref.far_state_ref
  52.9 0.0 copy-start.3
  52.9 0.0 collective-permute-done.1.taken_ref
  52.9 0.7 copy-done.3
  53.5 0.0 copy-done
  53.5 1.8 %shard_map.60.refs_3_ = bf16[8,8,1024]{2,1,0:T(8,128)(2,1)S(1)} custom-call(f32[72,512]{1,0:T(8,128)S(1)} %pad_maximum_fusion.1.state_ref.refs_2_, f32[72,512]{1,0:T(8,128)} %copy-done.3, bf16[512,2048]{1,0:T(8,128)(2,1)S(1)} %copy-done, bf16[512,1024]{1,0:T(8,128)(2,1)S(1)} %collective-permute-done.1.taken_ref), custom_call_target="tpu_custom_call" | custom-call | flops 134217728 | bytes 2097152 | tf_op jit(solution)/shard_map/pallas_call | solution.py:364
  55.3 4.1 %all-to-all-done.refs_0_ = bf16[64,8,128]{2,1,0:T(8,128)(2,1)S(1)} async-done(((bf16[64,8,128]{2,1,0:T(8,128)(2,1)}), bf16[64,8,128]{2,1,0:T(8,128)(2,1)S(1)}, u32[]{:S(2)}, u32[]{:S(2)}) %all-to-all-start) | async-done | bytes 131104 | tf_op jit(solution)/shard_map/all_to_all | solution.py:353
  59.4 1.8 %shard_map.61 = (bf16[8,8,1152]{2,1,0:T(8,128)(2,1)}, bf16[2,64,512]{2,1,0:T(8,128)(2,1)}) custom-call(bf16[64,8,128]{2,1,0:T(8,128)(2,1)S(1)} %all-to-all-done.refs_0_, s32[2,64]{1,0:T(2,128)} %refs_1_.1, f32[72,512]{1,0:T(8,128)S(1)} %pad_maximum_fusion.1.state_ref.refs_2_, bf16[8,8,1024]{2,1,0:T(8,128)(2,1)S(1)} %shard_map.60.refs_3_), custom_call_target="tpu_custom_call" | custom-call | bytes 2097152 | tf_op jit(solution)/shard_map/pallas_call | solution.py:376
  61.2 0.0 copy-start.2
  61.2 12.5 %all-to-all-start.1 = ((bf16[8,8,1152]{2,1,0:T(8,128)(2,1)}), bf16[8,8,1152]{2,1,0:T(8,128)(2,1)}, u32[]{:S(2)}, u32[]{:S(2)}) async-start(bf16[8,8,1152]{2,1,0:T(8,128)(2,1)} %get-tuple-element.20), calls=%async_computation.1 | async-start | bytes 294912 | tf_op jit(solution)/shard_map/all_to_all | solution.py:383
  73.7 2.4 %collective-permute-start.2 = (bf16[2,64,512]{2,1,0:T(8,128)(2,1)}, bf16[2,64,512]{2,1,0:T(8,128)(2,1)S(1)}, u32[]{:S(2)}, u32[]{:S(2)}) collective-permute-start(bf16[2,64,512]{2,1,0:T(8,128)(2,1)} %get-tuple-element.21.far_picked_ref), channel_id=1, source_target_pairs={{0,64},{64,0},{128,192},{192,128},{256,320},{320,256},{384,448},{4... | collective-permute-start | bytes 393224 | tf_op jit(solution)/shard_map/ppermute | solution.py:384
  76.1 1.2 collective-permute-done.2.far_picked_taken_ref
  77.3 0.0 copy-start.4
  77.3 14.1 %all-to-all-done.1.shared_ref = bf16[8,8,1152]{2,1,0:T(8,128)(2,1)} async-done(((bf16[8,8,1152]{2,1,0:T(8,128)(2,1)}), bf16[8,8,1152]{2,1,0:T(8,128)(2,1)}, u32[]{:S(2)}, u32[]{:S(2)}) %all-to-all-start.1) | async-done | bytes 147488 | tf_op jit(solution)/shard_map/all_to_all | solution.py:383
  91.4 0.0 copy-done.4
  91.4 0.0 copy-start.1
  91.4 0.9 copy-done.1
  92.3 2.4 %shard_map.62 = (bf16[8,8,1152]{2,1,0:T(8,128)(2,1)}, f32[64,128]{1,0:T(8,128)}) custom-call(bf16[8,8,1152]{2,1,0:T(8,128)(2,1)} %all-to-all-done.1.shared_ref, f32[72,512]{1,0:T(8,128)S(1)} %pad_maximum_fusion.1.state_ref.refs_2_, f32[72,512]{1,0:T(8,128)} %copy-done.3, bf16[2,64,512]{2,1,0:T(8,128)(2,1)S(1)} %copy-done.1, bf16[2,64,512]{2,1,0:T(8,128)(2,1)} %copy-done.4, ...), custom_call_target="tpu_custom_call" | custom-call | flops 134217728 | bytes 2097152 | tf_op jit(solution)/shard_map/pallas_call | solution.py:386
  94.7 4.0 %all-to-all-start.2 = ((bf16[8,8,1152]{2,1,0:T(8,128)(2,1)}), bf16[8,8,1152]{2,1,0:T(8,128)(2,1)}, u32[]{:S(2)}, u32[]{:S(2)}) async-start(bf16[8,8,1152]{2,1,0:T(8,128)(2,1)} %get-tuple-element.22), calls=%async_computation.2 | async-start | bytes 294912 | tf_op jit(solution)/shard_map/all_to_all | solution.py:394
  98.8 0.9 slice.32
  99.7 16.0 %all-to-all-done.2.shared_ref = bf16[8,8,1152]{2,1,0:T(8,128)(2,1)} async-done(((bf16[8,8,1152]{2,1,0:T(8,128)(2,1)}), bf16[8,8,1152]{2,1,0:T(8,128)(2,1)}, u32[]{:S(2)}, u32[]{:S(2)}) %all-to-all-start.2) | async-done | bytes 147488 | tf_op jit(solution)/shard_map/all_to_all | solution.py:394
  115.8 0.0 copy-done.2
  115.8 2.4 %shard_map.63 = (bf16[8,8,1024]{2,1,0:T(8,128)(2,1)}, f32[64,512]{1,0:T(8,128)}) custom-call(bf16[8,8,1152]{2,1,0:T(8,128)(2,1)} %all-to-all-done.2.shared_ref, f32[64,128]{1,0:T(8,128)} %get-tuple-element.23.far_coef_ref, f32[72,512]{1,0:T(8,128)S(1)} %pad_maximum_fusion.1.state_ref.refs_2_, f32[72,512]{1,0:T(8,128)} %copy-done.3, ...), custom_call_target="tpu_custom_call" | custom-call | flops 134217728 | bytes 2097152 | tf_op jit(solution)/shard_map/pallas_call | solution.py:396
  118.2 3.4 %all-to-all-start.3 = ((bf16[8,8,1024]{2,1,0:T(8,128)(2,1)}), bf16[8,8,1024]{2,1,0:T(8,128)(2,1)S(1)}, u32[]{:S(2)}, u32[]{:S(2)}) async-start(bf16[8,8,1024]{2,1,0:T(8,128)(2,1)} %get-tuple-element.25), calls=%async_computation.3 | async-start | bytes 262144 | tf_op jit(solution)/shard_map/all_to_all | solution.py:406
  121.6 0.9 slice.35
  122.6 15.8 %all-to-all-done.3 = bf16[8,8,1024]{2,1,0:T(8,128)(2,1)S(1)} async-done(((bf16[8,8,1024]{2,1,0:T(8,128)(2,1)}), bf16[8,8,1024]{2,1,0:T(8,128)(2,1)S(1)}, u32[]{:S(2)}, u32[]{:S(2)}) %all-to-all-start.3) | async-done | bytes 131104 | tf_op jit(solution)/shard_map/all_to_all | solution.py:406
  138.5 0.7 pad_maximum_fusion
  (10 shorter events, 0.1 us)
Async XLA Ops:
  0.6 52.9 %copy-start = (bf16[512,2048]{1,0:T(8,128)(2,1)S(1)}, bf16[512,2048]{1,0:T(8,128)(2,1)}, u32[]{:S(2)}) copy-start(bf16[512,2048]{1,0:T(8,128)(2,1)} %geno_ref.7) | copy-start | bytes 6291460
  0.6 34.4 %copy-start.5 = (s32[512]{0:T(512)S(1)}, s32[512]{0:T(512)}, u32[]{:S(2)}) copy-start(s32[512]{0:T(512)} %param.5) | copy-start | bytes 6148
  36.0 16.9 %collective-permute-start.1 = (bf16[512,1024]{1,0:T(8,128)(2,1)}, bf16[512,1024]{1,0:T(8,128)(2,1)S(1)}, u32[]{:S(2)}, u32[]{:S(2)}) collective-permute-start(bf16[512,1024]{1,0:T(8,128)(2,1)} %get-tuple-element.19), channel_id=1, source_target_pairs={{0,64},{64,0},{128,192},{192,128},{256,320},{320,256},{384,448},{4... | collective-permute-start | bytes 3145736 | tf_op jit(solution)/shard_map/ppermute | solution.py:360
  37.9 21.5 %all-to-all-start = ((bf16[64,8,128]{2,1,0:T(8,128)(2,1)}), bf16[64,8,128]{2,1,0:T(8,128)(2,1)S(1)}, u32[]{:S(2)}, u32[]{:S(2)}) async-start(bf16[64,8,128]{2,1,0:T(8,128)(2,1)} %get-tuple-element.14), calls=%async_computation | async-start | bytes 262144 | tf_op jit(solution)/shard_map/all_to_all | solution.py:353
  49.6 3.3 %collective-permute-start = (f32[72,512]{1,0:T(8,128)S(1)}, f32[72,512]{1,0:T(8,128)S(1)}, u32[]{:S(2)}, u32[]{:S(2)}) collective-permute-start(f32[72,512]{1,0:T(8,128)S(1)} %pad_maximum_fusion.1.state_ref.refs_2_), channel_id=1, source_target_pairs={{0,64},{64,0},{128,192},{192,128},{256,320},{320,256},{384,448},{4... | collective-permute-start | bytes 442376 | tf_op jit(solution)/shard_map/ppermute | solution.py:361
  52.9 0.7 copy-start.3
  61.2 54.6 %copy-start.2 = (bf16[2,64,512]{2,1,0:T(8,128)(2,1)S(1)}, bf16[2,64,512]{2,1,0:T(8,128)(2,1)}, u32[]{:S(2)}) copy-start(bf16[2,64,512]{2,1,0:T(8,128)(2,1)} %get-tuple-element.21.far_picked_ref) | copy-start | bytes 393220
  61.2 30.2 %all-to-all-start.1 = ((bf16[8,8,1152]{2,1,0:T(8,128)(2,1)}), bf16[8,8,1152]{2,1,0:T(8,128)(2,1)}, u32[]{:S(2)}, u32[]{:S(2)}) async-start(bf16[8,8,1152]{2,1,0:T(8,128)(2,1)} %get-tuple-element.20), calls=%async_computation.1 | async-start | bytes 294912 | tf_op jit(solution)/shard_map/all_to_all | solution.py:383
  73.7 3.6 %collective-permute-start.2 = (bf16[2,64,512]{2,1,0:T(8,128)(2,1)}, bf16[2,64,512]{2,1,0:T(8,128)(2,1)S(1)}, u32[]{:S(2)}, u32[]{:S(2)}) collective-permute-start(bf16[2,64,512]{2,1,0:T(8,128)(2,1)} %get-tuple-element.21.far_picked_ref), channel_id=1, source_target_pairs={{0,64},{64,0},{128,192},{192,128},{256,320},{320,256},{384,448},{4... | collective-permute-start | bytes 393224 | tf_op jit(solution)/shard_map/ppermute | solution.py:384
  77.3 14.1 %copy-start.4 = (bf16[2,64,512]{2,1,0:T(8,128)(2,1)}, bf16[2,64,512]{2,1,0:T(8,128)(2,1)S(1)}, u32[]{:S(2)}) copy-start(bf16[2,64,512]{2,1,0:T(8,128)(2,1)S(1)} %collective-permute-done.2.far_picked_taken_ref) | copy-start | bytes 393220
  91.4 0.9 copy-start.1
  94.7 21.0 %all-to-all-start.2 = ((bf16[8,8,1152]{2,1,0:T(8,128)(2,1)}), bf16[8,8,1152]{2,1,0:T(8,128)(2,1)}, u32[]{:S(2)}, u32[]{:S(2)}) async-start(bf16[8,8,1152]{2,1,0:T(8,128)(2,1)} %get-tuple-element.22), calls=%async_computation.2 | async-start | bytes 294912 | tf_op jit(solution)/shard_map/all_to_all | solution.py:394
  118.2 20.2 %all-to-all-start.3 = ((bf16[8,8,1024]{2,1,0:T(8,128)(2,1)}), bf16[8,8,1024]{2,1,0:T(8,128)(2,1)S(1)}, u32[]{:S(2)}, u32[]{:S(2)}) async-start(bf16[8,8,1024]{2,1,0:T(8,128)(2,1)} %get-tuple-element.25), calls=%async_computation.3 | async-start | bytes 262144 | tf_op jit(solution)/shard_map/all_to_all | solution.py:406

commit v5 on v4

--- a/solution.py
+++ b/solution.py
@@ -87,13 +87,19 @@
     return (onehot - prob).astype(bf16), prob
 
 
-def pick_body(win_ref, geno_ref, out_ref, given_ref, block_ref, sem_ref):
+def pick_body(
+    win_ref, geno_ref, margin_ref, labels_ref, out_ref, given_ref, state_ref, block_ref, half_ref,
+    sem_ref,
+):
     samples, columns = geno_ref.shape
     half = given_ref.shape[1]
     side = lax.rem(lax.axis_index("rows"), 2)
     other = pl.multiple_of((1 - side) * half, LANES)
-    give = pltpu.make_async_copy(geno_ref.at[:, pl.ds(other, half)], given_ref, sem_ref.at[ITERS])
+    give = pltpu.make_async_copy(geno_ref.at[:, pl.ds(other, half)], half_ref, sem_ref.at[ITERS])
     give.start()
+    margins = pltpu.make_async_copy(margin_ref, state_ref.at[pl.ds(0, K)], sem_ref.at[ITERS + 1])
+    margins.start()
+    state_ref[K:] = jnp.broadcast_to(labels_ref[...].astype(f32), (8, samples))
     local = win_ref[...] - lax.axis_index("feat") * columns
     mine = jnp.where((local >= 0) & (local < columns), local, 0).astype(f32)
     copies, lanes = [], []
@@ -109,6 +115,9 @@
     rows = lax.broadcasted_iota(i32, (8, LANES), 0)
     lane = lax.broadcasted_iota(i32, (8, LANES), 1)
     tile = jnp.zeros((8, LANES), f32)
+    give.wait()
+    give = pltpu.make_async_copy(half_ref, given_ref, sem_ref.at[ITERS])
+    give.start()
     for step in range(ITERS):
         copies[step].wait()
         pick = jnp.where(lane == lanes[step], 1.0, 0.0).astype(bf16)
@@ -119,6 +128,7 @@
             here = rows == step * (samples // LANES) + j
             tile = tile + jnp.where(here, x[:, j * LANES : (j + 1) * LANES], 0.0)
     out_ref[...] = jnp.broadcast_to(tile.astype(bf16)[None], out_ref.shape)
+    margins.wait()
     give.wait()
 
 
@@ -339,24 +349,24 @@
         pltpu.VMEM((K, LANES), f32),
     ]
 
-    sent, given = call(
+    sent, given, state = call(
         pick_body,
         (
             pltpu.VMEM((feat_count, ITERS * samples // LANES, LANES), bf16),
             pltpu.HBM((samples, half), bf16),
+            pltpu.VMEM((K + 8, samples), f32),
         ),
-        [VMEM, HBM],
-        [pltpu.VMEM((ITERS, samples, LANES), bf16), sems((ITERS + 1,))],
+        [VMEM, HBM, HBM, VMEM],
+        [
+            pltpu.VMEM((ITERS, samples, LANES), bf16),
+            pltpu.VMEM((samples, half), bf16),
+            sems((ITERS + 2,)),
+        ],
         moved=samples * LANES * 4,
         room=None,
-    )(winners, genotypes)
+    )(winners, far(genotypes), far(base_margin.T), labels[None, :])
     cols = lax.all_to_all(sent, "feat", 0, 0, tiled=True)
 
-    sent, margin, marks = lax.optimization_barrier((sent, base_margin, labels))
-    state = jnp.concatenate(
-        [margin.T, jnp.broadcast_to(marks.astype(f32)[None, :], (8, samples))]
-    )
-    state, given = lax.optimization_barrier((state, given))
     taken = lax.ppermute(given, "rows", partners)
     state_taken = far(lax.ppermute(state, "rows", partners))
     state = near(state)
@@ -390,7 +400,7 @@
         [both, pltpu.VMEM(table_shape, bf16), tiles] + loaded + [sems((6,)), sems((4,))],
         flops=work,
         moved=4 * samples * half,
-    )(far(shared0), state, state_taken, picked, picked_taken, genotypes, taken)
+    )(far(shared0), state, state_taken, far(picked), picked_taken, genotypes, taken)
     shared1 = lax.all_to_all(payload, "rows", 0, 0, tiled=True)
 
     payload, logits = call(
@@ -402,7 +412,7 @@
         + [sems((5,)), sems((5,))],
         flops=work,
         moved=4 * samples * half,
-    )(far(shared1), far(coef), state, state_taken, picked, picked_taken, genotypes, taken)
+    )(far(shared1), far(coef), state, state_taken, far(picked), picked_taken, genotypes, taken)
     shared2 = lax.all_to_all(payload, "rows", 0, 0, tiled=True)
 
     tables = []

time: 140 us -> 107 us (0.76)
  Pallas kernels: 42.8 us -> 12.2 us
    pallas_call x1, Pallas kernels: 34.4 us -> 3.74 us  [shards(): call(pick_body, (pltpu.VMEM((feat_count, ITERS * samples // LANES, LANES)...]
  transfers between devices with their start and end apart: 7 -> 7, of which waited for: 6 -> 6; matrix products, arithmetic and copies ran while one was open for 1% -> 2% of each run, Pallas kernels for 1% -> 2%
where the time goes in v5:
time: 107 us
  waiting for transfers between devices  52.6 us (49%)
  starting transfers between devices  37.7 us (35%)
  Pallas kernels  12.2 us (11%)
  local copies, waits for them, and re-layouts  2.52 us (2%)
    all_to_all x1, waiting for transfers between devices, shards(): shared1 = lax.all_to_all(payload, 'rows', 0, 0, tiled=True)  16 us
    all_to_all x1, waiting for transfers between devices, shards(): shared2 = lax.all_to_all(payload, 'rows', 0, 0, tiled=True)  15.8 us
    all_to_all x1, waiting for transfers between devices, shards(): shared0 = lax.all_to_all(payload, 'rows', 0, 0, tiled=True)  14.1 us
    all_to_all x1, starting transfers between devices, shards(): shared0 = lax.all_to_all(payload, 'rows', 0, 0, tiled=True)  12.4 us
    all_to_all x1, starting transfers between devices, shards(): cols = lax.all_to_all(sent, 'feat', 0, 0, tiled=True)  11.7 us
    all_to_all x1, waiting for transfers between devices, shards(): cols = lax.all_to_all(sent, 'feat', 0, 0, tiled=True)  4.07 us
    all_to_all x1, starting transfers between devices, shards(): shared1 = lax.all_to_all(payload, 'rows', 0, 0, tiled=True)  4.02 us
    pallas_call x1, Pallas kernels, shards(): call(pick_body, (pltpu.VMEM((feat_count, ITERS * samples // LANES, LANES)...  3.74 us
  transfers between devices with their start and end apart: 7, of which 6 were waited for; matrix products, arithmetic and copies ran while one was open for 2% of the time, Pallas kernels for 2%

profile of v5, /device:TPU:32, one launch (start us, length us, event | category | flops | bytes accessed | tf_op | source)
XLA Modules:
  0.0 106.5 jit_solution(14481544329807670711)
XLA Ops:
  0.6 0.0 copy-start
  0.6 3.7 %shard_map.59 = (bf16[64,8,128]{2,1,0:T(8,128)(2,1)}, bf16[512,1024]{1,0:T(8,128)(2,1)}, f32[72,512]{1,0:T(8,128)S(1)}) custom-call(s32[2,64]{1,0:T(2,128)} %refs_1_.1, bf16[512,2048]{1,0:T(8,128)(2,1)} %geno_ref.7, f32[64,512]{1,0:T(8,128)} %bitcast.30, s32[1,512]{1,0:T(1,128)} %bitcast.31), custom_call_target="tpu_custom_call" | custom-call | bytes 262144 | tf_op jit(solution)/shard_map/pallas_call | solution.py:352
  4.4 1.9 %collective-permute-start.1 = (bf16[512,1024]{1,0:T(8,128)(2,1)}, bf16[512,1024]{1,0:T(8,128)(2,1)S(1)}, u32[]{:S(2)}, u32[]{:S(2)}) collective-permute-start(bf16[512,1024]{1,0:T(8,128)(2,1)} %get-tuple-element.13), channel_id=1, source_target_pairs={{0,64},{64,0},{128,192},{192,128},{256,320},{320,256},{384,448},{4... | collective-permute-start | bytes 3145736 | tf_op jit(solution)/shard_map/ppermute | solution.py:370
  6.3 11.7 %all-to-all-start = ((bf16[64,8,128]{2,1,0:T(8,128)(2,1)}), bf16[64,8,128]{2,1,0:T(8,128)(2,1)S(1)}, u32[]{:S(2)}, u32[]{:S(2)}) async-start(bf16[64,8,128]{2,1,0:T(8,128)(2,1)} %get-tuple-element.11), calls=%async_computation | async-start | bytes 262144 | tf_op jit(solution)/shard_map/all_to_all | solution.py:368
  18.0 1.9 %collective-permute-start = (f32[72,512]{1,0:T(8,128)S(1)}, f32[72,512]{1,0:T(8,128)S(1)}, u32[]{:S(2)}, u32[]{:S(2)}) collective-permute-start(f32[72,512]{1,0:T(8,128)S(1)} %get-tuple-element.12.state_ref.refs_2_), channel_id=1, source_target_pairs={{0,64},{64,0},{128,192},{192,128},{256,320},{320,256},{384,448},{4... | collective-permute-start | bytes 442376 | tf_op jit(solution)/shard_map/ppermute | solution.py:371
  19.9 1.3 %collective-permute-done.state_taken_ref.far_state_ref = f32[72,512]{1,0:T(8,128)S(1)} collective-permute-done((f32[72,512]{1,0:T(8,128)S(1)}, f32[72,512]{1,0:T(8,128)S(1)}, u32[]{:S(2)}, u32[]{:S(2)}) %collective-permute-start) | collective-permute-done | bytes 147488 | tf_op jit(solution)/shard_map/ppermute | solution.py:371
  21.3 0.0 copy-start.1
  21.3 0.0 collective-permute-done.1.taken_ref
  21.3 0.7 copy-done.1
  21.9 0.0 copy-done
  21.9 1.8 %shard_map.60.refs_3_ = bf16[8,8,1024]{2,1,0:T(8,128)(2,1)S(1)} custom-call(f32[72,512]{1,0:T(8,128)S(1)} %get-tuple-element.12.state_ref.refs_2_, f32[72,512]{1,0:T(8,128)} %copy-done.1, bf16[512,2048]{1,0:T(8,128)(2,1)S(1)} %copy-done, bf16[512,1024]{1,0:T(8,128)(2,1)S(1)} %collective-permute-done.1.taken_ref), custom_call_target="tpu_custom_call" | custom-call | flops 134217728 | bytes 2097152 | tf_op jit(solution)/shard_map/pallas_call | solution.py:374
  23.7 4.1 %all-to-all-done.refs_0_ = bf16[64,8,128]{2,1,0:T(8,128)(2,1)S(1)} async-done(((bf16[64,8,128]{2,1,0:T(8,128)(2,1)}), bf16[64,8,128]{2,1,0:T(8,128)(2,1)S(1)}, u32[]{:S(2)}, u32[]{:S(2)}) %all-to-all-start) | async-done | bytes 131104 | tf_op jit(solution)/shard_map/all_to_all | solution.py:368
  27.8 1.7 %shard_map.61 = (bf16[8,8,1152]{2,1,0:T(8,128)(2,1)}, bf16[2,64,512]{2,1,0:T(8,128)(2,1)}) custom-call(bf16[64,8,128]{2,1,0:T(8,128)(2,1)S(1)} %all-to-all-done.refs_0_, s32[2,64]{1,0:T(2,128)} %refs_1_.1, f32[72,512]{1,0:T(8,128)S(1)} %get-tuple-element.12.state_ref.refs_2_, bf16[8,8,1024]{2,1,0:T(8,128)(2,1)S(1)} %shard_map.60.refs_3_), custom_call_target="tpu_custom_call" | custom-call | bytes 2097152 | tf_op jit(solution)/shard_map/pallas_call | solution.py:386
  29.6 12.4 %all-to-all-start.1 = ((bf16[8,8,1152]{2,1,0:T(8,128)(2,1)}), bf16[8,8,1152]{2,1,0:T(8,128)(2,1)}, u32[]{:S(2)}, u32[]{:S(2)}) async-start(bf16[8,8,1152]{2,1,0:T(8,128)(2,1)} %get-tuple-element.14), calls=%async_computation.1 | async-start | bytes 294912 | tf_op jit(solution)/shard_map/all_to_all | solution.py:393
  42.0 2.4 %collective-permute-start.2 = (bf16[2,64,512]{2,1,0:T(8,128)(2,1)}, bf16[2,64,512]{2,1,0:T(8,128)(2,1)S(1)}, u32[]{:S(2)}, u32[]{:S(2)}) collective-permute-start(bf16[2,64,512]{2,1,0:T(8,128)(2,1)} %get-tuple-element.15.far_picked_ref), channel_id=1, source_target_pairs={{0,64},{64,0},{128,192},{192,128},{256,320},{320,256},{384,448},{4... | collective-permute-start | bytes 393224 | tf_op jit(solution)/shard_map/ppermute | solution.py:394
  44.4 1.2 %collective-permute-done.2.far_picked_taken_ref = bf16[2,64,512]{2,1,0:T(8,128)(2,1)S(1)} collective-permute-done((bf16[2,64,512]{2,1,0:T(8,128)(2,1)}, bf16[2,64,512]{2,1,0:T(8,128)(2,1)S(1)}, u32[]{:S(2)}, u32[]{:S(2)}) %collective-permute-start.2) | collective-permute-done | bytes 131104 | tf_op jit(solution)/shard_map/ppermute | solution.py:394
  45.5 0.0 copy-start.2
  45.5 14.1 %all-to-all-done.1.shared_ref = bf16[8,8,1152]{2,1,0:T(8,128)(2,1)} async-done(((bf16[8,8,1152]{2,1,0:T(8,128)(2,1)}), bf16[8,8,1152]{2,1,0:T(8,128)(2,1)}, u32[]{:S(2)}, u32[]{:S(2)}) %all-to-all-start.1) | async-done | bytes 147488 | tf_op jit(solution)/shard_map/all_to_all | solution.py:393
  59.6 0.0 copy-done.2
  59.7 2.5 %shard_map.62 = (bf16[8,8,1152]{2,1,0:T(8,128)(2,1)}, f32[64,128]{1,0:T(8,128)}) custom-call(bf16[8,8,1152]{2,1,0:T(8,128)(2,1)} %all-to-all-done.1.shared_ref, f32[72,512]{1,0:T(8,128)S(1)} %get-tuple-element.12.state_ref.refs_2_, f32[72,512]{1,0:T(8,128)} %copy-done.1, bf16[2,64,512]{2,1,0:T(8,128)(2,1)} %get-tuple-element.15.far_picked_ref, ...), custom_call_target="tpu_custom_call" | custom-call | flops 134217728 | bytes 2097152 | tf_op jit(solution)/shard_map/pallas_call | solution.py:396
  62.2 4.0 %all-to-all-start.2 = ((bf16[8,8,1152]{2,1,0:T(8,128)(2,1)}), bf16[8,8,1152]{2,1,0:T(8,128)(2,1)}, u32[]{:S(2)}, u32[]{:S(2)}) async-start(bf16[8,8,1152]{2,1,0:T(8,128)(2,1)} %get-tuple-element.16), calls=%async_computation.2 | async-start | bytes 294912 | tf_op jit(solution)/shard_map/all_to_all | solution.py:404
  66.2 0.9 slice.32
  67.2 16.0 %all-to-all-done.2.shared_ref = bf16[8,8,1152]{2,1,0:T(8,128)(2,1)} async-done(((bf16[8,8,1152]{2,1,0:T(8,128)(2,1)}), bf16[8,8,1152]{2,1,0:T(8,128)(2,1)}, u32[]{:S(2)}, u32[]{:S(2)}) %all-to-all-start.2) | async-done | bytes 147488 | tf_op jit(solution)/shard_map/all_to_all | solution.py:404
  83.2 2.4 %shard_map.63 = (bf16[8,8,1024]{2,1,0:T(8,128)(2,1)}, f32[64,512]{1,0:T(8,128)}) custom-call(bf16[8,8,1152]{2,1,0:T(8,128)(2,1)} %all-to-all-done.2.shared_ref, f32[64,128]{1,0:T(8,128)} %get-tuple-element.17.far_coef_ref, f32[72,512]{1,0:T(8,128)S(1)} %get-tuple-element.12.state_ref.refs_2_, f32[72,512]{1,0:T(8,128)} %copy-done.1, ...), custom_call_target="tpu_custom_call" | custom-call | flops 134217728 | bytes 2097152 | tf_op jit(solution)/shard_map/pallas_call | solution.py:406
  85.6 3.4 %all-to-all-start.3 = ((bf16[8,8,1024]{2,1,0:T(8,128)(2,1)}), bf16[8,8,1024]{2,1,0:T(8,128)(2,1)S(1)}, u32[]{:S(2)}, u32[]{:S(2)}) async-start(bf16[8,8,1024]{2,1,0:T(8,128)(2,1)} %get-tuple-element.19), calls=%async_computation.3 | async-start | bytes 262144 | tf_op jit(solution)/shard_map/all_to_all | solution.py:416
  89.0 0.9 slice.35
  89.9 15.8 %all-to-all-done.3 = bf16[8,8,1024]{2,1,0:T(8,128)(2,1)S(1)} async-done(((bf16[8,8,1024]{2,1,0:T(8,128)(2,1)}), bf16[8,8,1024]{2,1,0:T(8,128)(2,1)S(1)}, u32[]{:S(2)}, u32[]{:S(2)}) %all-to-all-start.3) | async-done | bytes 131104 | tf_op jit(solution)/shard_map/all_to_all | solution.py:416
  105.8 0.7 pad_maximum_fusion
  (8 shorter events, 0.1 us)
Async XLA Ops:
  0.6 21.3 %copy-start = (bf16[512,2048]{1,0:T(8,128)(2,1)S(1)}, bf16[512,2048]{1,0:T(8,128)(2,1)}, u32[]{:S(2)}) copy-start(bf16[512,2048]{1,0:T(8,128)(2,1)} %geno_ref.7) | copy-start | bytes 6291460
  4.4 16.9 %collective-permute-start.1 = (bf16[512,1024]{1,0:T(8,128)(2,1)}, bf16[512,1024]{1,0:T(8,128)(2,1)S(1)}, u32[]{:S(2)}, u32[]{:S(2)}) collective-permute-start(bf16[512,1024]{1,0:T(8,128)(2,1)} %get-tuple-element.13), channel_id=1, source_target_pairs={{0,64},{64,0},{128,192},{192,128},{256,320},{320,256},{384,448},{4... | collective-permute-start | bytes 3145736 | tf_op jit(solution)/shard_map/ppermute | solution.py:370
  6.3 21.5 %all-to-all-start = ((bf16[64,8,128]{2,1,0:T(8,128)(2,1)}), bf16[64,8,128]{2,1,0:T(8,128)(2,1)S(1)}, u32[]{:S(2)}, u32[]{:S(2)}) async-start(bf16[64,8,128]{2,1,0:T(8,128)(2,1)} %get-tuple-element.11), calls=%async_computation | async-start | bytes 262144 | tf_op jit(solution)/shard_map/all_to_all | solution.py:368
  18.0 3.3 %collective-permute-start = (f32[72,512]{1,0:T(8,128)S(1)}, f32[72,512]{1,0:T(8,128)S(1)}, u32[]{:S(2)}, u32[]{:S(2)}) collective-permute-start(f32[72,512]{1,0:T(8,128)S(1)} %get-tuple-element.12.state_ref.refs_2_), channel_id=1, source_target_pairs={{0,64},{64,0},{128,192},{192,128},{256,320},{320,256},{384,448},{4... | collective-permute-start | bytes 442376 | tf_op jit(solution)/shard_map/ppermute | solution.py:371
  21.3 0.7 copy-start.1
  29.6 30.1 %all-to-all-start.1 = ((bf16[8,8,1152]{2,1,0:T(8,128)(2,1)}), bf16[8,8,1152]{2,1,0:T(8,128)(2,1)}, u32[]{:S(2)}, u32[]{:S(2)}) async-start(bf16[8,8,1152]{2,1,0:T(8,128)(2,1)} %get-tuple-element.14), calls=%async_computation.1 | async-start | bytes 294912 | tf_op jit(solution)/shard_map/all_to_all | solution.py:393
  42.0 3.6 %collective-permute-start.2 = (bf16[2,64,512]{2,1,0:T(8,128)(2,1)}, bf16[2,64,512]{2,1,0:T(8,128)(2,1)S(1)}, u32[]{:S(2)}, u32[]{:S(2)}) collective-permute-start(bf16[2,64,512]{2,1,0:T(8,128)(2,1)} %get-tuple-element.15.far_picked_ref), channel_id=1, source_target_pairs={{0,64},{64,0},{128,192},{192,128},{256,320},{320,256},{384,448},{4... | collective-permute-start | bytes 393224 | tf_op jit(solution)/shard_map/ppermute | solution.py:394
  45.5 14.1 %copy-start.2 = (bf16[2,64,512]{2,1,0:T(8,128)(2,1)}, bf16[2,64,512]{2,1,0:T(8,128)(2,1)S(1)}, u32[]{:S(2)}) copy-start(bf16[2,64,512]{2,1,0:T(8,128)(2,1)S(1)} %collective-permute-done.2.far_picked_taken_ref) | copy-start | bytes 393220
  62.2 21.0 %all-to-all-start.2 = ((bf16[8,8,1152]{2,1,0:T(8,128)(2,1)}), bf16[8,8,1152]{2,1,0:T(8,128)(2,1)}, u32[]{:S(2)}, u32[]{:S(2)}) async-start(bf16[8,8,1152]{2,1,0:T(8,128)(2,1)} %get-tuple-element.16), calls=%async_computation.2 | async-start | bytes 294912 | tf_op jit(solution)/shard_map/all_to_all | solution.py:404
  85.6 20.2 %all-to-all-start.3 = ((bf16[8,8,1024]{2,1,0:T(8,128)(2,1)}), bf16[8,8,1024]{2,1,0:T(8,128)(2,1)S(1)}, u32[]{:S(2)}, u32[]{:S(2)}) async-start(bf16[8,8,1024]{2,1,0:T(8,128)(2,1)} %get-tuple-element.19), calls=%async_computation.3 | async-start | bytes 262144 | tf_op jit(solution)/shard_map/all_to_all | solution.py:416

commit v6 on v5

--- a/solution.py
+++ b/solution.py
@@ -21,7 +21,7 @@
 HBM = pl.BlockSpec(memory_space=pltpu.HBM)
 
 
-def call(body, out_shape, in_specs, scratch=(), flops=0, moved=0, room=16 << 20):
+def call(body, out_shape, in_specs, scratch=(), flops=0, moved=0, room=8 << 20):
     out_specs = jax.tree.map(
         lambda out: BlockSpec(memory_space=out.memory_space), out_shape, is_leaf=is_out
     )
@@ -88,16 +88,10 @@
 
 
 def pick_body(
-    win_ref, geno_ref, margin_ref, labels_ref, out_ref, given_ref, state_ref, block_ref, half_ref,
-    sem_ref,
+    win_ref, geno_ref, margin_ref, labels_ref, out_ref, state_ref, block_ref, sem_ref
 ):
     samples, columns = geno_ref.shape
-    half = given_ref.shape[1]
-    side = lax.rem(lax.axis_index("rows"), 2)
-    other = pl.multiple_of((1 - side) * half, LANES)
-    give = pltpu.make_async_copy(geno_ref.at[:, pl.ds(other, half)], half_ref, sem_ref.at[ITERS])
-    give.start()
-    margins = pltpu.make_async_copy(margin_ref, state_ref.at[pl.ds(0, K)], sem_ref.at[ITERS + 1])
+    margins = pltpu.make_async_copy(margin_ref, state_ref.at[pl.ds(0, K)], sem_ref.at[ITERS])
     margins.start()
     state_ref[K:] = jnp.broadcast_to(labels_ref[...].astype(f32), (8, samples))
     local = win_ref[...] - lax.axis_index("feat") * columns
@@ -115,9 +109,6 @@
     rows = lax.broadcasted_iota(i32, (8, LANES), 0)
     lane = lax.broadcasted_iota(i32, (8, LANES), 1)
     tile = jnp.zeros((8, LANES), f32)
-    give.wait()
-    give = pltpu.make_async_copy(half_ref, given_ref, sem_ref.at[ITERS])
-    give.start()
     for step in range(ITERS):
         copies[step].wait()
         pick = jnp.where(lane == lanes[step], 1.0, 0.0).astype(bf16)
@@ -129,25 +120,27 @@
             tile = tile + jnp.where(here, x[:, j * LANES : (j + 1) * LANES], 0.0)
     out_ref[...] = jnp.broadcast_to(tile.astype(bf16)[None], out_ref.shape)
     margins.wait()
-    give.wait()
-
-
-def load_halves(geno_ref, taken_ref, both_ref, sem_ref):
-    samples, half = taken_ref.shape
-    side = lax.rem(lax.axis_index("rows"), 2)
-    start = pl.multiple_of(side * half, LANES)
-    first = pltpu.make_async_copy(
-        geno_ref.at[:, pl.ds(start, half)], both_ref.at[pl.ds(0, samples)], sem_ref.at[0]
-    )
-    second = pltpu.make_async_copy(taken_ref, both_ref.at[pl.ds(samples, samples)], sem_ref.at[1])
-    first.start()
-    second.start()
-    return first, second
-
-
-def half_table(resid, resid_taken, both_ref):
-    whole = jnp.concatenate([resid, resid_taken], axis=1)
-    return jnp.dot(whole, both_ref[...], preferred_element_type=f32)
+
+
+def half_start(geno_ref):
+    half = geno_ref.shape[1] // 2
+    return pl.multiple_of(lax.rem(lax.axis_index("rows"), 2) * half, LANES)
+
+
+def half_table(resid, resid_taken, geno_ref, taken_ref, start, width):
+    own_span = pl.ds(pl.multiple_of(half_start(geno_ref) + start, LANES), width)
+    first = jnp.dot(resid, geno_ref[:, own_span], preferred_element_type=f32)
+    second = taken_ref[:, pl.ds(start, width)]
+    return first + jnp.dot(resid_taken, second, preferred_element_type=f32)
+
+
+def load_half(whole_ref, half_ref, sem_ref):
+    start = half_start(whole_ref)
+    copy = pltpu.make_async_copy(
+        whole_ref.at[:, pl.ds(start, half_ref.shape[1])], half_ref, sem_ref
+    )
+    copy.start()
+    return copy
 
 
 def sums_tile(resid, prob, picked):
@@ -188,13 +181,14 @@
     return copy
 
 
-def send_table(resid, resid_taken, both_ref, table_ref, out_ref, sem_ref, pieces=2):
-    whole = jnp.concatenate([resid, resid_taken], axis=1)
+def send_table(resid, resid_taken, geno_ref, taken_ref, table_ref, out_ref, sem_ref, pieces=2):
     width = table_ref.shape[2] // pieces
     copies = []
     for piece in range(pieces):
         span = pl.ds(piece * width, width)
-        table = jnp.dot(whole, both_ref[:, span], preferred_element_type=f32)
+        table = half_table(
+            resid, resid_taken, geno_ref, taken_ref, piece * width, width
+        )
         table_ref[:, :, span] = table.reshape(table_ref.shape[0], -1, width).astype(bf16)
         copy = pltpu.make_async_copy(
             table_ref.at[:, :, span], out_ref.at[:, :, span], sem_ref.at[piece]
@@ -205,14 +199,13 @@
 
 
 def first_table_body(
-    state_ref, state_taken_ref, geno_ref, taken_ref, out_ref, both_ref, sem_ref
+    state_ref, state_taken_ref, geno_ref, far_taken_ref, out_ref, taken_ref, sem_ref
 ):
-    copies = load_halves(geno_ref, taken_ref, both_ref, sem_ref)
+    taken = load_half(far_taken_ref, taken_ref, sem_ref.at[0])
     resid, _ = residuals(state_ref[:K], state_ref[K : K + 1])
     resid_taken, _ = residuals(state_taken_ref[:K], state_taken_ref[K : K + 1])
-    for copy in copies:
-        copy.wait()
-    table = half_table(resid, resid_taken, both_ref)
+    taken.wait()
+    table = half_table(resid, resid_taken, geno_ref, taken_ref, 0, out_ref.shape[2])
     out_ref[...] = table.reshape(out_ref.shape).astype(bf16)
 
 
@@ -250,50 +243,47 @@
 
 def second_table_body(
     shared_ref, state_ref, far_state_ref, far_picked_ref, far_picked_taken_ref, geno_ref,
-    taken_ref, out_ref, far_coef_ref, both_ref, table_ref, tiles_ref, got_ref, state_taken_ref,
+    far_taken_ref, out_ref, far_coef_ref, taken_ref, table_ref, tiles_ref, state_taken_ref,
     picked_ref, picked_taken_ref, coef_ref, sem_ref, load_ref,
 ):
-    half = taken_ref.shape[1]
+    half = table_ref.shape[2]
     loads = load(
         [
-            (shared_ref.at[:, :, pl.ds(half, 2 * K)], got_ref),
             (far_picked_ref, picked_ref),
             (far_state_ref, state_taken_ref),
             (far_picked_taken_ref, picked_taken_ref),
         ],
         load_ref,
     )
-    copies = load_halves(geno_ref, taken_ref, both_ref, sem_ref)
-    loads[0].wait()
-    coef = coefficients(got_ref[...])
+    taken = load_half(far_taken_ref, taken_ref, sem_ref.at[4])
+    coef = coefficients(shared_ref[:, :, half:])
     coef_ref[...] = coef
-    coef_copy = pltpu.make_async_copy(coef_ref, far_coef_ref, sem_ref.at[5])
+    coef_copy = pltpu.make_async_copy(coef_ref, far_coef_ref, sem_ref.at[1])
     coef_copy.start()
     coef = lane_tile(coef, state_ref.shape[1] // LANES)
-    loads[1].wait()
+    loads[0].wait()
     logits = state_ref[:K] + coef * picked_ref[0].astype(f32)
     resid, prob = residuals(logits, state_ref[K : K + 1])
     tile = sums_tile(resid, prob, picked_ref[1].astype(f32))
-    sums_copy = send_tile(tile, tiles_ref, out_ref, sem_ref.at[2])
-    wait_all(loads[2:])
+    sums_copy = send_tile(tile, tiles_ref, out_ref, sem_ref.at[0])
+    wait_all(loads[1:])
     logits_taken = state_taken_ref[:K] + coef * picked_taken_ref[0].astype(f32)
     resid_taken, _ = residuals(logits_taken, state_taken_ref[K : K + 1])
-    wait_all(copies)
+    taken.wait()
     table_copies = send_table(
-        resid, resid_taken, both_ref, table_ref, out_ref, sem_ref.at[pl.ds(3, 2)]
+        resid, resid_taken, geno_ref, taken_ref, table_ref, out_ref, sem_ref.at[pl.ds(2, 2)]
     )
     wait_all([coef_copy, sums_copy] + table_copies)
 
 
 def third_table_body(
     shared_ref, far_coef_ref, state_ref, far_state_ref, far_picked_ref, far_picked_taken_ref,
-    geno_ref, taken_ref, out_ref, logits_ref, both_ref, table_ref, new_ref, got_ref,
+    geno_ref, far_taken_ref, out_ref, logits_ref, taken_ref, table_ref, new_ref,
     state_taken_ref, picked_ref, picked_taken_ref, coef_ref, sem_ref, load_ref,
 ):
-    half = taken_ref.shape[1]
+    half = table_ref.shape[2]
     loads = load(
         [
-            (shared_ref.at[:, :, pl.ds(half, 2 * K)], got_ref),
             (far_coef_ref, coef_ref),
             (far_picked_ref, picked_ref),
             (far_state_ref, state_taken_ref),
@@ -301,29 +291,30 @@
         ],
         load_ref,
     )
-    copies = load_halves(geno_ref, taken_ref, both_ref, sem_ref)
+    taken = load_half(far_taken_ref, taken_ref, sem_ref.at[4])
     blocks = state_ref.shape[1] // LANES
-    wait_all(loads[:2])
-    coefs = [lane_tile(coef, blocks) for coef in (coef_ref[...], coefficients(got_ref[...]))]
+    now = coefficients(shared_ref[:, :, half:])
+    loads[0].wait()
+    coefs = [lane_tile(coef, blocks) for coef in (coef_ref[...], now)]
 
     def updated(start, columns_ref):
         for step in range(ITERS):
             start = start + coefs[step] * columns_ref[step].astype(f32)
         return start
 
-    loads[2].wait()
+    loads[1].wait()
     logits = updated(state_ref[:K], picked_ref)
     new_ref[...] = logits
-    logits_copy = pltpu.make_async_copy(new_ref, logits_ref, sem_ref.at[2])
+    logits_copy = pltpu.make_async_copy(new_ref, logits_ref, sem_ref.at[0])
     logits_copy.start()
     resid, _ = residuals(logits, state_ref[K : K + 1])
-    wait_all(loads[3:])
+    wait_all(loads[2:])
     resid_taken, _ = residuals(
         updated(state_taken_ref[:K], picked_taken_ref), state_taken_ref[K : K + 1]
     )
-    wait_all(copies)
+    taken.wait()
     table_copies = send_table(
-        resid, resid_taken, both_ref, table_ref, out_ref, sem_ref.at[pl.ds(3, 2)]
+        resid, resid_taken, geno_ref, taken_ref, table_ref, out_ref, sem_ref.at[pl.ds(2, 2)]
     )
     wait_all([logits_copy] + table_copies)
 
@@ -339,46 +330,43 @@
     payload_shape = (rows_count, class_share, half + 2 * K)
     table_shape = (rows_count, class_share, half)
     tiles = pltpu.VMEM((rows_count, 8, 2 * K), bf16)
-    both = pltpu.VMEM((2 * samples, half), bf16)
     sems = pltpu.SemaphoreType.DMA
+    got_half = pltpu.VMEM((samples, half), bf16)
     loaded = [
-        tiles,
         pltpu.VMEM((K + 8, samples), f32),
         pltpu.VMEM((ITERS, K, samples), bf16),
         pltpu.VMEM((ITERS, K, samples), bf16),
         pltpu.VMEM((K, LANES), f32),
     ]
 
-    sent, given, state = call(
+    sent, state = call(
         pick_body,
         (
             pltpu.VMEM((feat_count, ITERS * samples // LANES, LANES), bf16),
-            pltpu.HBM((samples, half), bf16),
             pltpu.VMEM((K + 8, samples), f32),
         ),
         [VMEM, HBM, HBM, VMEM],
         [
             pltpu.VMEM((ITERS, samples, LANES), bf16),
-            pltpu.VMEM((samples, half), bf16),
-            sems((ITERS + 2,)),
+            sems((ITERS + 1,)),
         ],
         moved=samples * LANES * 4,
-        room=None,
     )(winners, far(genotypes), far(base_margin.T), labels[None, :])
     cols = lax.all_to_all(sent, "feat", 0, 0, tiled=True)
 
-    taken = lax.ppermute(given, "rows", partners)
+    taken = far(lax.ppermute(genotypes, "rows", partners))
+    geno = near(genotypes)
     state_taken = far(lax.ppermute(state, "rows", partners))
     state = near(state)
 
     table = call(
         first_table_body,
         pltpu.VMEM(table_shape, bf16),
-        [VMEM, VMEM, HBM, HBM],
-        [both, sems((2,))],
+        [VMEM] * 3 + [HBM],
+        [got_half, sems((1,))],
         flops=work,
         moved=4 * samples * half,
-    )(state, state_taken, genotypes, taken)
+    )(state, state_taken, geno, taken)
 
     def first_sums(*refs):
         first_sums_body(*refs, columns=columns)
@@ -396,23 +384,23 @@
     payload, coef = call(
         second_table_body,
         (pltpu.HBM(payload_shape, bf16), pltpu.HBM((K, LANES), f32)),
-        [HBM, VMEM] + [HBM] * 5,
-        [both, pltpu.VMEM(table_shape, bf16), tiles] + loaded + [sems((6,)), sems((4,))],
+        [VMEM, VMEM] + [HBM] * 3 + [VMEM, HBM],
+        [got_half, pltpu.VMEM(table_shape, bf16), tiles] + loaded + [sems((5,)), sems((3,))],
         flops=work,
         moved=4 * samples * half,
-    )(far(shared0), state, state_taken, far(picked), picked_taken, genotypes, taken)
+    )(near(shared0), state, state_taken, far(picked), picked_taken, geno, taken)
     shared1 = lax.all_to_all(payload, "rows", 0, 0, tiled=True)
 
     payload, logits = call(
         third_table_body,
         (pltpu.HBM(table_shape, bf16), pltpu.HBM((K, samples), f32)),
-        [HBM, HBM, VMEM] + [HBM] * 5,
-        [both, pltpu.VMEM(table_shape, bf16), pltpu.VMEM((K, samples), f32)]
+        [VMEM, HBM, VMEM] + [HBM] * 3 + [VMEM, HBM],
+        [got_half, pltpu.VMEM(table_shape, bf16), pltpu.VMEM((K, samples), f32)]
         + loaded
-        + [sems((5,)), sems((5,))],
+        + [sems((5,)), sems((4,))],
         flops=work,
         moved=4 * samples * half,
-    )(far(shared1), far(coef), state, state_taken, far(picked), picked_taken, genotypes, taken)
+    )(near(shared1), far(coef), state, state_taken, far(picked), picked_taken, geno, taken)
     shared2 = lax.all_to_all(payload, "rows", 0, 0, tiled=True)
 
     tables = []

time: 107 us -> 107 us (level)
    slice x2, local copies, waits for them, and re-layouts: 1.83 us -> 0.02 us  [shards(): shared[:, :, :half].astype(f32)]
    pallas_call x1, Pallas kernels: 3.74 us -> 2.05 us  [shards(): call(pick_body, (pltpu.VMEM((feat_count, ITERS * samples // LANES, LANES)...]
    unnamed x6 -> x10, local copies, waits for them, and re-layouts: 0.67 us -> 2.02 us
    all_to_all x1, waiting for transfers between devices: 15.8 us -> 16.9 us  [shards(): shared2 = lax.all_to_all(payload, 'rows', 0, 0, tiled=True)]
  transfers between devices with their start and end apart: 7 -> 7, of which waited for: 6 -> 6; matrix products, arithmetic and copies ran while one was open for 2% -> 0% of each run, Pallas kernels for 2% -> 4%
where the time goes in v6:
time: 107 us; the launch traced here: 106 us
  waiting for transfers between devices  53.3 us (50%)
  starting transfers between devices  37.2 us (35%)
  Pallas kernels  11.8 us (11%)
  local copies, waits for them, and re-layouts  2.06 us (2%)
    all_to_all x1, waiting for transfers between devices, shards(): shared2 = lax.all_to_all(payload, 'rows', 0, 0, tiled=True)  16.9 us
    all_to_all x1, waiting for transfers between devices, shards(): shared1 = lax.all_to_all(payload, 'rows', 0, 0, tiled=True)  16.7 us
    all_to_all x1, waiting for transfers between devices, shards(): shared0 = lax.all_to_all(payload, 'rows', 0, 0, tiled=True)  14 us
    all_to_all x1, starting transfers between devices, shards(): shared0 = lax.all_to_all(payload, 'rows', 0, 0, tiled=True)  12.4 us
    all_to_all x1, starting transfers between devices, shards(): cols = lax.all_to_all(sent, 'feat', 0, 0, tiled=True)  11.7 us
    all_to_all x1, starting transfers between devices, shards(): shared1 = lax.all_to_all(payload, 'rows', 0, 0, tiled=True)  3.39 us
    all_to_all x1, starting transfers between devices, shards(): shared2 = lax.all_to_all(payload, 'rows', 0, 0, tiled=True)  3.38 us
    all_to_all x1, waiting for transfers between devices, shards(): cols = lax.all_to_all(sent, 'feat', 0, 0, tiled=True)  3.2 us
  transfers between devices with their start and end apart: 7, of which 6 were waited for; matrix products, arithmetic and copies ran while one was open for 0% of the time, Pallas kernels for 4%

profile of v6, /device:TPU:32, one launch (start us, length us, event | category | flops | bytes accessed | tf_op | source)
XLA Modules:
  0.0 105.9 jit_solution(675827588508137230)
XLA Ops:
  0.6 0.0 copy-start
  0.6 2.1 %collective-permute-start.1 = (bf16[512,2048]{1,0:T(8,128)(2,1)}, bf16[512,2048]{1,0:T(8,128)(2,1)}, u32[]{:S(2)}, u32[]{:S(2)}) collective-permute-start(bf16[512,2048]{1,0:T(8,128)(2,1)} %geno_ref.7), channel_id=1, source_target_pairs={{0,64},{64,0},{128,192},{192,128},{256,320},{320,256},{384,448},{4... | collective-permute-start | bytes 6291464 | tf_op jit(solution)/shard_map/ppermute | solution.py:357
  2.7 0.0 copy-start.1
  2.7 0.7 copy-done.1
  3.4 0.0 copy-start.2
  3.4 0.7 copy-done.2
  4.1 2.0 %shard_map.59 = (bf16[64,8,128]{2,1,0:T(8,128)(2,1)}, f32[72,512]{1,0:T(8,128)S(1)}) custom-call(s32[2,64]{1,0:T(2,128)S(1)} %copy-done.1, bf16[512,2048]{1,0:T(8,128)(2,1)} %geno_ref.7, f32[64,512]{1,0:T(8,128)} %bitcast.31, s32[1,512]{1,0:T(1,128)S(1)} %bitcast.27), custom_call_target="tpu_custom_call" | custom-call | bytes 262144 | tf_op jit(solution)/shard_map/pallas_call | solution.py:342
  6.1 11.7 %all-to-all-start = ((bf16[64,8,128]{2,1,0:T(8,128)(2,1)}), bf16[64,8,128]{2,1,0:T(8,128)(2,1)S(1)}, u32[]{:S(2)}, u32[]{:S(2)}) async-start(bf16[64,8,128]{2,1,0:T(8,128)(2,1)} %get-tuple-element.10), calls=%async_computation | async-start | bytes 262144 | tf_op jit(solution)/shard_map/all_to_all | solution.py:355
  17.8 1.9 %collective-permute-start = (f32[72,512]{1,0:T(8,128)S(1)}, f32[72,512]{1,0:T(8,128)S(1)}, u32[]{:S(2)}, u32[]{:S(2)}) collective-permute-start(f32[72,512]{1,0:T(8,128)S(1)} %get-tuple-element.11.state_ref.refs_2_), channel_id=1, source_target_pairs={{0,64},{64,0},{128,192},{192,128},{256,320},{320,256},{384,448},{4... | collective-permute-start | bytes 442376 | tf_op jit(solution)/shard_map/ppermute | solution.py:359
  19.7 1.3 %collective-permute-done.state_taken_ref.far_state_ref = f32[72,512]{1,0:T(8,128)S(1)} collective-permute-done((f32[72,512]{1,0:T(8,128)S(1)}, f32[72,512]{1,0:T(8,128)S(1)}, u32[]{:S(2)}, u32[]{:S(2)}) %collective-permute-start) | collective-permute-done | bytes 147488 | tf_op jit(solution)/shard_map/ppermute | solution.py:359
  21.1 0.0 copy-start.3
  21.1 0.0 collective-permute-done.1.far_taken_ref
  21.1 0.7 copy-done.3
  21.7 0.0 copy-done
  21.7 2.7 %shard_map.60.refs_3_ = bf16[8,8,1024]{2,1,0:T(8,128)(2,1)S(1)} custom-call(f32[72,512]{1,0:T(8,128)S(1)} %get-tuple-element.11.state_ref.refs_2_, f32[72,512]{1,0:T(8,128)} %copy-done.3, bf16[512,2048]{1,0:T(8,128)(2,1)S(1)} %copy-done, bf16[512,2048]{1,0:T(8,128)(2,1)} %collective-permute-done.1.far_taken_ref), custom_call_target="tpu_custom_call" | custom-call | flops 134217728 | bytes 2097152 | tf_op jit(solution)/shard_map/pallas_call | solution.py:362
  24.4 3.2 %all-to-all-done.refs_0_ = bf16[64,8,128]{2,1,0:T(8,128)(2,1)S(1)} async-done(((bf16[64,8,128]{2,1,0:T(8,128)(2,1)}), bf16[64,8,128]{2,1,0:T(8,128)(2,1)S(1)}, u32[]{:S(2)}, u32[]{:S(2)}) %all-to-all-start) | async-done | bytes 131104 | tf_op jit(solution)/shard_map/all_to_all | solution.py:355
  27.6 1.7 %shard_map.61 = (bf16[8,8,1152]{2,1,0:T(8,128)(2,1)}, bf16[2,64,512]{2,1,0:T(8,128)(2,1)}) custom-call(bf16[64,8,128]{2,1,0:T(8,128)(2,1)S(1)} %all-to-all-done.refs_0_, s32[2,64]{1,0:T(2,128)} %refs_1_.1, f32[72,512]{1,0:T(8,128)S(1)} %get-tuple-element.11.state_ref.refs_2_, bf16[8,8,1024]{2,1,0:T(8,128)(2,1)S(1)} %shard_map.60.refs_3_), custom_call_target="tpu_custom_call" | custom-call | bytes 2097152 | tf_op jit(solution)/shard_map/pallas_call | solution.py:374
  29.4 12.4 %all-to-all-start.1 = ((bf16[8,8,1152]{2,1,0:T(8,128)(2,1)}), bf16[8,8,1152]{2,1,0:T(8,128)(2,1)S(1)}, u32[]{:S(2)}, u32[]{:S(2)}) async-start(bf16[8,8,1152]{2,1,0:T(8,128)(2,1)} %get-tuple-element.12), calls=%async_computation.1 | async-start | bytes 294912 | tf_op jit(solution)/shard_map/all_to_all | solution.py:381
  41.8 2.4 %collective-permute-start.2 = (bf16[2,64,512]{2,1,0:T(8,128)(2,1)}, bf16[2,64,512]{2,1,0:T(8,128)(2,1)S(1)}, u32[]{:S(2)}, u32[]{:S(2)}) collective-permute-start(bf16[2,64,512]{2,1,0:T(8,128)(2,1)} %get-tuple-element.13.far_picked_ref), channel_id=1, source_target_pairs={{0,64},{64,0},{128,192},{192,128},{256,320},{320,256},{384,448},{4... | collective-permute-start | bytes 393224 | tf_op jit(solution)/shard_map/ppermute | solution.py:382
  44.2 1.2 %collective-permute-done.2.far_picked_taken_ref = bf16[2,64,512]{2,1,0:T(8,128)(2,1)S(1)} collective-permute-done((bf16[2,64,512]{2,1,0:T(8,128)(2,1)}, bf16[2,64,512]{2,1,0:T(8,128)(2,1)S(1)}, u32[]{:S(2)}, u32[]{:S(2)}) %collective-permute-start.2) | collective-permute-done | bytes 131104 | tf_op jit(solution)/shard_map/ppermute | solution.py:382
  45.3 0.0 copy-start.4
  45.4 14.0 %all-to-all-done.1.shared_ref = bf16[8,8,1152]{2,1,0:T(8,128)(2,1)S(1)} async-done(((bf16[8,8,1152]{2,1,0:T(8,128)(2,1)}), bf16[8,8,1152]{2,1,0:T(8,128)(2,1)S(1)}, u32[]{:S(2)}, u32[]{:S(2)}) %all-to-all-start.1) | async-done | bytes 147488 | tf_op jit(solution)/shard_map/all_to_all | solution.py:381
  59.3 0.0 copy-done.4
  59.4 2.7 %shard_map.62 = (bf16[8,8,1152]{2,1,0:T(8,128)(2,1)}, f32[64,128]{1,0:T(8,128)}) custom-call(bf16[8,8,1152]{2,1,0:T(8,128)(2,1)S(1)} %all-to-all-done.1.shared_ref, f32[72,512]{1,0:T(8,128)S(1)} %get-tuple-element.11.state_ref.refs_2_, f32[72,512]{1,0:T(8,128)} %copy-done.3, bf16[2,64,512]{2,1,0:T(8,128)(2,1)} %get-tuple-element.13.far_picked_ref, ...), custom_call_target="tpu_custom_call" | custom-call | flops 134217728 | bytes 2097152 | tf_op jit(solution)/shard_map/pallas_call | solution.py:384
  62.0 3.4 %all-to-all-start.2 = ((bf16[8,8,1152]{2,1,0:T(8,128)(2,1)}), bf16[8,8,1152]{2,1,0:T(8,128)(2,1)S(1)}, u32[]{:S(2)}, u32[]{:S(2)}) async-start(bf16[8,8,1152]{2,1,0:T(8,128)(2,1)} %get-tuple-element.14), calls=%async_computation.2 | async-start | bytes 294912 | tf_op jit(solution)/shard_map/all_to_all | solution.py:392
  65.5 16.7 %all-to-all-done.2.shared_ref = bf16[8,8,1152]{2,1,0:T(8,128)(2,1)S(1)} async-done(((bf16[8,8,1152]{2,1,0:T(8,128)(2,1)}), bf16[8,8,1152]{2,1,0:T(8,128)(2,1)S(1)}, u32[]{:S(2)}, u32[]{:S(2)}) %all-to-all-start.2) | async-done | bytes 147488 | tf_op jit(solution)/shard_map/all_to_all | solution.py:392
  82.2 2.6 %shard_map.63 = (bf16[8,8,1024]{2,1,0:T(8,128)(2,1)}, f32[64,512]{1,0:T(8,128)}) custom-call(bf16[8,8,1152]{2,1,0:T(8,128)(2,1)S(1)} %all-to-all-done.2.shared_ref, f32[64,128]{1,0:T(8,128)} %get-tuple-element.15.far_coef_ref, f32[72,512]{1,0:T(8,128)S(1)} %get-tuple-element.11.state_ref.refs_2_, f32[72,512]{1,0:T(8,128)} %copy-done.3, ...), custom_call_target="tpu_custom_call" | custom-call | flops 134217728 | bytes 2097152 | tf_op jit(solution)/shard_map/pallas_call | solution.py:394
  84.8 3.4 %all-to-all-start.3 = ((bf16[8,8,1024]{2,1,0:T(8,128)(2,1)}), bf16[8,8,1024]{2,1,0:T(8,128)(2,1)S(1)}, u32[]{:S(2)}, u32[]{:S(2)}) async-start(bf16[8,8,1024]{2,1,0:T(8,128)(2,1)} %get-tuple-element.17), calls=%async_computation.3 | async-start | bytes 262144 | tf_op jit(solution)/shard_map/all_to_all | solution.py:404
  88.3 16.9 %all-to-all-done.3 = bf16[8,8,1024]{2,1,0:T(8,128)(2,1)S(1)} async-done(((bf16[8,8,1024]{2,1,0:T(8,128)(2,1)}), bf16[8,8,1024]{2,1,0:T(8,128)(2,1)S(1)}, u32[]{:S(2)}, u32[]{:S(2)}) %all-to-all-start.3) | async-done | bytes 131104 | tf_op jit(solution)/shard_map/all_to_all | solution.py:404
  105.3 0.7 pad_maximum_fusion
  (10 shorter events, 0.1 us)
Async XLA Ops:
  0.6 21.1 %copy-start = (bf16[512,2048]{1,0:T(8,128)(2,1)S(1)}, bf16[512,2048]{1,0:T(8,128)(2,1)}, u32[]{:S(2)}) copy-start(bf16[512,2048]{1,0:T(8,128)(2,1)} %geno_ref.7) | copy-start | bytes 6291460
  0.6 20.4 %collective-permute-start.1 = (bf16[512,2048]{1,0:T(8,128)(2,1)}, bf16[512,2048]{1,0:T(8,128)(2,1)}, u32[]{:S(2)}, u32[]{:S(2)}) collective-permute-start(bf16[512,2048]{1,0:T(8,128)(2,1)} %geno_ref.7), channel_id=1, source_target_pairs={{0,64},{64,0},{128,192},{192,128},{256,320},{320,256},{384,448},{4... | collective-permute-start | bytes 6291464 | tf_op jit(solution)/shard_map/ppermute | solution.py:357
  2.7 0.7 copy-start.1
  3.4 0.7 copy-start.2
  6.1 21.5 %all-to-all-start = ((bf16[64,8,128]{2,1,0:T(8,128)(2,1)}), bf16[64,8,128]{2,1,0:T(8,128)(2,1)S(1)}, u32[]{:S(2)}, u32[]{:S(2)}) async-start(bf16[64,8,128]{2,1,0:T(8,128)(2,1)} %get-tuple-element.10), calls=%async_computation | async-start | bytes 262144 | tf_op jit(solution)/shard_map/all_to_all | solution.py:355
  17.8 3.3 %collective-permute-start = (f32[72,512]{1,0:T(8,128)S(1)}, f32[72,512]{1,0:T(8,128)S(1)}, u32[]{:S(2)}, u32[]{:S(2)}) collective-permute-start(f32[72,512]{1,0:T(8,128)S(1)} %get-tuple-element.11.state_ref.refs_2_), channel_id=1, source_target_pairs={{0,64},{64,0},{128,192},{192,128},{256,320},{320,256},{384,448},{4... | collective-permute-start | bytes 442376 | tf_op jit(solution)/shard_map/ppermute | solution.py:359
  21.1 0.7 copy-start.3
  29.4 30.0 %all-to-all-start.1 = ((bf16[8,8,1152]{2,1,0:T(8,128)(2,1)}), bf16[8,8,1152]{2,1,0:T(8,128)(2,1)S(1)}, u32[]{:S(2)}, u32[]{:S(2)}) async-start(bf16[8,8,1152]{2,1,0:T(8,128)(2,1)} %get-tuple-element.12), calls=%async_computation.1 | async-start | bytes 294912 | tf_op jit(solution)/shard_map/all_to_all | solution.py:381
  41.8 3.6 %collective-permute-start.2 = (bf16[2,64,512]{2,1,0:T(8,128)(2,1)}, bf16[2,64,512]{2,1,0:T(8,128)(2,1)S(1)}, u32[]{:S(2)}, u32[]{:S(2)}) collective-permute-start(bf16[2,64,512]{2,1,0:T(8,128)(2,1)} %get-tuple-element.13.far_picked_ref), channel_id=1, source_target_pairs={{0,64},{64,0},{128,192},{192,128},{256,320},{320,256},{384,448},{4... | collective-permute-start | bytes 393224 | tf_op jit(solution)/shard_map/ppermute | solution.py:382
  45.3 14.0 %copy-start.4 = (bf16[2,64,512]{2,1,0:T(8,128)(2,1)}, bf16[2,64,512]{2,1,0:T(8,128)(2,1)S(1)}, u32[]{:S(2)}) copy-start(bf16[2,64,512]{2,1,0:T(8,128)(2,1)S(1)} %collective-permute-done.2.far_picked_taken_ref) | copy-start | bytes 393220
  62.0 20.2 %all-to-all-start.2 = ((bf16[8,8,1152]{2,1,0:T(8,128)(2,1)}), bf16[8,8,1152]{2,1,0:T(8,128)(2,1)S(1)}, u32[]{:S(2)}, u32[]{:S(2)}) async-start(bf16[8,8,1152]{2,1,0:T(8,128)(2,1)} %get-tuple-element.14), calls=%async_computation.2 | async-start | bytes 294912 | tf_op jit(solution)/shard_map/all_to_all | solution.py:392
  84.8 20.4 %all-to-all-start.3 = ((bf16[8,8,1024]{2,1,0:T(8,128)(2,1)}), bf16[8,8,1024]{2,1,0:T(8,128)(2,1)S(1)}, u32[]{:S(2)}, u32[]{:S(2)}) async-start(bf16[8,8,1024]{2,1,0:T(8,128)(2,1)} %get-tuple-element.17), calls=%async_computation.3 | async-start | bytes 262144 | tf_op jit(solution)/shard_map/all_to_all | solution.py:404

commit v7 on v6

--- a/solution.py
+++ b/solution.py
@@ -88,12 +88,17 @@
 
 
 def pick_body(
-    win_ref, geno_ref, margin_ref, labels_ref, out_ref, state_ref, block_ref, sem_ref
+    far_win_ref, geno_ref, margin_ref, far_labels_ref, out_ref, state_ref, block_ref, win_ref,
+    labels_ref, sem_ref,
 ):
     samples, columns = geno_ref.shape
+    wins = pltpu.make_async_copy(far_win_ref, win_ref, sem_ref.at[ITERS + 1])
+    wins.start()
+    marks = pltpu.make_async_copy(far_labels_ref, labels_ref, sem_ref.at[ITERS + 2])
+    marks.start()
     margins = pltpu.make_async_copy(margin_ref, state_ref.at[pl.ds(0, K)], sem_ref.at[ITERS])
     margins.start()
-    state_ref[K:] = jnp.broadcast_to(labels_ref[...].astype(f32), (8, samples))
+    wins.wait()
     local = win_ref[...] - lax.axis_index("feat") * columns
     mine = jnp.where((local >= 0) & (local < columns), local, 0).astype(f32)
     copies, lanes = [], []
@@ -106,6 +111,8 @@
         copy.start()
         copies.append(copy)
         lanes.append(col - start)
+    marks.wait()
+    state_ref[K:] = jnp.broadcast_to(labels_ref[...].astype(f32), (8, samples))
     rows = lax.broadcasted_iota(i32, (8, LANES), 0)
     lane = lax.broadcasted_iota(i32, (8, LANES), 1)
     tile = jnp.zeros((8, LANES), f32)
@@ -243,7 +250,7 @@
 
 def second_table_body(
     shared_ref, state_ref, far_state_ref, far_picked_ref, far_picked_taken_ref, geno_ref,
-    far_taken_ref, out_ref, far_coef_ref, taken_ref, table_ref, tiles_ref, state_taken_ref,
+    taken_ref, out_ref, far_coef_ref, table_ref, tiles_ref, state_taken_ref,
     picked_ref, picked_taken_ref, coef_ref, sem_ref, load_ref,
 ):
     half = table_ref.shape[2]
@@ -255,21 +262,18 @@
         ],
         load_ref,
     )
-    taken = load_half(far_taken_ref, taken_ref, sem_ref.at[4])
     coef = coefficients(shared_ref[:, :, half:])
     coef_ref[...] = coef
     coef_copy = pltpu.make_async_copy(coef_ref, far_coef_ref, sem_ref.at[1])
     coef_copy.start()
     coef = lane_tile(coef, state_ref.shape[1] // LANES)
-    loads[0].wait()
+    wait_all(loads)
     logits = state_ref[:K] + coef * picked_ref[0].astype(f32)
     resid, prob = residuals(logits, state_ref[K : K + 1])
     tile = sums_tile(resid, prob, picked_ref[1].astype(f32))
     sums_copy = send_tile(tile, tiles_ref, out_ref, sem_ref.at[0])
-    wait_all(loads[1:])
     logits_taken = state_taken_ref[:K] + coef * picked_taken_ref[0].astype(f32)
     resid_taken, _ = residuals(logits_taken, state_taken_ref[K : K + 1])
-    taken.wait()
     table_copies = send_table(
         resid, resid_taken, geno_ref, taken_ref, table_ref, out_ref, sem_ref.at[pl.ds(2, 2)]
     )
@@ -278,7 +282,7 @@
 
 def third_table_body(
     shared_ref, far_coef_ref, state_ref, far_state_ref, far_picked_ref, far_picked_taken_ref,
-    geno_ref, far_taken_ref, out_ref, logits_ref, taken_ref, table_ref, new_ref,
+    geno_ref, taken_ref, out_ref, logits_ref, table_ref, new_ref,
     state_taken_ref, picked_ref, picked_taken_ref, coef_ref, sem_ref, load_ref,
 ):
     half = table_ref.shape[2]
@@ -291,10 +295,9 @@
         ],
         load_ref,
     )
-    taken = load_half(far_taken_ref, taken_ref, sem_ref.at[4])
     blocks = state_ref.shape[1] // LANES
     now = coefficients(shared_ref[:, :, half:])
-    loads[0].wait()
+    wait_all(loads)
     coefs = [lane_tile(coef, blocks) for coef in (coef_ref[...], now)]
 
     def updated(start, columns_ref):
@@ -302,17 +305,14 @@
             start = start + coefs[step] * columns_ref[step].astype(f32)
         return start
 
-    loads[1].wait()
     logits = updated(state_ref[:K], picked_ref)
     new_ref[...] = logits
     logits_copy = pltpu.make_async_copy(new_ref, logits_ref, sem_ref.at[0])
     logits_copy.start()
     resid, _ = residuals(logits, state_ref[K : K + 1])
-    wait_all(loads[2:])
     resid_taken, _ = residuals(
         updated(state_taken_ref[:K], picked_taken_ref), state_taken_ref[K : K + 1]
     )
-    taken.wait()
     table_copies = send_table(
         resid, resid_taken, geno_ref, taken_ref, table_ref, out_ref, sem_ref.at[pl.ds(2, 2)]
     )
@@ -331,7 +331,6 @@
     table_shape = (rows_count, class_share, half)
     tiles = pltpu.VMEM((rows_count, 8, 2 * K), bf16)
     sems = pltpu.SemaphoreType.DMA
-    got_half = pltpu.VMEM((samples, half), bf16)
     loaded = [
         pltpu.VMEM((K + 8, samples), f32),
         pltpu.VMEM((ITERS, K, samples), bf16),
@@ -345,13 +344,15 @@
             pltpu.VMEM((feat_count, ITERS * samples // LANES, LANES), bf16),
             pltpu.VMEM((K + 8, samples), f32),
         ),
-        [VMEM, HBM, HBM, VMEM],
+        [HBM] * 4,
         [
             pltpu.VMEM((ITERS, samples, LANES), bf16),
-            sems((ITERS + 1,)),
+            pltpu.VMEM((ITERS, K), i32),
+            pltpu.VMEM((1, samples), i32),
+            sems((ITERS + 3,)),
         ],
         moved=samples * LANES * 4,
-    )(winners, far(genotypes), far(base_margin.T), labels[None, :])
+    )(far(winners), far(genotypes), far(base_margin.T), far(labels[None, :]))
     cols = lax.all_to_all(sent, "feat", 0, 0, tiled=True)
 
     taken = far(lax.ppermute(genotypes, "rows", partners))
@@ -359,11 +360,11 @@
     state_taken = far(lax.ppermute(state, "rows", partners))
     state = near(state)
 
-    table = call(
+    table, taken = call(
         first_table_body,
-        pltpu.VMEM(table_shape, bf16),
+        (pltpu.VMEM(table_shape, bf16), pltpu.VMEM((samples, half), bf16)),
         [VMEM] * 3 + [HBM],
-        [got_half, sems((1,))],
+        [sems((1,))],
         flops=work,
         moved=4 * samples * half,
     )(state, state_taken, geno, taken)
@@ -384,8 +385,8 @@
     payload, coef = call(
         second_table_body,
         (pltpu.HBM(payload_shape, bf16), pltpu.HBM((K, LANES), f32)),
-        [VMEM, VMEM] + [HBM] * 3 + [VMEM, HBM],
-        [got_half, pltpu.VMEM(table_shape, bf16), tiles] + loaded + [sems((5,)), sems((3,))],
+        [VMEM, VMEM] + [HBM] * 3 + [VMEM] * 2,
+        [pltpu.VMEM(table_shape, bf16), tiles] + loaded + [sems((5,)), sems((3,))],
         flops=work,
         moved=4 * samples * half,
     )(near(shared0), state, state_taken, far(picked), picked_taken, geno, taken)
@@ -394,8 +395,8 @@
     payload, logits = call(
         third_table_body,
         (pltpu.HBM(table_shape, bf16), pltpu.HBM((K, samples), f32)),
-        [VMEM, HBM, VMEM] + [HBM] * 3 + [VMEM, HBM],
-        [got_half, pltpu.VMEM(table_shape, bf16), pltpu.VMEM((K, samples), f32)]
+        [VMEM, HBM, VMEM] + [HBM] * 3 + [VMEM] * 2,
+        [pltpu.VMEM(table_shape, bf16), pltpu.VMEM((K, samples), f32)]
         + loaded
         + [sems((5,)), sems((4,))],
         flops=work,

time: 107 us -> 105 us (0.981)
    unnamed x10 -> x6, local copies, waits for them, and re-layouts: 2.02 us -> 0.67 us
  transfers between devices with their start and end apart: 7 -> 7, of which waited for: 6 -> 6; matrix products, arithmetic and copies ran while one was open for 0% -> 1% of each run, Pallas kernels for 4% -> 5%
where the time goes in v7:
time: 105 us
  waiting for transfers between devices  52.4 us (50%)
  starting transfers between devices  37.2 us (35%)
  Pallas kernels  11.9 us (11%)
  local copies, waits for them, and re-layouts  1.61 us (2%)
    all_to_all x1, waiting for transfers between devices, shards(): shared2 = lax.all_to_all(payload, 'rows', 0, 0, tiled=True)  16.9 us
    all_to_all x1, waiting for transfers between devices, shards(): shared1 = lax.all_to_all(payload, 'rows', 0, 0, tiled=True)  15.8 us
    all_to_all x1, waiting for transfers between devices, shards(): shared0 = lax.all_to_all(payload, 'rows', 0, 0, tiled=True)  13.9 us
    all_to_all x1, starting transfers between devices, shards(): shared0 = lax.all_to_all(payload, 'rows', 0, 0, tiled=True)  12.4 us
    all_to_all x1, starting transfers between devices, shards(): cols = lax.all_to_all(sent, 'feat', 0, 0, tiled=True)  11.7 us
    all_to_all x1, starting transfers between devices, shards(): shared1 = lax.all_to_all(payload, 'rows', 0, 0, tiled=True)  3.39 us
    all_to_all x1, starting transfers between devices, shards(): shared2 = lax.all_to_all(payload, 'rows', 0, 0, tiled=True)  3.38 us
    all_to_all x1, waiting for transfers between devices, shards(): cols = lax.all_to_all(sent, 'feat', 0, 0, tiled=True)  3.2 us
  transfers between devices with their start and end apart: 7, of which 6 were waited for; matrix products, arithmetic and copies ran while one was open for 1% of the time, Pallas kernels for 5%

profile of v7, /device:TPU:32, one launch (start us, length us, event | category | flops | bytes accessed | tf_op | source)
XLA Modules:
  0.0 104.7 jit_solution(6648651281948655882)
XLA Ops:
  0.6 0.0 copy-start
  0.6 2.1 %collective-permute-start.1 = (bf16[512,2048]{1,0:T(8,128)(2,1)}, bf16[512,2048]{1,0:T(8,128)(2,1)}, u32[]{:S(2)}, u32[]{:S(2)}) collective-permute-start(bf16[512,2048]{1,0:T(8,128)(2,1)} %geno_ref.7), channel_id=1, source_target_pairs={{0,64},{64,0},{128,192},{192,128},{256,320},{320,256},{384,448},{4... | collective-permute-start | bytes 6291464 | tf_op jit(solution)/shard_map/ppermute | solution.py:358
  2.7 2.7 %shard_map.59 = (bf16[64,8,128]{2,1,0:T(8,128)(2,1)}, f32[72,512]{1,0:T(8,128)S(1)}) custom-call(s32[2,64]{1,0:T(2,128)} %refs_1_.1, bf16[512,2048]{1,0:T(8,128)(2,1)} %geno_ref.7, f32[64,512]{1,0:T(8,128)} %bitcast.30, s32[1,512]{1,0:T(1,128)} %bitcast.31), custom_call_target="tpu_custom_call" | custom-call | bytes 262144 | tf_op jit(solution)/shard_map/pallas_call | solution.py:341
  5.5 11.7 %all-to-all-start = ((bf16[64,8,128]{2,1,0:T(8,128)(2,1)}), bf16[64,8,128]{2,1,0:T(8,128)(2,1)S(1)}, u32[]{:S(2)}, u32[]{:S(2)}) async-start(bf16[64,8,128]{2,1,0:T(8,128)(2,1)} %get-tuple-element.12), calls=%async_computation | async-start | bytes 262144 | tf_op jit(solution)/shard_map/all_to_all | solution.py:356
  17.1 1.9 %collective-permute-start = (f32[72,512]{1,0:T(8,128)S(1)}, f32[72,512]{1,0:T(8,128)S(1)}, u32[]{:S(2)}, u32[]{:S(2)}) collective-permute-start(f32[72,512]{1,0:T(8,128)S(1)} %get-tuple-element.13.state_ref.refs_2_), channel_id=1, source_target_pairs={{0,64},{64,0},{128,192},{192,128},{256,320},{320,256},{384,448},{4... | collective-permute-start | bytes 442376 | tf_op jit(solution)/shard_map/ppermute | solution.py:360
  19.1 1.3 %collective-permute-done.state_taken_ref.far_state_ref = f32[72,512]{1,0:T(8,128)S(1)} collective-permute-done((f32[72,512]{1,0:T(8,128)S(1)}, f32[72,512]{1,0:T(8,128)S(1)}, u32[]{:S(2)}, u32[]{:S(2)}) %collective-permute-start) | collective-permute-done | bytes 147488 | tf_op jit(solution)/shard_map/ppermute | solution.py:360
  20.4 0.0 copy-start.2
  20.4 0.0 collective-permute-done.1.far_taken_ref
  20.4 0.7 copy-done.2
  21.1 0.0 copy-done
  21.1 2.7 %shard_map.60 = (bf16[8,8,1024]{2,1,0:T(8,128)(2,1)S(1)}, bf16[512,1024]{1,0:T(8,128)(2,1)S(1)}) custom-call(f32[72,512]{1,0:T(8,128)S(1)} %get-tuple-element.13.state_ref.refs_2_, f32[72,512]{1,0:T(8,128)} %copy-done.2, bf16[512,2048]{1,0:T(8,128)(2,1)S(1)} %copy-done, bf16[512,2048]{1,0:T(8,128)(2,1)} %collective-permute-done.1.far_taken_ref), custom_call_target="tpu_custom_call" | custom-call | flops 134217728 | bytes 2097152 | tf_op jit(solution)/shard_map/pallas_call | solution.py:363
  23.7 3.2 %all-to-all-done.refs_0_ = bf16[64,8,128]{2,1,0:T(8,128)(2,1)S(1)} async-done(((bf16[64,8,128]{2,1,0:T(8,128)(2,1)}), bf16[64,8,128]{2,1,0:T(8,128)(2,1)S(1)}, u32[]{:S(2)}, u32[]{:S(2)}) %all-to-all-start) | async-done | bytes 131104 | tf_op jit(solution)/shard_map/all_to_all | solution.py:356
  26.9 1.7 %shard_map.61 = (bf16[8,8,1152]{2,1,0:T(8,128)(2,1)}, bf16[2,64,512]{2,1,0:T(8,128)(2,1)}) custom-call(bf16[64,8,128]{2,1,0:T(8,128)(2,1)S(1)} %all-to-all-done.refs_0_, s32[2,64]{1,0:T(2,128)} %refs_1_.1, f32[72,512]{1,0:T(8,128)S(1)} %get-tuple-element.13.state_ref.refs_2_, bf16[8,8,1024]{2,1,0:T(8,128)(2,1)S(1)} %get-tuple-element.14.refs_3_), custom_call_target="tpu_custom_call" | custom-call | bytes 2097152 | tf_op jit(solution)/shard_map/pallas_call | solution.py:375
  28.7 12.4 %all-to-all-start.1 = ((bf16[8,8,1152]{2,1,0:T(8,128)(2,1)}), bf16[8,8,1152]{2,1,0:T(8,128)(2,1)S(1)}, u32[]{:S(2)}, u32[]{:S(2)}) async-start(bf16[8,8,1152]{2,1,0:T(8,128)(2,1)} %get-tuple-element.15), calls=%async_computation.1 | async-start | bytes 294912 | tf_op jit(solution)/shard_map/all_to_all | solution.py:382
  41.1 2.4 %collective-permute-start.2 = (bf16[2,64,512]{2,1,0:T(8,128)(2,1)}, bf16[2,64,512]{2,1,0:T(8,128)(2,1)}, u32[]{:S(2)}, u32[]{:S(2)}) collective-permute-start(bf16[2,64,512]{2,1,0:T(8,128)(2,1)} %get-tuple-element.16.far_picked_ref), channel_id=1, source_target_pairs={{0,64},{64,0},{128,192},{192,128},{256,320},{320,256},{384,448},{4... | collective-permute-start | bytes 393224 | tf_op jit(solution)/shard_map/ppermute | solution.py:383
  43.5 1.3 %collective-permute-done.2.far_picked_taken_ref = bf16[2,64,512]{2,1,0:T(8,128)(2,1)} collective-permute-done((bf16[2,64,512]{2,1,0:T(8,128)(2,1)}, bf16[2,64,512]{2,1,0:T(8,128)(2,1)}, u32[]{:S(2)}, u32[]{:S(2)}) %collective-permute-start.2) | collective-permute-done | bytes 131104 | tf_op jit(solution)/shard_map/ppermute | solution.py:383
  44.8 13.9 %all-to-all-done.1.shared_ref = bf16[8,8,1152]{2,1,0:T(8,128)(2,1)S(1)} async-done(((bf16[8,8,1152]{2,1,0:T(8,128)(2,1)}), bf16[8,8,1152]{2,1,0:T(8,128)(2,1)S(1)}, u32[]{:S(2)}, u32[]{:S(2)}) %all-to-all-start.1) | async-done | bytes 147488 | tf_op jit(solution)/shard_map/all_to_all | solution.py:382
  58.7 0.0 copy-start.1
  58.7 2.4 %shard_map.62 = (bf16[8,8,1152]{2,1,0:T(8,128)(2,1)}, f32[64,128]{1,0:T(8,128)}) custom-call(bf16[8,8,1152]{2,1,0:T(8,128)(2,1)S(1)} %all-to-all-done.1.shared_ref, f32[72,512]{1,0:T(8,128)S(1)} %get-tuple-element.13.state_ref.refs_2_, f32[72,512]{1,0:T(8,128)} %copy-done.2, bf16[2,64,512]{2,1,0:T(8,128)(2,1)} %get-tuple-element.16.far_picked_ref, ...), custom_call_target="tpu_custom_call" | custom-call | flops 134217728 | bytes 2097152 | tf_op jit(solution)/shard_map/pallas_call | solution.py:385
  61.1 0.0 copy-done.1
  61.1 3.4 %all-to-all-start.2 = ((bf16[8,8,1152]{2,1,0:T(8,128)(2,1)}), bf16[8,8,1152]{2,1,0:T(8,128)(2,1)S(1)}, u32[]{:S(2)}, u32[]{:S(2)}) async-start(bf16[8,8,1152]{2,1,0:T(8,128)(2,1)} %get-tuple-element.18), calls=%async_computation.2 | async-start | bytes 294912 | tf_op jit(solution)/shard_map/all_to_all | solution.py:393
  64.5 0.9 slice.32
  65.4 15.8 %all-to-all-done.2.shared_ref = bf16[8,8,1152]{2,1,0:T(8,128)(2,1)S(1)} async-done(((bf16[8,8,1152]{2,1,0:T(8,128)(2,1)}), bf16[8,8,1152]{2,1,0:T(8,128)(2,1)S(1)}, u32[]{:S(2)}, u32[]{:S(2)}) %all-to-all-start.2) | async-done | bytes 147488 | tf_op jit(solution)/shard_map/all_to_all | solution.py:393
  81.2 2.3 %shard_map.63 = (bf16[8,8,1024]{2,1,0:T(8,128)(2,1)}, f32[64,512]{1,0:T(8,128)}) custom-call(bf16[8,8,1152]{2,1,0:T(8,128)(2,1)S(1)} %all-to-all-done.2.shared_ref, f32[64,128]{1,0:T(8,128)} %get-tuple-element.19.far_coef_ref, f32[72,512]{1,0:T(8,128)S(1)} %get-tuple-element.13.state_ref.refs_2_, f32[72,512]{1,0:T(8,128)} %copy-done.2, ...), custom_call_target="tpu_custom_call" | custom-call | flops 134217728 | bytes 2097152 | tf_op jit(solution)/shard_map/pallas_call | solution.py:395
  83.6 3.4 %all-to-all-start.3 = ((bf16[8,8,1024]{2,1,0:T(8,128)(2,1)}), bf16[8,8,1024]{2,1,0:T(8,128)(2,1)S(1)}, u32[]{:S(2)}, u32[]{:S(2)}) async-start(bf16[8,8,1024]{2,1,0:T(8,128)(2,1)} %get-tuple-element.21), calls=%async_computation.3 | async-start | bytes 262144 | tf_op jit(solution)/shard_map/all_to_all | solution.py:405
  87.1 16.9 %all-to-all-done.3 = bf16[8,8,1024]{2,1,0:T(8,128)(2,1)S(1)} async-done(((bf16[8,8,1024]{2,1,0:T(8,128)(2,1)}), bf16[8,8,1024]{2,1,0:T(8,128)(2,1)S(1)}, u32[]{:S(2)}, u32[]{:S(2)}) %all-to-all-start.3) | async-done | bytes 131104 | tf_op jit(solution)/shard_map/all_to_all | solution.py:405
  104.0 0.7 pad_maximum_fusion
  (9 shorter events, 0.1 us)
Async XLA Ops:
  0.6 20.4 %copy-start = (bf16[512,2048]{1,0:T(8,128)(2,1)S(1)}, bf16[512,2048]{1,0:T(8,128)(2,1)}, u32[]{:S(2)}) copy-start(bf16[512,2048]{1,0:T(8,128)(2,1)} %geno_ref.7) | copy-start | bytes 6291460
  0.6 19.8 %collective-permute-start.1 = (bf16[512,2048]{1,0:T(8,128)(2,1)}, bf16[512,2048]{1,0:T(8,128)(2,1)}, u32[]{:S(2)}, u32[]{:S(2)}) collective-permute-start(bf16[512,2048]{1,0:T(8,128)(2,1)} %geno_ref.7), channel_id=1, source_target_pairs={{0,64},{64,0},{128,192},{192,128},{256,320},{320,256},{384,448},{4... | collective-permute-start | bytes 6291464 | tf_op jit(solution)/shard_map/ppermute | solution.py:358
  5.5 21.5 %all-to-all-start = ((bf16[64,8,128]{2,1,0:T(8,128)(2,1)}), bf16[64,8,128]{2,1,0:T(8,128)(2,1)S(1)}, u32[]{:S(2)}, u32[]{:S(2)}) async-start(bf16[64,8,128]{2,1,0:T(8,128)(2,1)} %get-tuple-element.12), calls=%async_computation | async-start | bytes 262144 | tf_op jit(solution)/shard_map/all_to_all | solution.py:356
  17.1 3.3 %collective-permute-start = (f32[72,512]{1,0:T(8,128)S(1)}, f32[72,512]{1,0:T(8,128)S(1)}, u32[]{:S(2)}, u32[]{:S(2)}) collective-permute-start(f32[72,512]{1,0:T(8,128)S(1)} %get-tuple-element.13.state_ref.refs_2_), channel_id=1, source_target_pairs={{0,64},{64,0},{128,192},{192,128},{256,320},{320,256},{384,448},{4... | collective-permute-start | bytes 442376 | tf_op jit(solution)/shard_map/ppermute | solution.py:360
  20.4 0.7 copy-start.2
  28.7 30.0 %all-to-all-start.1 = ((bf16[8,8,1152]{2,1,0:T(8,128)(2,1)}), bf16[8,8,1152]{2,1,0:T(8,128)(2,1)S(1)}, u32[]{:S(2)}, u32[]{:S(2)}) async-start(bf16[8,8,1152]{2,1,0:T(8,128)(2,1)} %get-tuple-element.15), calls=%async_computation.1 | async-start | bytes 294912 | tf_op jit(solution)/shard_map/all_to_all | solution.py:382
  41.1 3.7 %collective-permute-start.2 = (bf16[2,64,512]{2,1,0:T(8,128)(2,1)}, bf16[2,64,512]{2,1,0:T(8,128)(2,1)}, u32[]{:S(2)}, u32[]{:S(2)}) collective-permute-start(bf16[2,64,512]{2,1,0:T(8,128)(2,1)} %get-tuple-element.16.far_picked_ref), channel_id=1, source_target_pairs={{0,64},{64,0},{128,192},{192,128},{256,320},{320,256},{384,448},{4... | collective-permute-start | bytes 393224 | tf_op jit(solution)/shard_map/ppermute | solution.py:383
  58.7 2.4 %copy-start.1 = (bf16[8,8,1152]{2,1,0:T(8,128)(2,1)}, bf16[8,8,1152]{2,1,0:T(8,128)(2,1)S(1)}, u32[]{:S(2)}) copy-start(bf16[8,8,1152]{2,1,0:T(8,128)(2,1)S(1)} %all-to-all-done.1.shared_ref) | copy-start | bytes 442372
  61.1 20.1 %all-to-all-start.2 = ((bf16[8,8,1152]{2,1,0:T(8,128)(2,1)}), bf16[8,8,1152]{2,1,0:T(8,128)(2,1)S(1)}, u32[]{:S(2)}, u32[]{:S(2)}) async-start(bf16[8,8,1152]{2,1,0:T(8,128)(2,1)} %get-tuple-element.18), calls=%async_computation.2 | async-start | bytes 294912 | tf_op jit(solution)/shard_map/all_to_all | solution.py:393
  83.6 20.4 %all-to-all-start.3 = ((bf16[8,8,1024]{2,1,0:T(8,128)(2,1)}), bf16[8,8,1024]{2,1,0:T(8,128)(2,1)S(1)}, u32[]{:S(2)}, u32[]{:S(2)}) async-start(bf16[8,8,1024]{2,1,0:T(8,128)(2,1)} %get-tuple-element.21), calls=%async_computation.3 | async-start | bytes 262144 | tf_op jit(solution)/shard_map/all_to_all | solution.py:405

commit v8 on v7

--- a/solution.py
+++ b/solution.py
@@ -42,16 +42,6 @@
 
 def far(values):
     return pltpu.with_memory_space_constraint(values, pltpu.HBM)
-
-
-def load(pairs, sem_ref):
-    copies = [
-        pltpu.make_async_copy(source, target, sem_ref.at[i])
-        for i, (source, target) in enumerate(pairs)
-    ]
-    for copy in copies:
-        copy.start()
-    return copies
 
 
 def wait_all(copies):
@@ -129,25 +119,26 @@
     margins.wait()
 
 
-def half_start(geno_ref):
-    half = geno_ref.shape[1] // 2
-    return pl.multiple_of(lax.rem(lax.axis_index("rows"), 2) * half, LANES)
-
-
-def half_table(resid, resid_taken, geno_ref, taken_ref, start, width):
-    own_span = pl.ds(pl.multiple_of(half_start(geno_ref) + start, LANES), width)
-    first = jnp.dot(resid, geno_ref[:, own_span], preferred_element_type=f32)
-    second = taken_ref[:, pl.ds(start, width)]
-    return first + jnp.dot(resid_taken, second, preferred_element_type=f32)
-
-
-def load_half(whole_ref, half_ref, sem_ref):
-    start = half_start(whole_ref)
-    copy = pltpu.make_async_copy(
-        whole_ref.at[:, pl.ds(start, half_ref.shape[1])], half_ref, sem_ref
-    )
-    copy.start()
-    return copy
+def load_halves(geno_ref, far_taken_ref, both_ref, sem_ref):
+    samples = geno_ref.shape[0]
+    half = both_ref.shape[1]
+    start = pl.multiple_of(lax.rem(lax.axis_index("rows"), 2) * half, LANES)
+    copies = [
+        pltpu.make_async_copy(
+            whole_ref.at[:, pl.ds(start, half)],
+            both_ref.at[pl.ds(place * samples, samples)],
+            sem_ref.at[place],
+        )
+        for place, whole_ref in enumerate((geno_ref, far_taken_ref))
+    ]
+    for copy in copies:
+        copy.start()
+    return copies
+
+
+def half_table(resid, resid_taken, both_ref, start, width):
+    whole = jnp.concatenate([resid, resid_taken], axis=1)
+    return jnp.dot(whole, both_ref[:, pl.ds(start, width)], preferred_element_type=f32)
 
 
 def sums_tile(resid, prob, picked):
@@ -188,14 +179,12 @@
     return copy
 
 
-def send_table(resid, resid_taken, geno_ref, taken_ref, table_ref, out_ref, sem_ref, pieces=2):
+def send_table(resid, resid_taken, both_ref, table_ref, out_ref, sem_ref, pieces=2):
     width = table_ref.shape[2] // pieces
     copies = []
     for piece in range(pieces):
         span = pl.ds(piece * width, width)
-        table = half_table(
-            resid, resid_taken, geno_ref, taken_ref, piece * width, width
-        )
+        table = half_table(resid, resid_taken, both_ref, piece * width, width)
         table_ref[:, :, span] = table.reshape(table_ref.shape[0], -1, width).astype(bf16)
         copy = pltpu.make_async_copy(
             table_ref.at[:, :, span], out_ref.at[:, :, span], sem_ref.at[piece]
@@ -206,18 +195,18 @@
 
 
 def first_table_body(
-    state_ref, state_taken_ref, geno_ref, far_taken_ref, out_ref, taken_ref, sem_ref
-):
-    taken = load_half(far_taken_ref, taken_ref, sem_ref.at[0])
+    state_ref, state_taken_ref, geno_ref, far_taken_ref, out_ref, both_ref, sem_ref
+):
+    copies = load_halves(geno_ref, far_taken_ref, both_ref, sem_ref)
     resid, _ = residuals(state_ref[:K], state_ref[K : K + 1])
     resid_taken, _ = residuals(state_taken_ref[:K], state_taken_ref[K : K + 1])
-    taken.wait()
-    table = half_table(resid, resid_taken, geno_ref, taken_ref, 0, out_ref.shape[2])
+    wait_all(copies)
+    table = half_table(resid, resid_taken, both_ref, 0, out_ref.shape[2])
     out_ref[...] = table.reshape(out_ref.shape).astype(bf16)
 
 
 def first_sums_body(
-    cols_ref, far_win_ref, state_ref, table_ref, out_ref, far_picked_ref, tiles_ref, picked_ref,
+    cols_ref, far_win_ref, state_ref, table_ref, out_ref, picked_ref, far_picked_ref, tiles_ref,
     win_ref, sem_ref, *, columns,
 ):
     half = table_ref.shape[2]
@@ -225,7 +214,7 @@
     first = pltpu.make_async_copy(
         table_ref, out_ref.at[:, :, pl.ds(0, half)], sem_ref.at[0]
     )
-    wins = pltpu.make_async_copy(far_win_ref, win_ref, sem_ref.at[3])
+    wins = pltpu.make_async_copy(far_win_ref, win_ref, sem_ref.at[2])
     wins.start()
     first.start()
     resid, prob = residuals(state_ref[:K], state_ref[K : K + 1])
@@ -241,7 +230,7 @@
                 place, piece, (((0,), (0,)), ((), ())), preferred_element_type=f32
             )
             picked_ref[step, :, j * LANES : (j + 1) * LANES] = picked.astype(bf16)
-    third = pltpu.make_async_copy(picked_ref, far_picked_ref, sem_ref.at[2])
+    third = pltpu.make_async_copy(picked_ref, far_picked_ref, sem_ref.at[3])
     third.start()
     tile = sums_tile(resid, prob, picked_ref[0].astype(f32))
     second = send_tile(tile, tiles_ref, out_ref, sem_ref.at[1])
@@ -249,25 +238,13 @@
 
 
 def second_table_body(
-    shared_ref, state_ref, far_state_ref, far_picked_ref, far_picked_taken_ref, geno_ref,
-    taken_ref, out_ref, far_coef_ref, table_ref, tiles_ref, state_taken_ref,
-    picked_ref, picked_taken_ref, coef_ref, sem_ref, load_ref,
+    shared_ref, state_ref, state_taken_ref, picked_ref, picked_taken_ref, both_ref,
+    out_ref, coef_ref, table_ref, tiles_ref, sem_ref,
 ):
     half = table_ref.shape[2]
-    loads = load(
-        [
-            (far_picked_ref, picked_ref),
-            (far_state_ref, state_taken_ref),
-            (far_picked_taken_ref, picked_taken_ref),
-        ],
-        load_ref,
-    )
     coef = coefficients(shared_ref[:, :, half:])
     coef_ref[...] = coef
-    coef_copy = pltpu.make_async_copy(coef_ref, far_coef_ref, sem_ref.at[1])
-    coef_copy.start()
     coef = lane_tile(coef, state_ref.shape[1] // LANES)
-    wait_all(loads)
     logits = state_ref[:K] + coef * picked_ref[0].astype(f32)
     resid, prob = residuals(logits, state_ref[K : K + 1])
     tile = sums_tile(resid, prob, picked_ref[1].astype(f32))
@@ -275,29 +252,18 @@
     logits_taken = state_taken_ref[:K] + coef * picked_taken_ref[0].astype(f32)
     resid_taken, _ = residuals(logits_taken, state_taken_ref[K : K + 1])
     table_copies = send_table(
-        resid, resid_taken, geno_ref, taken_ref, table_ref, out_ref, sem_ref.at[pl.ds(2, 2)]
-    )
-    wait_all([coef_copy, sums_copy] + table_copies)
+        resid, resid_taken, both_ref, table_ref, out_ref, sem_ref.at[pl.ds(2, 2)]
+    )
+    wait_all([sums_copy] + table_copies)
 
 
 def third_table_body(
-    shared_ref, far_coef_ref, state_ref, far_state_ref, far_picked_ref, far_picked_taken_ref,
-    geno_ref, taken_ref, out_ref, logits_ref, table_ref, new_ref,
-    state_taken_ref, picked_ref, picked_taken_ref, coef_ref, sem_ref, load_ref,
+    shared_ref, coef_ref, state_ref, state_taken_ref, picked_ref, picked_taken_ref, both_ref,
+    out_ref, logits_ref, table_ref, new_ref, sem_ref,
 ):
     half = table_ref.shape[2]
-    loads = load(
-        [
-            (far_coef_ref, coef_ref),
-            (far_picked_ref, picked_ref),
-            (far_state_ref, state_taken_ref),
-            (far_picked_taken_ref, picked_taken_ref),
-        ],
-        load_ref,
-    )
     blocks = state_ref.shape[1] // LANES
     now = coefficients(shared_ref[:, :, half:])
-    wait_all(loads)
     coefs = [lane_tile(coef, blocks) for coef in (coef_ref[...], now)]
 
     def updated(start, columns_ref):
@@ -314,7 +280,7 @@
         updated(state_taken_ref[:K], picked_taken_ref), state_taken_ref[K : K + 1]
     )
     table_copies = send_table(
-        resid, resid_taken, geno_ref, taken_ref, table_ref, out_ref, sem_ref.at[pl.ds(2, 2)]
+        resid, resid_taken, both_ref, table_ref, out_ref, sem_ref.at[pl.ds(2, 2)]
     )
     wait_all([logits_copy] + table_copies)
 
@@ -331,12 +297,6 @@
     table_shape = (rows_count, class_share, half)
     tiles = pltpu.VMEM((rows_count, 8, 2 * K), bf16)
     sems = pltpu.SemaphoreType.DMA
-    loaded = [
-        pltpu.VMEM((K + 8, samples), f32),
-        pltpu.VMEM((ITERS, K, samples), bf16),
-        pltpu.VMEM((ITERS, K, samples), bf16),
-        pltpu.VMEM((K, LANES), f32),
-    ]
 
     sent, state = call(
         pick_body,
@@ -356,15 +316,15 @@
     cols = lax.all_to_all(sent, "feat", 0, 0, tiled=True)
 
     taken = far(lax.ppermute(genotypes, "rows", partners))
-    geno = near(genotypes)
-    state_taken = far(lax.ppermute(state, "rows", partners))
+    geno = far(genotypes)
+    state_taken = near(lax.ppermute(state, "rows", partners))
     state = near(state)
 
-    table, taken = call(
+    table, both = call(
         first_table_body,
-        (pltpu.VMEM(table_shape, bf16), pltpu.VMEM((samples, half), bf16)),
-        [VMEM] * 3 + [HBM],
-        [sems((1,))],
+        (pltpu.VMEM(table_shape, bf16), pltpu.VMEM((2 * samples, half), bf16)),
+        [VMEM, VMEM, HBM, HBM],
+        [sems((2,))],
         flops=work,
         moved=4 * samples * half,
     )(state, state_taken, geno, taken)
@@ -372,36 +332,39 @@
     def first_sums(*refs):
         first_sums_body(*refs, columns=columns)
 
-    payload, picked = call(
+    picked_shape = (ITERS, K, samples)
+    payload, picked, far_picked = call(
         first_sums,
-        (pltpu.HBM(payload_shape, bf16), pltpu.HBM((ITERS, K, samples), bf16)),
+        (
+            pltpu.HBM(payload_shape, bf16),
+            pltpu.VMEM(picked_shape, bf16),
+            pltpu.HBM(picked_shape, bf16),
+        ),
         [VMEM, HBM, VMEM, VMEM],
-        [tiles, pltpu.VMEM((ITERS, K, samples), bf16), pltpu.VMEM((ITERS, K), i32), sems((4,))],
+        [tiles, pltpu.VMEM((ITERS, K), i32), sems((4,))],
         moved=4 * samples * half,
     )(near(cols), far(winners), state, table)
     shared0 = lax.all_to_all(payload, "rows", 0, 0, tiled=True)
-    picked_taken = far(lax.ppermute(picked, "rows", partners))
+    picked_taken = near(lax.ppermute(far_picked, "rows", partners))
 
     payload, coef = call(
         second_table_body,
-        (pltpu.HBM(payload_shape, bf16), pltpu.HBM((K, LANES), f32)),
-        [VMEM, VMEM] + [HBM] * 3 + [VMEM] * 2,
-        [pltpu.VMEM(table_shape, bf16), tiles] + loaded + [sems((5,)), sems((3,))],
+        (pltpu.HBM(payload_shape, bf16), pltpu.VMEM((K, LANES), f32)),
+        [VMEM] * 6,
+        [pltpu.VMEM(table_shape, bf16), tiles, sems((4,))],
         flops=work,
         moved=4 * samples * half,
-    )(near(shared0), state, state_taken, far(picked), picked_taken, geno, taken)
+    )(near(shared0), state, state_taken, near(picked), picked_taken, both)
     shared1 = lax.all_to_all(payload, "rows", 0, 0, tiled=True)
 
     payload, logits = call(
         third_table_body,
         (pltpu.HBM(table_shape, bf16), pltpu.HBM((K, samples), f32)),
-        [VMEM, HBM, VMEM] + [HBM] * 3 + [VMEM] * 2,
-        [pltpu.VMEM(table_shape, bf16), pltpu.VMEM((K, samples), f32)]
-        + loaded
-        + [sems((5,)), sems((4,))],
+        [VMEM] * 7,
+        [pltpu.VMEM(table_shape, bf16), pltpu.VMEM((K, samples), f32), sems((4,))],
         flops=work,
         moved=4 * samples * half,
-    )(near(shared1), far(coef), state, state_taken, far(picked), picked_taken, geno, taken)
+    )(near(shared1), near(coef), state, state_taken, near(picked), picked_taken, both)
     shared2 = lax.all_to_all(payload, "rows", 0, 0, tiled=True)
 
     tables = []

time: 105 us -> 103 us (0.981)
  Pallas kernels: 11.9 us -> 9.28 us
  waiting for transfers between devices: 52.4 us -> 54.6 us
  local copies, waits for them, and re-layouts: 1.61 us -> 0.04 us
    pallas_call x3, Pallas kernels: 6.79 us -> 5.23 us  [the longest x1 2.05 us: shards(): call(first_table_body, (pltpu.VMEM(table_shape, bf16), pltpu.VMEM((2 * sa...]
    all_to_all x1, waiting for transfers between devices: 3.2 us -> 4.47 us  [shards(): cols = lax.all_to_all(sent, 'feat', 0, 0, tiled=True)]
  transfers between devices with their start and end apart: 7 -> 7, of which waited for: 6 -> 6; matrix products, arithmetic and copies ran while one was open for 1% -> 0% of each run, Pallas kernels for 5% -> 5%
where the time goes in v8:
time: 103 us
  waiting for transfers between devices  54.6 us (53%)
  starting transfers between devices  37.1 us (36%)
  Pallas kernels  9.28 us (9%)
    all_to_all x1, waiting for transfers between devices, shards(): shared2 = lax.all_to_all(payload, 'rows', 0, 0, tiled=True)  16.9 us
    all_to_all x1, waiting for transfers between devices, shards(): shared1 = lax.all_to_all(payload, 'rows', 0, 0, tiled=True)  16.7 us
    all_to_all x1, waiting for transfers between devices, shards(): shared0 = lax.all_to_all(payload, 'rows', 0, 0, tiled=True)  14 us
    all_to_all x1, starting transfers between devices, shards(): shared0 = lax.all_to_all(payload, 'rows', 0, 0, tiled=True)  12.4 us
    all_to_all x1, starting transfers between devices, shards(): cols = lax.all_to_all(sent, 'feat', 0, 0, tiled=True)  11.7 us
    all_to_all x1, waiting for transfers between devices, shards(): cols = lax.all_to_all(sent, 'feat', 0, 0, tiled=True)  4.47 us
    all_to_all x1, starting transfers between devices, shards(): shared1 = lax.all_to_all(payload, 'rows', 0, 0, tiled=True)  3.39 us
    all_to_all x1, starting transfers between devices, shards(): shared2 = lax.all_to_all(payload, 'rows', 0, 0, tiled=True)  3.38 us
  transfers between devices with their start and end apart: 7, of which 6 were waited for; matrix products, arithmetic and copies ran while one was open for 0% of the time, Pallas kernels for 5%

profile of v8, /device:TPU:32, one launch (start us, length us, event | category | flops | bytes accessed | tf_op | source)
XLA Modules:
  0.0 102.6 jit_solution(14488780454123164734)
XLA Ops:
  0.6 1.9 %collective-permute-start.1 = (bf16[512,2048]{1,0:T(8,128)(2,1)}, bf16[512,2048]{1,0:T(8,128)(2,1)}, u32[]{:S(2)}, u32[]{:S(2)}) collective-permute-start(bf16[512,2048]{1,0:T(8,128)(2,1)} %geno_ref.3), channel_id=1, source_target_pairs={{0,64},{64,0},{128,192},{192,128},{256,320},{320,256},{384,448},{4... | collective-permute-start | bytes 6291464 | tf_op jit(solution)/shard_map/ppermute | solution.py:318
  2.6 2.7 %shard_map.59 = (bf16[64,8,128]{2,1,0:T(8,128)(2,1)}, f32[72,512]{1,0:T(8,128)S(1)}) custom-call(s32[2,64]{1,0:T(2,128)} %refs_1_.1, bf16[512,2048]{1,0:T(8,128)(2,1)} %geno_ref.3, f32[64,512]{1,0:T(8,128)} %bitcast.30, s32[1,512]{1,0:T(1,128)} %bitcast.31), custom_call_target="tpu_custom_call" | custom-call | bytes 262144 | tf_op jit(solution)/shard_map/pallas_call | solution.py:301
  5.3 11.7 %all-to-all-start = ((bf16[64,8,128]{2,1,0:T(8,128)(2,1)}), bf16[64,8,128]{2,1,0:T(8,128)(2,1)S(1)}, u32[]{:S(2)}, u32[]{:S(2)}) async-start(bf16[64,8,128]{2,1,0:T(8,128)(2,1)} %get-tuple-element.13), calls=%async_computation | async-start | bytes 262144 | tf_op jit(solution)/shard_map/all_to_all | solution.py:316
  17.0 1.9 %collective-permute-start = (f32[72,512]{1,0:T(8,128)S(1)}, f32[72,512]{1,0:T(8,128)S(1)}, u32[]{:S(2)}, u32[]{:S(2)}) collective-permute-start(f32[72,512]{1,0:T(8,128)S(1)} %get-tuple-element.14.state_ref.refs_2_), channel_id=1, source_target_pairs={{0,64},{64,0},{128,192},{192,128},{256,320},{320,256},{384,448},{4... | collective-permute-start | bytes 442376 | tf_op jit(solution)/shard_map/ppermute | solution.py:320
  18.9 1.3 %collective-permute-done.state_taken_ref = f32[72,512]{1,0:T(8,128)S(1)} collective-permute-done((f32[72,512]{1,0:T(8,128)S(1)}, f32[72,512]{1,0:T(8,128)S(1)}, u32[]{:S(2)}, u32[]{:S(2)}) %collective-permute-start) | collective-permute-done | bytes 147488 | tf_op jit(solution)/shard_map/ppermute | solution.py:320
  20.3 0.0 collective-permute-done.1.far_taken_ref
  20.3 2.1 %shard_map.60 = (bf16[8,8,1024]{2,1,0:T(8,128)(2,1)S(1)}, bf16[1024,1024]{1,0:T(8,128)(2,1)S(1)}) custom-call(f32[72,512]{1,0:T(8,128)S(1)} %get-tuple-element.14.state_ref.refs_2_, f32[72,512]{1,0:T(8,128)S(1)} %collective-permute-done.state_taken_ref, bf16[512,2048]{1,0:T(8,128)(2,1)} %geno_ref.3, bf16[512,2048]{1,0:T(8,128)(2,1)} %collective-permute-done.1.far_taken_ref), custom_call_target="tpu_custom_call" | custom-call | flops 134217728 | bytes 2097152 | tf_op jit(solution)/shard_map/pallas_call | solution.py:323
  22.3 4.5 %all-to-all-done.refs_0_ = bf16[64,8,128]{2,1,0:T(8,128)(2,1)S(1)} async-done(((bf16[64,8,128]{2,1,0:T(8,128)(2,1)}), bf16[64,8,128]{2,1,0:T(8,128)(2,1)S(1)}, u32[]{:S(2)}, u32[]{:S(2)}) %all-to-all-start) | async-done | bytes 131104 | tf_op jit(solution)/shard_map/all_to_all | solution.py:316
  26.8 1.8 %shard_map.61 = (bf16[8,8,1152]{2,1,0:T(8,128)(2,1)}, bf16[2,64,512]{2,1,0:T(8,128)(2,1)S(1)}, bf16[2,64,512]{2,1,0:T(8,128)(2,1)}) custom-call(bf16[64,8,128]{2,1,0:T(8,128)(2,1)S(1)} %all-to-all-done.refs_0_, s32[2,64]{1,0:T(2,128)} %refs_1_.1, f32[72,512]{1,0:T(8,128)S(1)} %get-tuple-element.14.state_ref.refs_2_, ...), custom_call_target="tpu_custom_call" | custom-call | bytes 2097152 | tf_op jit(solution)/shard_map/pallas_call | solution.py:336
  28.6 12.4 %all-to-all-start.1 = ((bf16[8,8,1152]{2,1,0:T(8,128)(2,1)}), bf16[8,8,1152]{2,1,0:T(8,128)(2,1)S(1)}, u32[]{:S(2)}, u32[]{:S(2)}) async-start(bf16[8,8,1152]{2,1,0:T(8,128)(2,1)} %get-tuple-element.16), calls=%async_computation.1 | async-start | bytes 294912 | tf_op jit(solution)/shard_map/all_to_all | solution.py:347
  41.0 2.4 %collective-permute-start.2 = (bf16[2,64,512]{2,1,0:T(8,128)(2,1)}, bf16[2,64,512]{2,1,0:T(8,128)(2,1)S(1)}, u32[]{:S(2)}, u32[]{:S(2)}) collective-permute-start(bf16[2,64,512]{2,1,0:T(8,128)(2,1)} %get-tuple-element.18), channel_id=1, source_target_pairs={{0,64},{64,0},{128,192},{192,128},{256,320},{320,256},{384,448},{4... | collective-permute-start | bytes 393224 | tf_op jit(solution)/shard_map/ppermute | solution.py:348
  43.4 1.2 %collective-permute-done.2.picked_taken_ref = bf16[2,64,512]{2,1,0:T(8,128)(2,1)S(1)} collective-permute-done((bf16[2,64,512]{2,1,0:T(8,128)(2,1)}, bf16[2,64,512]{2,1,0:T(8,128)(2,1)S(1)}, u32[]{:S(2)}, u32[]{:S(2)}) %collective-permute-start.2) | collective-permute-done | bytes 131104 | tf_op jit(solution)/shard_map/ppermute | solution.py:348
  44.6 14.0 %all-to-all-done.1.shared_ref = bf16[8,8,1152]{2,1,0:T(8,128)(2,1)S(1)} async-done(((bf16[8,8,1152]{2,1,0:T(8,128)(2,1)}), bf16[8,8,1152]{2,1,0:T(8,128)(2,1)S(1)}, u32[]{:S(2)}, u32[]{:S(2)}) %all-to-all-start.1) | async-done | bytes 147488 | tf_op jit(solution)/shard_map/all_to_all | solution.py:347
  58.6 1.4 %shard_map.62 = (bf16[8,8,1152]{2,1,0:T(8,128)(2,1)}, f32[64,128]{1,0:T(8,128)S(1)}) custom-call(bf16[8,8,1152]{2,1,0:T(8,128)(2,1)S(1)} %all-to-all-done.1.shared_ref, f32[72,512]{1,0:T(8,128)S(1)} %get-tuple-element.14.state_ref.refs_2_, f32[72,512]{1,0:T(8,128)S(1)} %collective-permute-done.state_taken_ref, ...), custom_call_target="tpu_custom_call" | custom-call | flops 134217728 | bytes 2097152 | tf_op jit(solution)/shard_map/pallas_call | solution.py:350
  60.0 3.4 %all-to-all-start.2 = ((bf16[8,8,1152]{2,1,0:T(8,128)(2,1)}), bf16[8,8,1152]{2,1,0:T(8,128)(2,1)S(1)}, u32[]{:S(2)}, u32[]{:S(2)}) async-start(bf16[8,8,1152]{2,1,0:T(8,128)(2,1)} %get-tuple-element.20), calls=%async_computation.2 | async-start | bytes 294912 | tf_op jit(solution)/shard_map/all_to_all | solution.py:358
  63.4 16.7 %all-to-all-done.2.shared_ref = bf16[8,8,1152]{2,1,0:T(8,128)(2,1)S(1)} async-done(((bf16[8,8,1152]{2,1,0:T(8,128)(2,1)}), bf16[8,8,1152]{2,1,0:T(8,128)(2,1)S(1)}, u32[]{:S(2)}, u32[]{:S(2)}) %all-to-all-start.2) | async-done | bytes 147488 | tf_op jit(solution)/shard_map/all_to_all | solution.py:358
  80.1 1.3 %shard_map.63 = (bf16[8,8,1024]{2,1,0:T(8,128)(2,1)}, f32[64,512]{1,0:T(8,128)}) custom-call(bf16[8,8,1152]{2,1,0:T(8,128)(2,1)S(1)} %all-to-all-done.2.shared_ref, f32[64,128]{1,0:T(8,128)S(1)} %get-tuple-element.21.coef_ref, f32[72,512]{1,0:T(8,128)S(1)} %get-tuple-element.14.state_ref.refs_2_, f32[72,512]{1,0:T(8,128)S(1)} %collective-permute-done.state_taken_ref, ...), custom_call_target="tpu_custom_call" | custom-call | flops 134217728 | bytes 2097152 | tf_op jit(solution)/shard_map/pallas_call | solution.py:360
  81.4 3.4 %all-to-all-start.3 = ((bf16[8,8,1024]{2,1,0:T(8,128)(2,1)}), bf16[8,8,1024]{2,1,0:T(8,128)(2,1)S(1)}, u32[]{:S(2)}, u32[]{:S(2)}) async-start(bf16[8,8,1024]{2,1,0:T(8,128)(2,1)} %get-tuple-element.23), calls=%async_computation.3 | async-start | bytes 262144 | tf_op jit(solution)/shard_map/all_to_all | solution.py:368
  84.9 16.9 %all-to-all-done.3 = bf16[8,8,1024]{2,1,0:T(8,128)(2,1)S(1)} async-done(((bf16[8,8,1024]{2,1,0:T(8,128)(2,1)}), bf16[8,8,1024]{2,1,0:T(8,128)(2,1)S(1)}, u32[]{:S(2)}, u32[]{:S(2)}) %all-to-all-start.3) | async-done | bytes 131104 | tf_op jit(solution)/shard_map/all_to_all | solution.py:368
  101.9 0.7 pad_maximum_fusion
  (10 shorter events, 0.1 us)
Async XLA Ops:
  0.6 19.6 %collective-permute-start.1 = (bf16[512,2048]{1,0:T(8,128)(2,1)}, bf16[512,2048]{1,0:T(8,128)(2,1)}, u32[]{:S(2)}, u32[]{:S(2)}) collective-permute-start(bf16[512,2048]{1,0:T(8,128)(2,1)} %geno_ref.3), channel_id=1, source_target_pairs={{0,64},{64,0},{128,192},{192,128},{256,320},{320,256},{384,448},{4... | collective-permute-start | bytes 6291464 | tf_op jit(solution)/shard_map/ppermute | solution.py:318
  5.3 21.5 %all-to-all-start = ((bf16[64,8,128]{2,1,0:T(8,128)(2,1)}), bf16[64,8,128]{2,1,0:T(8,128)(2,1)S(1)}, u32[]{:S(2)}, u32[]{:S(2)}) async-start(bf16[64,8,128]{2,1,0:T(8,128)(2,1)} %get-tuple-element.13), calls=%async_computation | async-start | bytes 262144 | tf_op jit(solution)/shard_map/all_to_all | solution.py:316
  17.0 3.3 %collective-permute-start = (f32[72,512]{1,0:T(8,128)S(1)}, f32[72,512]{1,0:T(8,128)S(1)}, u32[]{:S(2)}, u32[]{:S(2)}) collective-permute-start(f32[72,512]{1,0:T(8,128)S(1)} %get-tuple-element.14.state_ref.refs_2_), channel_id=1, source_target_pairs={{0,64},{64,0},{128,192},{192,128},{256,320},{320,256},{384,448},{4... | collective-permute-start | bytes 442376 | tf_op jit(solution)/shard_map/ppermute | solution.py:320
  28.6 30.0 %all-to-all-start.1 = ((bf16[8,8,1152]{2,1,0:T(8,128)(2,1)}), bf16[8,8,1152]{2,1,0:T(8,128)(2,1)S(1)}, u32[]{:S(2)}, u32[]{:S(2)}) async-start(bf16[8,8,1152]{2,1,0:T(8,128)(2,1)} %get-tuple-element.16), calls=%async_computation.1 | async-start | bytes 294912 | tf_op jit(solution)/shard_map/all_to_all | solution.py:347
  41.0 3.6 %collective-permute-start.2 = (bf16[2,64,512]{2,1,0:T(8,128)(2,1)}, bf16[2,64,512]{2,1,0:T(8,128)(2,1)S(1)}, u32[]{:S(2)}, u32[]{:S(2)}) collective-permute-start(bf16[2,64,512]{2,1,0:T(8,128)(2,1)} %get-tuple-element.18), channel_id=1, source_target_pairs={{0,64},{64,0},{128,192},{192,128},{256,320},{320,256},{384,448},{4... | collective-permute-start | bytes 393224 | tf_op jit(solution)/shard_map/ppermute | solution.py:348
  60.0 20.1 %all-to-all-start.2 = ((bf16[8,8,1152]{2,1,0:T(8,128)(2,1)}), bf16[8,8,1152]{2,1,0:T(8,128)(2,1)S(1)}, u32[]{:S(2)}, u32[]{:S(2)}) async-start(bf16[8,8,1152]{2,1,0:T(8,128)(2,1)} %get-tuple-element.20), calls=%async_computation.2 | async-start | bytes 294912 | tf_op jit(solution)/shard_map/all_to_all | solution.py:358
  81.4 20.4 %all-to-all-start.3 = ((bf16[8,8,1024]{2,1,0:T(8,128)(2,1)}), bf16[8,8,1024]{2,1,0:T(8,128)(2,1)S(1)}, u32[]{:S(2)}, u32[]{:S(2)}) async-start(bf16[8,8,1024]{2,1,0:T(8,128)(2,1)} %get-tuple-element.23), calls=%async_computation.3 | async-start | bytes 262144 | tf_op jit(solution)/shard_map/all_to_all | solution.py:368

commit v9 on v8

--- a/solution.py
+++ b/solution.py
@@ -78,17 +78,14 @@
 
 
 def pick_body(
-    far_win_ref, geno_ref, margin_ref, far_labels_ref, out_ref, state_ref, block_ref, win_ref,
-    labels_ref, sem_ref,
+    win_ref, geno_ref, margin_ref, far_labels_ref, out_ref, state_ref, block_ref, labels_ref,
+    sem_ref,
 ):
     samples, columns = geno_ref.shape
-    wins = pltpu.make_async_copy(far_win_ref, win_ref, sem_ref.at[ITERS + 1])
-    wins.start()
-    marks = pltpu.make_async_copy(far_labels_ref, labels_ref, sem_ref.at[ITERS + 2])
+    marks = pltpu.make_async_copy(far_labels_ref, labels_ref, sem_ref.at[1])
     marks.start()
-    margins = pltpu.make_async_copy(margin_ref, state_ref.at[pl.ds(0, K)], sem_ref.at[ITERS])
+    margins = pltpu.make_async_copy(margin_ref, state_ref.at[pl.ds(0, K)], sem_ref.at[0])
     margins.start()
-    wins.wait()
     local = win_ref[...] - lax.axis_index("feat") * columns
     mine = jnp.where((local >= 0) & (local < columns), local, 0).astype(f32)
     copies, lanes = [], []
@@ -96,7 +93,7 @@
         col = jnp.sum(mine[step : step + 1]).astype(i32)
         start = pl.multiple_of((col // LANES) * LANES, LANES)
         copy = pltpu.make_async_copy(
-            geno_ref.at[:, pl.ds(start, LANES)], block_ref.at[step], sem_ref.at[step]
+            geno_ref.at[:, pl.ds(start, LANES)], block_ref.at[step], sem_ref.at[2 + step]
         )
         copy.start()
         copies.append(copy)
@@ -195,9 +192,17 @@
 
 
 def first_table_body(
-    state_ref, state_taken_ref, geno_ref, far_taken_ref, out_ref, both_ref, sem_ref
-):
+    state_ref, state_taken_ref, geno_ref, far_taken_ref, far_win_ref, out_ref, both_ref,
+    place_ref, win_ref, sem_ref,
+):
+    wins = pltpu.make_async_copy(far_win_ref, win_ref, sem_ref.at[2])
+    wins.start()
     copies = load_halves(geno_ref, far_taken_ref, both_ref, sem_ref)
+    feat = lax.broadcasted_iota(i32, place_ref.shape[1:], 0)
+    wins.wait()
+    for step in range(ITERS):
+        owner = win_ref[step : step + 1] // geno_ref.shape[1]
+        place_ref[step] = jnp.where(feat == owner, 1.0, 0.0).astype(bf16)
     resid, _ = residuals(state_ref[:K], state_ref[K : K + 1])
     resid_taken, _ = residuals(state_taken_ref[:K], state_taken_ref[K : K + 1])
     wait_all(copies)
@@ -206,24 +211,19 @@
 
 
 def first_sums_body(
-    cols_ref, far_win_ref, state_ref, table_ref, out_ref, picked_ref, far_picked_ref, tiles_ref,
-    win_ref, sem_ref, *, columns,
+    cols_ref, place_ref, state_ref, table_ref, out_ref, picked_ref, far_picked_ref, tiles_ref,
+    sem_ref,
 ):
     half = table_ref.shape[2]
     blocks = state_ref.shape[1] // LANES
     first = pltpu.make_async_copy(
         table_ref, out_ref.at[:, :, pl.ds(0, half)], sem_ref.at[0]
     )
-    wins = pltpu.make_async_copy(far_win_ref, win_ref, sem_ref.at[2])
-    wins.start()
     first.start()
     resid, prob = residuals(state_ref[:K], state_ref[K : K + 1])
     cols = cols_ref[...].astype(f32)
-    feat = lax.broadcasted_iota(i32, (cols.shape[0], K), 0)
-    wins.wait()
     for step in range(ITERS):
-        owner = win_ref[step : step + 1] // columns
-        place = jnp.where(feat == owner, 1.0, 0.0).astype(bf16)
+        place = place_ref[step]
         for j in range(blocks):
             piece = cols[:, step * blocks + j, :].astype(bf16)
             picked = lax.dot_general(
@@ -304,15 +304,14 @@
             pltpu.VMEM((feat_count, ITERS * samples // LANES, LANES), bf16),
             pltpu.VMEM((K + 8, samples), f32),
         ),
-        [HBM] * 4,
+        [VMEM, HBM, HBM, HBM],
         [
             pltpu.VMEM((ITERS, samples, LANES), bf16),
-            pltpu.VMEM((ITERS, K), i32),
             pltpu.VMEM((1, samples), i32),
-            sems((ITERS + 3,)),
+            sems((2 + ITERS,)),
         ],
         moved=samples * LANES * 4,
-    )(far(winners), far(genotypes), far(base_margin.T), far(labels[None, :]))
+    )(near(winners), far(genotypes), far(base_margin.T), far(labels[None, :]))
     cols = lax.all_to_all(sent, "feat", 0, 0, tiled=True)
 
     taken = far(lax.ppermute(genotypes, "rows", partners))
@@ -320,30 +319,31 @@
     state_taken = near(lax.ppermute(state, "rows", partners))
     state = near(state)
 
-    table, both = call(
+    table, both, place = call(
         first_table_body,
-        (pltpu.VMEM(table_shape, bf16), pltpu.VMEM((2 * samples, half), bf16)),
-        [VMEM, VMEM, HBM, HBM],
-        [sems((2,))],
+        (
+            pltpu.VMEM(table_shape, bf16),
+            pltpu.VMEM((2 * samples, half), bf16),
+            pltpu.VMEM((ITERS, feat_count, K), bf16),
+        ),
+        [VMEM, VMEM, HBM, HBM, HBM],
+        [pltpu.VMEM((ITERS, K), i32), sems((3,))],
         flops=work,
         moved=4 * samples * half,
-    )(state, state_taken, geno, taken)
-
-    def first_sums(*refs):
-        first_sums_body(*refs, columns=columns)
+    )(state, state_taken, geno, taken, far(winners))
 
     picked_shape = (ITERS, K, samples)
     payload, picked, far_picked = call(
-        first_sums,
+        first_sums_body,
         (
             pltpu.HBM(payload_shape, bf16),
             pltpu.VMEM(picked_shape, bf16),
             pltpu.HBM(picked_shape, bf16),
         ),
-        [VMEM, HBM, VMEM, VMEM],
-        [tiles, pltpu.VMEM((ITERS, K), i32), sems((4,))],
+        [VMEM] * 4,
+        [tiles, sems((4,))],
         moved=4 * samples * half,
-    )(near(cols), far(winners), state, table)
+    )(near(cols), place, state, table)
     shared0 = lax.all_to_all(payload, "rows", 0, 0, tiled=True)
     picked_taken = near(lax.ppermute(far_picked, "rows", partners))
 

time: 103 us -> 102 us (level)
  Pallas kernels: 9.28 us -> 7.93 us
  transfers between devices with their start and end apart: 7 -> 7, of which waited for: 6 -> 6; matrix products, arithmetic and copies ran while one was open for 0% -> 0% of each run, Pallas kernels for 5% -> 4%
where the time goes in v9:
time: 102 us
  waiting for transfers between devices  54.6 us (54%)
  starting transfers between devices  37.1 us (36%)
  Pallas kernels  7.93 us (8%)
    all_to_all x1, waiting for transfers between devices, shards(): shared2 = lax.all_to_all(payload, 'rows', 0, 0, tiled=True)  16.9 us
    all_to_all x1, waiting for transfers between devices, shards(): shared1 = lax.all_to_all(payload, 'rows', 0, 0, tiled=True)  16.7 us
    all_to_all x1, waiting for transfers between devices, shards(): shared0 = lax.all_to_all(payload, 'rows', 0, 0, tiled=True)  14 us
    all_to_all x1, starting transfers between devices, shards(): shared0 = lax.all_to_all(payload, 'rows', 0, 0, tiled=True)  12.4 us
    all_to_all x1, starting transfers between devices, shards(): cols = lax.all_to_all(sent, 'feat', 0, 0, tiled=True)  11.7 us
    all_to_all x1, waiting for transfers between devices, shards(): cols = lax.all_to_all(sent, 'feat', 0, 0, tiled=True)  4.46 us
    all_to_all x1, starting transfers between devices, shards(): shared1 = lax.all_to_all(payload, 'rows', 0, 0, tiled=True)  3.39 us
    all_to_all x1, starting transfers between devices, shards(): shared2 = lax.all_to_all(payload, 'rows', 0, 0, tiled=True)  3.38 us
  transfers between devices with their start and end apart: 7, of which 6 were waited for; matrix products, arithmetic and copies ran while one was open for 0% of the time, Pallas kernels for 4%

profile of v9, /device:TPU:32, one launch (start us, length us, event | category | flops | bytes accessed | tf_op | source)
XLA Modules:
  0.0 101.9 jit_solution(3405000448354311765)
XLA Ops:
  0.6 1.9 %collective-permute-start.1 = (bf16[512,2048]{1,0:T(8,128)(2,1)}, bf16[512,2048]{1,0:T(8,128)(2,1)}, u32[]{:S(2)}, u32[]{:S(2)}) collective-permute-start(bf16[512,2048]{1,0:T(8,128)(2,1)} %geno_ref.3), channel_id=1, source_target_pairs={{0,64},{64,0},{128,192},{192,128},{256,320},{320,256},{384,448},{4... | collective-permute-start | bytes 6291464 | tf_op jit(solution)/shard_map/ppermute | solution.py:317
  2.6 0.0 copy-start
  2.6 0.7 copy-done
  3.2 2.1 %shard_map.59 = (bf16[64,8,128]{2,1,0:T(8,128)(2,1)}, f32[72,512]{1,0:T(8,128)S(1)}) custom-call(s32[2,64]{1,0:T(2,128)S(1)} %copy-done, bf16[512,2048]{1,0:T(8,128)(2,1)} %geno_ref.3, f32[64,512]{1,0:T(8,128)} %bitcast.30, s32[1,512]{1,0:T(1,128)} %bitcast.31), custom_call_target="tpu_custom_call" | custom-call | bytes 262144 | tf_op jit(solution)/shard_map/pallas_call | solution.py:301
  5.3 11.7 %all-to-all-start = ((bf16[64,8,128]{2,1,0:T(8,128)(2,1)}), bf16[64,8,128]{2,1,0:T(8,128)(2,1)S(1)}, u32[]{:S(2)}, u32[]{:S(2)}) async-start(bf16[64,8,128]{2,1,0:T(8,128)(2,1)} %get-tuple-element.14), calls=%async_computation | async-start | bytes 262144 | tf_op jit(solution)/shard_map/all_to_all | solution.py:315
  17.0 1.9 %collective-permute-start = (f32[72,512]{1,0:T(8,128)S(1)}, f32[72,512]{1,0:T(8,128)S(1)}, u32[]{:S(2)}, u32[]{:S(2)}) collective-permute-start(f32[72,512]{1,0:T(8,128)S(1)} %get-tuple-element.15.state_ref), channel_id=1, source_target_pairs={{0,64},{64,0},{128,192},{192,128},{256,320},{320,256},{384,448},{4... | collective-permute-start | bytes 442376 | tf_op jit(solution)/shard_map/ppermute | solution.py:319
  18.9 1.3 %collective-permute-done.state_taken_ref = f32[72,512]{1,0:T(8,128)S(1)} collective-permute-done((f32[72,512]{1,0:T(8,128)S(1)}, f32[72,512]{1,0:T(8,128)S(1)}, u32[]{:S(2)}, u32[]{:S(2)}) %collective-permute-start) | collective-permute-done | bytes 147488 | tf_op jit(solution)/shard_map/ppermute | solution.py:319
  20.3 0.0 collective-permute-done.1.far_taken_ref
  20.3 2.1 %shard_map.60 = (bf16[8,8,1024]{2,1,0:T(8,128)(2,1)S(1)}, bf16[1024,1024]{1,0:T(8,128)(2,1)S(1)}, bf16[2,64,64]{2,1,0:T(8,128)(2,1)S(1)}) custom-call(f32[72,512]{1,0:T(8,128)S(1)} %get-tuple-element.15.state_ref, f32[72,512]{1,0:T(8,128)S(1)} %collective-permute-done.state_taken_ref, bf16[512,2048]{1,0:T(8,128)(2,1)} %geno_ref.3, ...), custom_call_target="tpu_custom_call" | custom-call | flops 134217728 | bytes 2097152 | tf_op jit(solution)/shard_map/pallas_call | solution.py:322
  22.3 4.5 %all-to-all-done.cols_ref = bf16[64,8,128]{2,1,0:T(8,128)(2,1)S(1)} async-done(((bf16[64,8,128]{2,1,0:T(8,128)(2,1)}), bf16[64,8,128]{2,1,0:T(8,128)(2,1)S(1)}, u32[]{:S(2)}, u32[]{:S(2)}) %all-to-all-start) | async-done | bytes 131104 | tf_op jit(solution)/shard_map/all_to_all | solution.py:315
  26.8 1.1 %shard_map.61 = (bf16[8,8,1152]{2,1,0:T(8,128)(2,1)}, bf16[2,64,512]{2,1,0:T(8,128)(2,1)S(1)}, bf16[2,64,512]{2,1,0:T(8,128)(2,1)}) custom-call(bf16[64,8,128]{2,1,0:T(8,128)(2,1)S(1)} %all-to-all-done.cols_ref, bf16[2,64,64]{2,1,0:T(8,128)(2,1)S(1)} %get-tuple-element.16.place_ref, f32[72,512]{1,0:T(8,128)S(1)} %get-tuple-element.15.state_ref, ...), custom_call_target="tpu_custom_call" | custom-call | bytes 2097152 | tf_op jit(solution)/shard_map/pallas_call | solution.py:336
  27.9 12.4 %all-to-all-start.1 = ((bf16[8,8,1152]{2,1,0:T(8,128)(2,1)}), bf16[8,8,1152]{2,1,0:T(8,128)(2,1)S(1)}, u32[]{:S(2)}, u32[]{:S(2)}) async-start(bf16[8,8,1152]{2,1,0:T(8,128)(2,1)} %get-tuple-element.18), calls=%async_computation.1 | async-start | bytes 294912 | tf_op jit(solution)/shard_map/all_to_all | solution.py:347
  40.3 2.4 %collective-permute-start.2 = (bf16[2,64,512]{2,1,0:T(8,128)(2,1)}, bf16[2,64,512]{2,1,0:T(8,128)(2,1)S(1)}, u32[]{:S(2)}, u32[]{:S(2)}) collective-permute-start(bf16[2,64,512]{2,1,0:T(8,128)(2,1)} %get-tuple-element.20), channel_id=1, source_target_pairs={{0,64},{64,0},{128,192},{192,128},{256,320},{320,256},{384,448},{4... | collective-permute-start | bytes 393224 | tf_op jit(solution)/shard_map/ppermute | solution.py:348
  42.7 1.2 %collective-permute-done.2.picked_taken_ref = bf16[2,64,512]{2,1,0:T(8,128)(2,1)S(1)} collective-permute-done((bf16[2,64,512]{2,1,0:T(8,128)(2,1)}, bf16[2,64,512]{2,1,0:T(8,128)(2,1)S(1)}, u32[]{:S(2)}, u32[]{:S(2)}) %collective-permute-start.2) | collective-permute-done | bytes 131104 | tf_op jit(solution)/shard_map/ppermute | solution.py:348
  43.9 14.0 %all-to-all-done.1.shared_ref = bf16[8,8,1152]{2,1,0:T(8,128)(2,1)S(1)} async-done(((bf16[8,8,1152]{2,1,0:T(8,128)(2,1)}), bf16[8,8,1152]{2,1,0:T(8,128)(2,1)S(1)}, u32[]{:S(2)}, u32[]{:S(2)}) %all-to-all-start.1) | async-done | bytes 147488 | tf_op jit(solution)/shard_map/all_to_all | solution.py:347
  57.9 1.4 %shard_map.62 = (bf16[8,8,1152]{2,1,0:T(8,128)(2,1)}, f32[64,128]{1,0:T(8,128)S(1)}) custom-call(bf16[8,8,1152]{2,1,0:T(8,128)(2,1)S(1)} %all-to-all-done.1.shared_ref, f32[72,512]{1,0:T(8,128)S(1)} %get-tuple-element.15.state_ref, f32[72,512]{1,0:T(8,128)S(1)} %collective-permute-done.state_taken_ref, bf16[2,64,512]{2,1,0:T(8,128)(2,1)S(1)} %get-tuple-element.19.picked_ref, ...), custom_call_target="tpu_custom_call" | custom-call | flops 134217728 | bytes 2097152 | tf_op jit(solution)/shard_map/pallas_call | solution.py:350
  59.3 3.4 %all-to-all-start.2 = ((bf16[8,8,1152]{2,1,0:T(8,128)(2,1)}), bf16[8,8,1152]{2,1,0:T(8,128)(2,1)S(1)}, u32[]{:S(2)}, u32[]{:S(2)}) async-start(bf16[8,8,1152]{2,1,0:T(8,128)(2,1)} %get-tuple-element.22), calls=%async_computation.2 | async-start | bytes 294912 | tf_op jit(solution)/shard_map/all_to_all | solution.py:358
  62.7 16.7 %all-to-all-done.2.shared_ref = bf16[8,8,1152]{2,1,0:T(8,128)(2,1)S(1)} async-done(((bf16[8,8,1152]{2,1,0:T(8,128)(2,1)}), bf16[8,8,1152]{2,1,0:T(8,128)(2,1)S(1)}, u32[]{:S(2)}, u32[]{:S(2)}) %all-to-all-start.2) | async-done | bytes 147488 | tf_op jit(solution)/shard_map/all_to_all | solution.py:358
  79.4 1.3 %shard_map.63 = (bf16[8,8,1024]{2,1,0:T(8,128)(2,1)}, f32[64,512]{1,0:T(8,128)}) custom-call(bf16[8,8,1152]{2,1,0:T(8,128)(2,1)S(1)} %all-to-all-done.2.shared_ref, f32[64,128]{1,0:T(8,128)S(1)} %get-tuple-element.23.coef_ref, f32[72,512]{1,0:T(8,128)S(1)} %get-tuple-element.15.state_ref, f32[72,512]{1,0:T(8,128)S(1)} %collective-permute-done.state_taken_ref, ...), custom_call_target="tpu_custom_call" | custom-call | flops 134217728 | bytes 2097152 | tf_op jit(solution)/shard_map/pallas_call | solution.py:360
  80.8 3.4 %all-to-all-start.3 = ((bf16[8,8,1024]{2,1,0:T(8,128)(2,1)}), bf16[8,8,1024]{2,1,0:T(8,128)(2,1)S(1)}, u32[]{:S(2)}, u32[]{:S(2)}) async-start(bf16[8,8,1024]{2,1,0:T(8,128)(2,1)} %get-tuple-element.25), calls=%async_computation.3 | async-start | bytes 262144 | tf_op jit(solution)/shard_map/all_to_all | solution.py:368
  84.2 16.9 %all-to-all-done.3 = bf16[8,8,1024]{2,1,0:T(8,128)(2,1)S(1)} async-done(((bf16[8,8,1024]{2,1,0:T(8,128)(2,1)}), bf16[8,8,1024]{2,1,0:T(8,128)(2,1)S(1)}, u32[]{:S(2)}, u32[]{:S(2)}) %all-to-all-start.3) | async-done | bytes 131104 | tf_op jit(solution)/shard_map/all_to_all | solution.py:368
  101.2 0.7 pad_maximum_fusion
  (10 shorter events, 0.1 us)
Async XLA Ops:
  0.6 19.6 %collective-permute-start.1 = (bf16[512,2048]{1,0:T(8,128)(2,1)}, bf16[512,2048]{1,0:T(8,128)(2,1)}, u32[]{:S(2)}, u32[]{:S(2)}) collective-permute-start(bf16[512,2048]{1,0:T(8,128)(2,1)} %geno_ref.3), channel_id=1, source_target_pairs={{0,64},{64,0},{128,192},{192,128},{256,320},{320,256},{384,448},{4... | collective-permute-start | bytes 6291464 | tf_op jit(solution)/shard_map/ppermute | solution.py:317
  2.6 0.7 copy-start
  5.3 21.5 %all-to-all-start = ((bf16[64,8,128]{2,1,0:T(8,128)(2,1)}), bf16[64,8,128]{2,1,0:T(8,128)(2,1)S(1)}, u32[]{:S(2)}, u32[]{:S(2)}) async-start(bf16[64,8,128]{2,1,0:T(8,128)(2,1)} %get-tuple-element.14), calls=%async_computation | async-start | bytes 262144 | tf_op jit(solution)/shard_map/all_to_all | solution.py:315
  17.0 3.3 %collective-permute-start = (f32[72,512]{1,0:T(8,128)S(1)}, f32[72,512]{1,0:T(8,128)S(1)}, u32[]{:S(2)}, u32[]{:S(2)}) collective-permute-start(f32[72,512]{1,0:T(8,128)S(1)} %get-tuple-element.15.state_ref), channel_id=1, source_target_pairs={{0,64},{64,0},{128,192},{192,128},{256,320},{320,256},{384,448},{4... | collective-permute-start | bytes 442376 | tf_op jit(solution)/shard_map/ppermute | solution.py:319
  27.9 30.0 %all-to-all-start.1 = ((bf16[8,8,1152]{2,1,0:T(8,128)(2,1)}), bf16[8,8,1152]{2,1,0:T(8,128)(2,1)S(1)}, u32[]{:S(2)}, u32[]{:S(2)}) async-start(bf16[8,8,1152]{2,1,0:T(8,128)(2,1)} %get-tuple-element.18), calls=%async_computation.1 | async-start | bytes 294912 | tf_op jit(solution)/shard_map/all_to_all | solution.py:347
  40.3 3.6 %collective-permute-start.2 = (bf16[2,64,512]{2,1,0:T(8,128)(2,1)}, bf16[2,64,512]{2,1,0:T(8,128)(2,1)S(1)}, u32[]{:S(2)}, u32[]{:S(2)}) collective-permute-start(bf16[2,64,512]{2,1,0:T(8,128)(2,1)} %get-tuple-element.20), channel_id=1, source_target_pairs={{0,64},{64,0},{128,192},{192,128},{256,320},{320,256},{384,448},{4... | collective-permute-start | bytes 393224 | tf_op jit(solution)/shard_map/ppermute | solution.py:348
  59.3 20.1 %all-to-all-start.2 = ((bf16[8,8,1152]{2,1,0:T(8,128)(2,1)}), bf16[8,8,1152]{2,1,0:T(8,128)(2,1)S(1)}, u32[]{:S(2)}, u32[]{:S(2)}) async-start(bf16[8,8,1152]{2,1,0:T(8,128)(2,1)} %get-tuple-element.22), calls=%async_computation.2 | async-start | bytes 294912 | tf_op jit(solution)/shard_map/all_to_all | solution.py:358
  80.8 20.4 %all-to-all-start.3 = ((bf16[8,8,1024]{2,1,0:T(8,128)(2,1)}), bf16[8,8,1024]{2,1,0:T(8,128)(2,1)S(1)}, u32[]{:S(2)}, u32[]{:S(2)}) async-start(bf16[8,8,1024]{2,1,0:T(8,128)(2,1)} %get-tuple-element.25), calls=%async_computation.3 | async-start | bytes 262144 | tf_op jit(solution)/shard_map/all_to_all | solution.py:368

commit v10 on v9

--- a/solution.py
+++ b/solution.py
@@ -191,22 +191,27 @@
     return copies
 
 
-def first_table_body(
-    state_ref, state_taken_ref, geno_ref, far_taken_ref, far_win_ref, out_ref, both_ref,
-    place_ref, win_ref, sem_ref,
+def own_table_body(
+    state_ref, geno_ref, far_taken_ref, far_win_ref, out_ref, both_ref, place_ref, win_ref, sem_ref
 ):
     wins = pltpu.make_async_copy(far_win_ref, win_ref, sem_ref.at[2])
     wins.start()
     copies = load_halves(geno_ref, far_taken_ref, both_ref, sem_ref)
+    resid, _ = residuals(state_ref[:K], state_ref[K : K + 1])
     feat = lax.broadcasted_iota(i32, place_ref.shape[1:], 0)
     wins.wait()
     for step in range(ITERS):
         owner = win_ref[step : step + 1] // geno_ref.shape[1]
         place_ref[step] = jnp.where(feat == owner, 1.0, 0.0).astype(bf16)
-    resid, _ = residuals(state_ref[:K], state_ref[K : K + 1])
+    copies[0].wait()
+    out_ref[...] = jnp.dot(resid, both_ref[: geno_ref.shape[0]], preferred_element_type=f32)
+    copies[1].wait()
+
+
+def pair_table_body(own_ref, state_taken_ref, both_ref, out_ref):
+    samples = state_taken_ref.shape[1]
     resid_taken, _ = residuals(state_taken_ref[:K], state_taken_ref[K : K + 1])
-    wait_all(copies)
-    table = half_table(resid, resid_taken, both_ref, 0, out_ref.shape[2])
+    table = own_ref[...] + jnp.dot(resid_taken, both_ref[samples:], preferred_element_type=f32)
     out_ref[...] = table.reshape(out_ref.shape).astype(bf16)
 
 
@@ -319,18 +324,25 @@
     state_taken = near(lax.ppermute(state, "rows", partners))
     state = near(state)
 
-    table, both, place = call(
-        first_table_body,
+    own, both, place = call(
+        own_table_body,
         (
-            pltpu.VMEM(table_shape, bf16),
+            pltpu.VMEM((K, half), f32),
             pltpu.VMEM((2 * samples, half), bf16),
             pltpu.VMEM((ITERS, feat_count, K), bf16),
         ),
-        [VMEM, VMEM, HBM, HBM, HBM],
+        [VMEM, HBM, HBM, HBM],
         [pltpu.VMEM((ITERS, K), i32), sems((3,))],
-        flops=work,
+        flops=work // 2,
         moved=4 * samples * half,
-    )(state, state_taken, geno, taken, far(winners))
+    )(state, geno, taken, far(winners))
+    table = call(
+        pair_table_body,
+        pltpu.VMEM(table_shape, bf16),
+        [VMEM] * 3,
+        flops=work // 2,
+        moved=2 * samples * half,
+    )(own, state_taken, both)
 
     picked_shape = (ITERS, K, samples)
     payload, picked, far_picked = call(

time: 102 us -> 102 us (level)
    all_to_all x1, waiting for transfers between devices: 4.46 us -> 5.92 us  [shards(): cols = lax.all_to_all(sent, 'feat', 0, 0, tiled=True)]
    ppermute x1, waiting for transfers between devices: 1.34 us -> 0.01 us  [shards(): state_taken = near(lax.ppermute(state, 'rows', partners))]
    pallas_call x1 -> x2, Pallas kernels: 2.06 us -> 1.91 us  [the longest x1 1.59 us: shards(): call(own_table_body, (pltpu.VMEM((K, half), f32), pltpu.VMEM((2 * samples...]
  transfers between devices with their start and end apart: 7 -> 7, of which waited for: 6 -> 5; matrix products, arithmetic and copies ran while one was open for 0% -> 0% of each run, Pallas kernels for 4% -> 4%
where the time goes in v10:
time: 102 us
  waiting for transfers between devices  54.7 us (54%)
  starting transfers between devices  37.1 us (36%)
  Pallas kernels  7.77 us (8%)
    all_to_all x1, waiting for transfers between devices, shards(): shared2 = lax.all_to_all(payload, 'rows', 0, 0, tiled=True)  16.9 us
    all_to_all x1, waiting for transfers between devices, shards(): shared1 = lax.all_to_all(payload, 'rows', 0, 0, tiled=True)  16.7 us
    all_to_all x1, waiting for transfers between devices, shards(): shared0 = lax.all_to_all(payload, 'rows', 0, 0, tiled=True)  14 us
    all_to_all x1, starting transfers between devices, shards(): shared0 = lax.all_to_all(payload, 'rows', 0, 0, tiled=True)  12.4 us
    all_to_all x1, starting transfers between devices, shards(): cols = lax.all_to_all(sent, 'feat', 0, 0, tiled=True)  11.7 us
    all_to_all x1, waiting for transfers between devices, shards(): cols = lax.all_to_all(sent, 'feat', 0, 0, tiled=True)  5.92 us
    all_to_all x1, starting transfers between devices, shards(): shared1 = lax.all_to_all(payload, 'rows', 0, 0, tiled=True)  3.39 us
    all_to_all x1, starting transfers between devices, shards(): shared2 = lax.all_to_all(payload, 'rows', 0, 0, tiled=True)  3.38 us
  transfers between devices with their start and end apart: 7, of which 5 were waited for; matrix products, arithmetic and copies ran while one was open for 0% of the time, Pallas kernels for 4%

profile of v10, /device:TPU:32, one launch (start us, length us, event | category | flops | bytes accessed | tf_op | source)
XLA Modules:
  0.0 101.9 jit_solution(9642414182406031046)
XLA Ops:
  0.6 1.9 %collective-permute-start = (bf16[512,2048]{1,0:T(8,128)(2,1)}, bf16[512,2048]{1,0:T(8,128)(2,1)}, u32[]{:S(2)}, u32[]{:S(2)}) collective-permute-start(bf16[512,2048]{1,0:T(8,128)(2,1)} %geno_ref.3), channel_id=1, source_target_pairs={{0,64},{64,0},{128,192},{192,128},{256,320},{320,256},{384,448},{4... | collective-permute-start | bytes 6291464 | tf_op jit(solution)/shard_map/ppermute | solution.py:322
  2.6 0.0 copy-start
  2.6 0.7 copy-done
  3.2 2.1 %shard_map.59 = (bf16[64,8,128]{2,1,0:T(8,128)(2,1)}, f32[72,512]{1,0:T(8,128)S(1)}) custom-call(s32[2,64]{1,0:T(2,128)S(1)} %copy-done, bf16[512,2048]{1,0:T(8,128)(2,1)} %geno_ref.3, f32[64,512]{1,0:T(8,128)} %bitcast.30, s32[1,512]{1,0:T(1,128)} %bitcast.31), custom_call_target="tpu_custom_call" | custom-call | bytes 262144 | tf_op jit(solution)/shard_map/pallas_call | solution.py:306
  5.3 11.7 %all-to-all-start = ((bf16[64,8,128]{2,1,0:T(8,128)(2,1)}), bf16[64,8,128]{2,1,0:T(8,128)(2,1)S(1)}, u32[]{:S(2)}, u32[]{:S(2)}) async-start(bf16[64,8,128]{2,1,0:T(8,128)(2,1)} %get-tuple-element.14), calls=%async_computation | async-start | bytes 262144 | tf_op jit(solution)/shard_map/all_to_all | solution.py:320
  17.0 1.9 %collective-permute-start.1 = (f32[72,512]{1,0:T(8,128)S(1)}, f32[72,512]{1,0:T(8,128)S(1)}, u32[]{:S(2)}, u32[]{:S(2)}) collective-permute-start(f32[72,512]{1,0:T(8,128)S(1)} %get-tuple-element.15.state_ref), channel_id=1, source_target_pairs={{0,64},{64,0},{128,192},{192,128},{256,320},{320,256},{384,448},{4... | collective-permute-start | bytes 442376 | tf_op jit(solution)/shard_map/ppermute | solution.py:324
  18.9 0.0 collective-permute-done.far_taken_ref
  18.9 1.6 %shard_map.60 = (f32[64,1024]{1,0:T(8,128)S(1)}, bf16[1024,1024]{1,0:T(8,128)(2,1)S(1)}, bf16[2,64,64]{2,1,0:T(8,128)(2,1)S(1)}) custom-call(f32[72,512]{1,0:T(8,128)S(1)} %get-tuple-element.15.state_ref, bf16[512,2048]{1,0:T(8,128)(2,1)} %geno_ref.3, bf16[512,2048]{1,0:T(8,128)(2,1)} %collective-permute-done.far_taken_ref, s32[2,64]{1,0:T(2,128)} %far_win_ref.1), custom_call_target="tpu_custom_call" | custom-call | flops 67108864 | bytes 2097152 | tf_op jit(solution)/shard_map/pallas_call | solution.py:327
  20.5 0.0 collective-permute-done.1.state_taken_ref
  20.5 0.3 shard_map.61.table_ref
  20.9 5.9 %all-to-all-done.cols_ref = bf16[64,8,128]{2,1,0:T(8,128)(2,1)S(1)} async-done(((bf16[64,8,128]{2,1,0:T(8,128)(2,1)}), bf16[64,8,128]{2,1,0:T(8,128)(2,1)S(1)}, u32[]{:S(2)}, u32[]{:S(2)}) %all-to-all-start) | async-done | bytes 131104 | tf_op jit(solution)/shard_map/all_to_all | solution.py:320
  26.8 1.1 %shard_map.62 = (bf16[8,8,1152]{2,1,0:T(8,128)(2,1)}, bf16[2,64,512]{2,1,0:T(8,128)(2,1)S(1)}, bf16[2,64,512]{2,1,0:T(8,128)(2,1)}) custom-call(bf16[64,8,128]{2,1,0:T(8,128)(2,1)S(1)} %all-to-all-done.cols_ref, bf16[2,64,64]{2,1,0:T(8,128)(2,1)S(1)} %get-tuple-element.16.place_ref, f32[72,512]{1,0:T(8,128)S(1)} %get-tuple-element.15.state_ref, ...), custom_call_target="tpu_custom_call" | custom-call | bytes 2097152 | tf_op jit(solution)/shard_map/pallas_call | solution.py:348
  27.9 12.4 %all-to-all-start.1 = ((bf16[8,8,1152]{2,1,0:T(8,128)(2,1)}), bf16[8,8,1152]{2,1,0:T(8,128)(2,1)S(1)}, u32[]{:S(2)}, u32[]{:S(2)}) async-start(bf16[8,8,1152]{2,1,0:T(8,128)(2,1)} %get-tuple-element.19), calls=%async_computation.1 | async-start | bytes 294912 | tf_op jit(solution)/shard_map/all_to_all | solution.py:359
  40.3 2.4 %collective-permute-start.2 = (bf16[2,64,512]{2,1,0:T(8,128)(2,1)}, bf16[2,64,512]{2,1,0:T(8,128)(2,1)S(1)}, u32[]{:S(2)}, u32[]{:S(2)}) collective-permute-start(bf16[2,64,512]{2,1,0:T(8,128)(2,1)} %get-tuple-element.21), channel_id=1, source_target_pairs={{0,64},{64,0},{128,192},{192,128},{256,320},{320,256},{384,448},{4... | collective-permute-start | bytes 393224 | tf_op jit(solution)/shard_map/ppermute | solution.py:360
  42.7 1.2 %collective-permute-done.2.picked_taken_ref = bf16[2,64,512]{2,1,0:T(8,128)(2,1)S(1)} collective-permute-done((bf16[2,64,512]{2,1,0:T(8,128)(2,1)}, bf16[2,64,512]{2,1,0:T(8,128)(2,1)S(1)}, u32[]{:S(2)}, u32[]{:S(2)}) %collective-permute-start.2) | collective-permute-done | bytes 131104 | tf_op jit(solution)/shard_map/ppermute | solution.py:360
  43.9 14.0 %all-to-all-done.1.shared_ref = bf16[8,8,1152]{2,1,0:T(8,128)(2,1)S(1)} async-done(((bf16[8,8,1152]{2,1,0:T(8,128)(2,1)}), bf16[8,8,1152]{2,1,0:T(8,128)(2,1)S(1)}, u32[]{:S(2)}, u32[]{:S(2)}) %all-to-all-start.1) | async-done | bytes 147488 | tf_op jit(solution)/shard_map/all_to_all | solution.py:359
  57.9 1.4 %shard_map.63 = (bf16[8,8,1152]{2,1,0:T(8,128)(2,1)}, f32[64,128]{1,0:T(8,128)S(1)}) custom-call(bf16[8,8,1152]{2,1,0:T(8,128)(2,1)S(1)} %all-to-all-done.1.shared_ref, f32[72,512]{1,0:T(8,128)S(1)} %get-tuple-element.15.state_ref, f32[72,512]{1,0:T(8,128)S(1)} %collective-permute-done.1.state_taken_ref, ...), custom_call_target="tpu_custom_call" | custom-call | flops 134217728 | bytes 2097152 | tf_op jit(solution)/shard_map/pallas_call | solution.py:362
  59.3 3.4 %all-to-all-start.2 = ((bf16[8,8,1152]{2,1,0:T(8,128)(2,1)}), bf16[8,8,1152]{2,1,0:T(8,128)(2,1)S(1)}, u32[]{:S(2)}, u32[]{:S(2)}) async-start(bf16[8,8,1152]{2,1,0:T(8,128)(2,1)} %get-tuple-element.22), calls=%async_computation.2 | async-start | bytes 294912 | tf_op jit(solution)/shard_map/all_to_all | solution.py:370
  62.7 16.7 %all-to-all-done.2.shared_ref = bf16[8,8,1152]{2,1,0:T(8,128)(2,1)S(1)} async-done(((bf16[8,8,1152]{2,1,0:T(8,128)(2,1)}), bf16[8,8,1152]{2,1,0:T(8,128)(2,1)S(1)}, u32[]{:S(2)}, u32[]{:S(2)}) %all-to-all-start.2) | async-done | bytes 147488 | tf_op jit(solution)/shard_map/all_to_all | solution.py:370
  79.4 1.3 %shard_map.64 = (bf16[8,8,1024]{2,1,0:T(8,128)(2,1)}, f32[64,512]{1,0:T(8,128)}) custom-call(bf16[8,8,1152]{2,1,0:T(8,128)(2,1)S(1)} %all-to-all-done.2.shared_ref, f32[64,128]{1,0:T(8,128)S(1)} %get-tuple-element.23.coef_ref, f32[72,512]{1,0:T(8,128)S(1)} %get-tuple-element.15.state_ref, f32[72,512]{1,0:T(8,128)S(1)} %collective-permute-done.1.state_taken_ref, ...), custom_call_target="tpu_custom_call" | custom-call | flops 134217728 | bytes 2097152 | tf_op jit(solution)/shard_map/pallas_call | solution.py:372
  80.8 3.4 %all-to-all-start.3 = ((bf16[8,8,1024]{2,1,0:T(8,128)(2,1)}), bf16[8,8,1024]{2,1,0:T(8,128)(2,1)S(1)}, u32[]{:S(2)}, u32[]{:S(2)}) async-start(bf16[8,8,1024]{2,1,0:T(8,128)(2,1)} %get-tuple-element.25), calls=%async_computation.3 | async-start | bytes 262144 | tf_op jit(solution)/shard_map/all_to_all | solution.py:380
  84.2 16.9 %all-to-all-done.3 = bf16[8,8,1024]{2,1,0:T(8,128)(2,1)S(1)} async-done(((bf16[8,8,1024]{2,1,0:T(8,128)(2,1)}), bf16[8,8,1024]{2,1,0:T(8,128)(2,1)S(1)}, u32[]{:S(2)}, u32[]{:S(2)}) %all-to-all-start.3) | async-done | bytes 131104 | tf_op jit(solution)/shard_map/all_to_all | solution.py:380
  101.2 0.7 pad_maximum_fusion
  (10 shorter events, 0.1 us)
Async XLA Ops:
  0.6 18.3 %collective-permute-start = (bf16[512,2048]{1,0:T(8,128)(2,1)}, bf16[512,2048]{1,0:T(8,128)(2,1)}, u32[]{:S(2)}, u32[]{:S(2)}) collective-permute-start(bf16[512,2048]{1,0:T(8,128)(2,1)} %geno_ref.3), channel_id=1, source_target_pairs={{0,64},{64,0},{128,192},{192,128},{256,320},{320,256},{384,448},{4... | collective-permute-start | bytes 6291464 | tf_op jit(solution)/shard_map/ppermute | solution.py:322
  2.6 0.7 copy-start
  5.3 21.5 %all-to-all-start = ((bf16[64,8,128]{2,1,0:T(8,128)(2,1)}), bf16[64,8,128]{2,1,0:T(8,128)(2,1)S(1)}, u32[]{:S(2)}, u32[]{:S(2)}) async-start(bf16[64,8,128]{2,1,0:T(8,128)(2,1)} %get-tuple-element.14), calls=%async_computation | async-start | bytes 262144 | tf_op jit(solution)/shard_map/all_to_all | solution.py:320
  17.0 3.5 %collective-permute-start.1 = (f32[72,512]{1,0:T(8,128)S(1)}, f32[72,512]{1,0:T(8,128)S(1)}, u32[]{:S(2)}, u32[]{:S(2)}) collective-permute-start(f32[72,512]{1,0:T(8,128)S(1)} %get-tuple-element.15.state_ref), channel_id=1, source_target_pairs={{0,64},{64,0},{128,192},{192,128},{256,320},{320,256},{384,448},{4... | collective-permute-start | bytes 442376 | tf_op jit(solution)/shard_map/ppermute | solution.py:324
  27.9 30.0 %all-to-all-start.1 = ((bf16[8,8,1152]{2,1,0:T(8,128)(2,1)}), bf16[8,8,1152]{2,1,0:T(8,128)(2,1)S(1)}, u32[]{:S(2)}, u32[]{:S(2)}) async-start(bf16[8,8,1152]{2,1,0:T(8,128)(2,1)} %get-tuple-element.19), calls=%async_computation.1 | async-start | bytes 294912 | tf_op jit(solution)/shard_map/all_to_all | solution.py:359
  40.3 3.6 %collective-permute-start.2 = (bf16[2,64,512]{2,1,0:T(8,128)(2,1)}, bf16[2,64,512]{2,1,0:T(8,128)(2,1)S(1)}, u32[]{:S(2)}, u32[]{:S(2)}) collective-permute-start(bf16[2,64,512]{2,1,0:T(8,128)(2,1)} %get-tuple-element.21), channel_id=1, source_target_pairs={{0,64},{64,0},{128,192},{192,128},{256,320},{320,256},{384,448},{4... | collective-permute-start | bytes 393224 | tf_op jit(solution)/shard_map/ppermute | solution.py:360
  59.3 20.1 %all-to-all-start.2 = ((bf16[8,8,1152]{2,1,0:T(8,128)(2,1)}), bf16[8,8,1152]{2,1,0:T(8,128)(2,1)S(1)}, u32[]{:S(2)}, u32[]{:S(2)}) async-start(bf16[8,8,1152]{2,1,0:T(8,128)(2,1)} %get-tuple-element.22), calls=%async_computation.2 | async-start | bytes 294912 | tf_op jit(solution)/shard_map/all_to_all | solution.py:370
  80.8 20.4 %all-to-all-start.3 = ((bf16[8,8,1024]{2,1,0:T(8,128)(2,1)}), bf16[8,8,1024]{2,1,0:T(8,128)(2,1)S(1)}, u32[]{:S(2)}, u32[]{:S(2)}) async-start(bf16[8,8,1024]{2,1,0:T(8,128)(2,1)} %get-tuple-element.25), calls=%async_computation.3 | async-start | bytes 262144 | tf_op jit(solution)/shard_map/all_to_all | solution.py:380

commit v11 on v10

--- a/solution.py
+++ b/solution.py
@@ -133,11 +133,6 @@
     return copies
 
 
-def half_table(resid, resid_taken, both_ref, start, width):
-    whole = jnp.concatenate([resid, resid_taken], axis=1)
-    return jnp.dot(whole, both_ref[:, pl.ds(start, width)], preferred_element_type=f32)
-
-
 def sums_tile(resid, prob, picked):
     grad = resid.astype(f32) * picked
     curv = prob * (1.0 - prob) * picked * picked
@@ -168,27 +163,24 @@
     return jnp.concatenate([values] * count, axis=1)
 
 
-def send_tile(tile, both_ref, out_ref, sem_ref):
-    half = out_ref.shape[2] - 2 * K
-    both_ref[...] = jnp.broadcast_to(tile[None], both_ref.shape)
-    copy = pltpu.make_async_copy(both_ref, out_ref.at[:, :, pl.ds(half, 2 * K)], sem_ref)
-    copy.start()
-    return copy
-
-
-def send_table(resid, resid_taken, both_ref, table_ref, out_ref, sem_ref, pieces=2):
-    width = table_ref.shape[2] // pieces
-    copies = []
-    for piece in range(pieces):
-        span = pl.ds(piece * width, width)
-        table = half_table(resid, resid_taken, both_ref, piece * width, width)
-        table_ref[:, :, span] = table.reshape(table_ref.shape[0], -1, width).astype(bf16)
-        copy = pltpu.make_async_copy(
-            table_ref.at[:, :, span], out_ref.at[:, :, span], sem_ref.at[piece]
-        )
+def fill_tile(tile, tiles_ref):
+    tiles_ref[...] = jnp.broadcast_to(tile[None], tiles_ref.shape)
+
+
+def send(pairs, sem_ref):
+    copies = [
+        pltpu.make_async_copy(source, target, sem_ref.at[i])
+        for i, (source, target) in enumerate(pairs)
+    ]
+    for copy in copies:
         copy.start()
-        copies.append(copy)
-    return copies
+    wait_all(copies)
+
+
+def fill_table(resid, resid_taken, both_ref, table_ref):
+    whole = jnp.concatenate([resid, resid_taken], axis=1)
+    table = jnp.dot(whole, both_ref[...], preferred_element_type=f32)
+    table_ref[...] = table.reshape(table_ref.shape).astype(bf16)
 
 
 def own_table_body(
@@ -238,8 +230,9 @@
     third = pltpu.make_async_copy(picked_ref, far_picked_ref, sem_ref.at[3])
     third.start()
     tile = sums_tile(resid, prob, picked_ref[0].astype(f32))
-    second = send_tile(tile, tiles_ref, out_ref, sem_ref.at[1])
-    wait_all([first, second, third])
+    fill_tile(tile, tiles_ref)
+    send([(tiles_ref, out_ref.at[:, :, pl.ds(half, 2 * K)])], sem_ref.at[pl.ds(1, 1)])
+    wait_all([first, third])
 
 
 def second_table_body(
@@ -253,13 +246,17 @@
     logits = state_ref[:K] + coef * picked_ref[0].astype(f32)
     resid, prob = residuals(logits, state_ref[K : K + 1])
     tile = sums_tile(resid, prob, picked_ref[1].astype(f32))
-    sums_copy = send_tile(tile, tiles_ref, out_ref, sem_ref.at[0])
+    fill_tile(tile, tiles_ref)
     logits_taken = state_taken_ref[:K] + coef * picked_taken_ref[0].astype(f32)
     resid_taken, _ = residuals(logits_taken, state_taken_ref[K : K + 1])
-    table_copies = send_table(
-        resid, resid_taken, both_ref, table_ref, out_ref, sem_ref.at[pl.ds(2, 2)]
-    )
-    wait_all([sums_copy] + table_copies)
+    fill_table(resid, resid_taken, both_ref, table_ref)
+    send(
+        [
+            (table_ref, out_ref.at[:, :, pl.ds(0, half)]),
+            (tiles_ref, out_ref.at[:, :, pl.ds(half, 2 * K)]),
+        ],
+        sem_ref,
+    )
 
 
 def third_table_body(
@@ -278,16 +275,12 @@
 
     logits = updated(state_ref[:K], picked_ref)
     new_ref[...] = logits
-    logits_copy = pltpu.make_async_copy(new_ref, logits_ref, sem_ref.at[0])
-    logits_copy.start()
     resid, _ = residuals(logits, state_ref[K : K + 1])
     resid_taken, _ = residuals(
         updated(state_taken_ref[:K], picked_taken_ref), state_taken_ref[K : K + 1]
     )
-    table_copies = send_table(
-        resid, resid_taken, both_ref, table_ref, out_ref, sem_ref.at[pl.ds(2, 2)]
-    )
-    wait_all([logits_copy] + table_copies)
+    fill_table(resid, resid_taken, both_ref, table_ref)
+    send([(table_ref, out_ref), (new_ref, logits_ref)], sem_ref)
 
 
 def shards(genotypes, labels, base_margin, winners):
@@ -363,7 +356,7 @@
         second_table_body,
         (pltpu.HBM(payload_shape, bf16), pltpu.VMEM((K, LANES), f32)),
         [VMEM] * 6,
-        [pltpu.VMEM(table_shape, bf16), tiles, sems((4,))],
+        [pltpu.VMEM(table_shape, bf16), tiles, sems((2,))],
         flops=work,
         moved=4 * samples * half,
     )(near(shared0), state, state_taken, near(picked), picked_taken, both)
@@ -373,7 +366,7 @@
         third_table_body,
         (pltpu.HBM(table_shape, bf16), pltpu.HBM((K, samples), f32)),
         [VMEM] * 7,
-        [pltpu.VMEM(table_shape, bf16), pltpu.VMEM((K, samples), f32), sems((4,))],
+        [pltpu.VMEM(table_shape, bf16), pltpu.VMEM((K, samples), f32), sems((2,))],
         flops=work,
         moved=4 * samples * half,
     )(near(shared1), near(coef), state, state_taken, near(picked), picked_taken, both)

time: 102 us -> 103 us (level)
  no operation moved by 1% of the time
where the time goes in v11:
time: 103 us; the launch traced here: 102 us
  waiting for transfers between devices  54.7 us (53%)
  starting transfers between devices  37.1 us (36%)
  Pallas kernels  7.83 us (8%)
    all_to_all x1, waiting for transfers between devices, shards(): shared2 = lax.all_to_all(payload, 'rows', 0, 0, tiled=True)  16.9 us
    all_to_all x1, waiting for transfers between devices, shards(): shared1 = lax.all_to_all(payload, 'rows', 0, 0, tiled=True)  16.7 us
    all_to_all x1, waiting for transfers between devices, shards(): shared0 = lax.all_to_all(payload, 'rows', 0, 0, tiled=True)  14 us
    all_to_all x1, starting transfers between devices, shards(): shared0 = lax.all_to_all(payload, 'rows', 0, 0, tiled=True)  12.4 us
    all_to_all x1, starting transfers between devices, shards(): cols = lax.all_to_all(sent, 'feat', 0, 0, tiled=True)  11.7 us
    all_to_all x1, waiting for transfers between devices, shards(): cols = lax.all_to_all(sent, 'feat', 0, 0, tiled=True)  5.92 us
    all_to_all x1, starting transfers between devices, shards(): shared1 = lax.all_to_all(payload, 'rows', 0, 0, tiled=True)  3.39 us
    all_to_all x1, starting transfers between devices, shards(): shared2 = lax.all_to_all(payload, 'rows', 0, 0, tiled=True)  3.38 us
  transfers between devices with their start and end apart: 7, of which 5 were waited for; matrix products, arithmetic and copies ran while one was open for 0% of the time, Pallas kernels for 4%

profile of v11, /device:TPU:32, one launch (start us, length us, event | category | flops | bytes accessed | tf_op | source)
XLA Modules:
  0.0 102.0 jit_solution(12312022875992127905)
XLA Ops:
  0.6 1.9 %collective-permute-start = (bf16[512,2048]{1,0:T(8,128)(2,1)}, bf16[512,2048]{1,0:T(8,128)(2,1)}, u32[]{:S(2)}, u32[]{:S(2)}) collective-permute-start(bf16[512,2048]{1,0:T(8,128)(2,1)} %geno_ref.3), channel_id=1, source_target_pairs={{0,64},{64,0},{128,192},{192,128},{256,320},{320,256},{384,448},{4... | collective-permute-start | bytes 6291464 | tf_op jit(solution)/shard_map/ppermute | solution.py:315
  2.6 0.0 copy-start
  2.6 0.7 copy-done
  3.2 2.1 %shard_map.59 = (bf16[64,8,128]{2,1,0:T(8,128)(2,1)}, f32[72,512]{1,0:T(8,128)S(1)}) custom-call(s32[2,64]{1,0:T(2,128)S(1)} %copy-done, bf16[512,2048]{1,0:T(8,128)(2,1)} %geno_ref.3, f32[64,512]{1,0:T(8,128)} %bitcast.30, s32[1,512]{1,0:T(1,128)} %bitcast.31), custom_call_target="tpu_custom_call" | custom-call | bytes 262144 | tf_op jit(solution)/shard_map/pallas_call | solution.py:299
  5.3 11.7 %all-to-all-start = ((bf16[64,8,128]{2,1,0:T(8,128)(2,1)}), bf16[64,8,128]{2,1,0:T(8,128)(2,1)S(1)}, u32[]{:S(2)}, u32[]{:S(2)}) async-start(bf16[64,8,128]{2,1,0:T(8,128)(2,1)} %get-tuple-element.14), calls=%async_computation | async-start | bytes 262144 | tf_op jit(solution)/shard_map/all_to_all | solution.py:313
  17.0 1.9 %collective-permute-start.1 = (f32[72,512]{1,0:T(8,128)S(1)}, f32[72,512]{1,0:T(8,128)S(1)}, u32[]{:S(2)}, u32[]{:S(2)}) collective-permute-start(f32[72,512]{1,0:T(8,128)S(1)} %get-tuple-element.15.state_ref), channel_id=1, source_target_pairs={{0,64},{64,0},{128,192},{192,128},{256,320},{320,256},{384,448},{4... | collective-permute-start | bytes 442376 | tf_op jit(solution)/shard_map/ppermute | solution.py:317
  18.9 0.0 collective-permute-done.far_taken_ref
  18.9 1.6 %shard_map.60 = (f32[64,1024]{1,0:T(8,128)S(1)}, bf16[1024,1024]{1,0:T(8,128)(2,1)S(1)}, bf16[2,64,64]{2,1,0:T(8,128)(2,1)S(1)}) custom-call(f32[72,512]{1,0:T(8,128)S(1)} %get-tuple-element.15.state_ref, bf16[512,2048]{1,0:T(8,128)(2,1)} %geno_ref.3, bf16[512,2048]{1,0:T(8,128)(2,1)} %collective-permute-done.far_taken_ref, s32[2,64]{1,0:T(2,128)} %far_win_ref.1), custom_call_target="tpu_custom_call" | custom-call | flops 67108864 | bytes 2097152 | tf_op jit(solution)/shard_map/pallas_call | solution.py:320
  20.5 0.0 collective-permute-done.1.state_taken_ref
  20.5 0.3 shard_map.61.table_ref
  20.9 5.9 %all-to-all-done.cols_ref = bf16[64,8,128]{2,1,0:T(8,128)(2,1)S(1)} async-done(((bf16[64,8,128]{2,1,0:T(8,128)(2,1)}), bf16[64,8,128]{2,1,0:T(8,128)(2,1)S(1)}, u32[]{:S(2)}, u32[]{:S(2)}) %all-to-all-start) | async-done | bytes 131104 | tf_op jit(solution)/shard_map/all_to_all | solution.py:313
  26.8 1.1 %shard_map.62 = (bf16[8,8,1152]{2,1,0:T(8,128)(2,1)}, bf16[2,64,512]{2,1,0:T(8,128)(2,1)S(1)}, bf16[2,64,512]{2,1,0:T(8,128)(2,1)}) custom-call(bf16[64,8,128]{2,1,0:T(8,128)(2,1)S(1)} %all-to-all-done.cols_ref, bf16[2,64,64]{2,1,0:T(8,128)(2,1)S(1)} %get-tuple-element.16.place_ref, f32[72,512]{1,0:T(8,128)S(1)} %get-tuple-element.15.state_ref, ...), custom_call_target="tpu_custom_call" | custom-call | bytes 2097152 | tf_op jit(solution)/shard_map/pallas_call | solution.py:341
  27.9 12.4 %all-to-all-start.1 = ((bf16[8,8,1152]{2,1,0:T(8,128)(2,1)}), bf16[8,8,1152]{2,1,0:T(8,128)(2,1)S(1)}, u32[]{:S(2)}, u32[]{:S(2)}) async-start(bf16[8,8,1152]{2,1,0:T(8,128)(2,1)} %get-tuple-element.19), calls=%async_computation.1 | async-start | bytes 294912 | tf_op jit(solution)/shard_map/all_to_all | solution.py:352
  40.3 2.4 %collective-permute-start.2 = (bf16[2,64,512]{2,1,0:T(8,128)(2,1)}, bf16[2,64,512]{2,1,0:T(8,128)(2,1)S(1)}, u32[]{:S(2)}, u32[]{:S(2)}) collective-permute-start(bf16[2,64,512]{2,1,0:T(8,128)(2,1)} %get-tuple-element.21), channel_id=1, source_target_pairs={{0,64},{64,0},{128,192},{192,128},{256,320},{320,256},{384,448},{4... | collective-permute-start | bytes 393224 | tf_op jit(solution)/shard_map/ppermute | solution.py:353
  42.7 1.2 %collective-permute-done.2.picked_taken_ref = bf16[2,64,512]{2,1,0:T(8,128)(2,1)S(1)} collective-permute-done((bf16[2,64,512]{2,1,0:T(8,128)(2,1)}, bf16[2,64,512]{2,1,0:T(8,128)(2,1)S(1)}, u32[]{:S(2)}, u32[]{:S(2)}) %collective-permute-start.2) | collective-permute-done | bytes 131104 | tf_op jit(solution)/shard_map/ppermute | solution.py:353
  43.9 14.0 %all-to-all-done.1.shared_ref = bf16[8,8,1152]{2,1,0:T(8,128)(2,1)S(1)} async-done(((bf16[8,8,1152]{2,1,0:T(8,128)(2,1)}), bf16[8,8,1152]{2,1,0:T(8,128)(2,1)S(1)}, u32[]{:S(2)}, u32[]{:S(2)}) %all-to-all-start.1) | async-done | bytes 147488 | tf_op jit(solution)/shard_map/all_to_all | solution.py:352
  57.9 1.4 %shard_map.63 = (bf16[8,8,1152]{2,1,0:T(8,128)(2,1)}, f32[64,128]{1,0:T(8,128)S(1)}) custom-call(bf16[8,8,1152]{2,1,0:T(8,128)(2,1)S(1)} %all-to-all-done.1.shared_ref, f32[72,512]{1,0:T(8,128)S(1)} %get-tuple-element.15.state_ref, f32[72,512]{1,0:T(8,128)S(1)} %collective-permute-done.1.state_taken_ref, ...), custom_call_target="tpu_custom_call" | custom-call | flops 134217728 | bytes 2097152 | tf_op jit(solution)/shard_map/pallas_call | solution.py:355
  59.3 3.4 %all-to-all-start.2 = ((bf16[8,8,1152]{2,1,0:T(8,128)(2,1)}), bf16[8,8,1152]{2,1,0:T(8,128)(2,1)S(1)}, u32[]{:S(2)}, u32[]{:S(2)}) async-start(bf16[8,8,1152]{2,1,0:T(8,128)(2,1)} %get-tuple-element.22), calls=%async_computation.2 | async-start | bytes 294912 | tf_op jit(solution)/shard_map/all_to_all | solution.py:363
  62.8 16.7 %all-to-all-done.2.shared_ref = bf16[8,8,1152]{2,1,0:T(8,128)(2,1)S(1)} async-done(((bf16[8,8,1152]{2,1,0:T(8,128)(2,1)}), bf16[8,8,1152]{2,1,0:T(8,128)(2,1)S(1)}, u32[]{:S(2)}, u32[]{:S(2)}) %all-to-all-start.2) | async-done | bytes 147488 | tf_op jit(solution)/shard_map/all_to_all | solution.py:363
  79.5 1.4 %shard_map.64 = (bf16[8,8,1024]{2,1,0:T(8,128)(2,1)}, f32[64,512]{1,0:T(8,128)}) custom-call(bf16[8,8,1152]{2,1,0:T(8,128)(2,1)S(1)} %all-to-all-done.2.shared_ref, f32[64,128]{1,0:T(8,128)S(1)} %get-tuple-element.23.coef_ref, f32[72,512]{1,0:T(8,128)S(1)} %get-tuple-element.15.state_ref, f32[72,512]{1,0:T(8,128)S(1)} %collective-permute-done.1.state_taken_ref, ...), custom_call_target="tpu_custom_call" | custom-call | flops 134217728 | bytes 2097152 | tf_op jit(solution)/shard_map/pallas_call | solution.py:365
  80.8 3.4 %all-to-all-start.3 = ((bf16[8,8,1024]{2,1,0:T(8,128)(2,1)}), bf16[8,8,1024]{2,1,0:T(8,128)(2,1)S(1)}, u32[]{:S(2)}, u32[]{:S(2)}) async-start(bf16[8,8,1024]{2,1,0:T(8,128)(2,1)} %get-tuple-element.25), calls=%async_computation.3 | async-start | bytes 262144 | tf_op jit(solution)/shard_map/all_to_all | solution.py:373
  84.3 16.9 %all-to-all-done.3 = bf16[8,8,1024]{2,1,0:T(8,128)(2,1)S(1)} async-done(((bf16[8,8,1024]{2,1,0:T(8,128)(2,1)}), bf16[8,8,1024]{2,1,0:T(8,128)(2,1)S(1)}, u32[]{:S(2)}, u32[]{:S(2)}) %all-to-all-start.3) | async-done | bytes 131104 | tf_op jit(solution)/shard_map/all_to_all | solution.py:373
  101.3 0.7 pad_maximum_fusion
  (10 shorter events, 0.1 us)
Async XLA Ops:
  0.6 18.3 %collective-permute-start = (bf16[512,2048]{1,0:T(8,128)(2,1)}, bf16[512,2048]{1,0:T(8,128)(2,1)}, u32[]{:S(2)}, u32[]{:S(2)}) collective-permute-start(bf16[512,2048]{1,0:T(8,128)(2,1)} %geno_ref.3), channel_id=1, source_target_pairs={{0,64},{64,0},{128,192},{192,128},{256,320},{320,256},{384,448},{4... | collective-permute-start | bytes 6291464 | tf_op jit(solution)/shard_map/ppermute | solution.py:315
  2.6 0.7 copy-start
  5.3 21.5 %all-to-all-start = ((bf16[64,8,128]{2,1,0:T(8,128)(2,1)}), bf16[64,8,128]{2,1,0:T(8,128)(2,1)S(1)}, u32[]{:S(2)}, u32[]{:S(2)}) async-start(bf16[64,8,128]{2,1,0:T(8,128)(2,1)} %get-tuple-element.14), calls=%async_computation | async-start | bytes 262144 | tf_op jit(solution)/shard_map/all_to_all | solution.py:313
  17.0 3.5 %collective-permute-start.1 = (f32[72,512]{1,0:T(8,128)S(1)}, f32[72,512]{1,0:T(8,128)S(1)}, u32[]{:S(2)}, u32[]{:S(2)}) collective-permute-start(f32[72,512]{1,0:T(8,128)S(1)} %get-tuple-element.15.state_ref), channel_id=1, source_target_pairs={{0,64},{64,0},{128,192},{192,128},{256,320},{320,256},{384,448},{4... | collective-permute-start | bytes 442376 | tf_op jit(solution)/shard_map/ppermute | solution.py:317
  27.9 30.0 %all-to-all-start.1 = ((bf16[8,8,1152]{2,1,0:T(8,128)(2,1)}), bf16[8,8,1152]{2,1,0:T(8,128)(2,1)S(1)}, u32[]{:S(2)}, u32[]{:S(2)}) async-start(bf16[8,8,1152]{2,1,0:T(8,128)(2,1)} %get-tuple-element.19), calls=%async_computation.1 | async-start | bytes 294912 | tf_op jit(solution)/shard_map/all_to_all | solution.py:352
  40.3 3.6 %collective-permute-start.2 = (bf16[2,64,512]{2,1,0:T(8,128)(2,1)}, bf16[2,64,512]{2,1,0:T(8,128)(2,1)S(1)}, u32[]{:S(2)}, u32[]{:S(2)}) collective-permute-start(bf16[2,64,512]{2,1,0:T(8,128)(2,1)} %get-tuple-element.21), channel_id=1, source_target_pairs={{0,64},{64,0},{128,192},{192,128},{256,320},{320,256},{384,448},{4... | collective-permute-start | bytes 393224 | tf_op jit(solution)/shard_map/ppermute | solution.py:353
  59.3 20.1 %all-to-all-start.2 = ((bf16[8,8,1152]{2,1,0:T(8,128)(2,1)}), bf16[8,8,1152]{2,1,0:T(8,128)(2,1)S(1)}, u32[]{:S(2)}, u32[]{:S(2)}) async-start(bf16[8,8,1152]{2,1,0:T(8,128)(2,1)} %get-tuple-element.22), calls=%async_computation.2 | async-start | bytes 294912 | tf_op jit(solution)/shard_map/all_to_all | solution.py:363
  80.8 20.4 %all-to-all-start.3 = ((bf16[8,8,1024]{2,1,0:T(8,128)(2,1)}), bf16[8,8,1024]{2,1,0:T(8,128)(2,1)S(1)}, u32[]{:S(2)}, u32[]{:S(2)}) async-start(bf16[8,8,1024]{2,1,0:T(8,128)(2,1)} %get-tuple-element.25), calls=%async_computation.3 | async-start | bytes 262144 | tf_op jit(solution)/shard_map/all_to_all | solution.py:373

commit v12 on v10

--- a/solution.py
+++ b/solution.py
@@ -8,6 +8,8 @@
 K = 64
 ITERS = 2
 LANES = 128
+SUMS_ORDER = (0, 4, 2, 6, 1, 5, 3, 7)
+LAST_ORDER = (0, 2, 6, 4, 1, 3, 7, 5)
 
 
 shrink_rate = 0.5
@@ -51,6 +53,23 @@
 
 def near(values):
     return pltpu.with_memory_space_constraint(values, pltpu.VMEM)
+
+
+def reverse_bits(values, count):
+    bits = count.bit_length() - 1
+    return sum(((values >> bit) & 1) << (bits - 1 - bit) for bit in range(bits))
+
+
+def place_classes(table, out_ref, span, order):
+    share = out_ref.shape[1]
+    for place, peer in enumerate(order):
+        out_ref[place, :, span] = table[peer * share : (peer + 1) * share].astype(bf16)
+
+
+def exchange(payload, order):
+    return lax.all_to_all(
+        payload, "rows", 0, 0, tiled=True, axis_index_groups=[list(order)]
+    )
 
 
 def rounded(values):
@@ -176,13 +195,13 @@
     return copy
 
 
-def send_table(resid, resid_taken, both_ref, table_ref, out_ref, sem_ref, pieces=2):
+def send_table(resid, resid_taken, both_ref, table_ref, out_ref, sem_ref, order, pieces=2):
     width = table_ref.shape[2] // pieces
     copies = []
     for piece in range(pieces):
         span = pl.ds(piece * width, width)
         table = half_table(resid, resid_taken, both_ref, piece * width, width)
-        table_ref[:, :, span] = table.reshape(table_ref.shape[0], -1, width).astype(bf16)
+        place_classes(table, table_ref, span, order)
         copy = pltpu.make_async_copy(
             table_ref.at[:, :, span], out_ref.at[:, :, span], sem_ref.at[piece]
         )
@@ -198,7 +217,9 @@
     wins.start()
     copies = load_halves(geno_ref, far_taken_ref, both_ref, sem_ref)
     resid, _ = residuals(state_ref[:K], state_ref[K : K + 1])
-    feat = lax.broadcasted_iota(i32, place_ref.shape[1:], 0)
+    feat = reverse_bits(
+        lax.broadcasted_iota(i32, place_ref.shape[1:], 0), place_ref.shape[1]
+    )
     wins.wait()
     for step in range(ITERS):
         owner = win_ref[step : step + 1] // geno_ref.shape[1]
@@ -212,7 +233,7 @@
     samples = state_taken_ref.shape[1]
     resid_taken, _ = residuals(state_taken_ref[:K], state_taken_ref[K : K + 1])
     table = own_ref[...] + jnp.dot(resid_taken, both_ref[samples:], preferred_element_type=f32)
-    out_ref[...] = table.reshape(out_ref.shape).astype(bf16)
+    place_classes(table, out_ref, slice(None), SUMS_ORDER)
 
 
 def first_sums_body(
@@ -257,7 +278,8 @@
     logits_taken = state_taken_ref[:K] + coef * picked_taken_ref[0].astype(f32)
     resid_taken, _ = residuals(logits_taken, state_taken_ref[K : K + 1])
     table_copies = send_table(
-        resid, resid_taken, both_ref, table_ref, out_ref, sem_ref.at[pl.ds(2, 2)]
+        resid, resid_taken, both_ref, table_ref, out_ref, sem_ref.at[pl.ds(2, 2)],
+        SUMS_ORDER,
     )
     wait_all([sums_copy] + table_copies)
 
@@ -285,7 +307,8 @@
         updated(state_taken_ref[:K], picked_taken_ref), state_taken_ref[K : K + 1]
     )
     table_copies = send_table(
-        resid, resid_taken, both_ref, table_ref, out_ref, sem_ref.at[pl.ds(2, 2)]
+        resid, resid_taken, both_ref, table_ref, out_ref, sem_ref.at[pl.ds(2, 2)],
+        LAST_ORDER,
     )
     wait_all([logits_copy] + table_copies)
 
@@ -317,7 +340,8 @@
         ],
         moved=samples * LANES * 4,
     )(near(winners), far(genotypes), far(base_margin.T), far(labels[None, :]))
-    cols = lax.all_to_all(sent, "feat", 0, 0, tiled=True)
+    listed = [reverse_bits(i, feat_count) for i in range(feat_count)]
+    cols = lax.all_to_all(sent, "feat", 0, 0, tiled=True, axis_index_groups=[listed])
 
     taken = far(lax.ppermute(genotypes, "rows", partners))
     geno = far(genotypes)
@@ -356,7 +380,7 @@
         [tiles, sems((4,))],
         moved=4 * samples * half,
     )(near(cols), place, state, table)
-    shared0 = lax.all_to_all(payload, "rows", 0, 0, tiled=True)
+    shared0 = exchange(payload, SUMS_ORDER)
     picked_taken = near(lax.ppermute(far_picked, "rows", partners))
 
     payload, coef = call(
@@ -367,7 +391,7 @@
         flops=work,
         moved=4 * samples * half,
     )(near(shared0), state, state_taken, near(picked), picked_taken, both)
-    shared1 = lax.all_to_all(payload, "rows", 0, 0, tiled=True)
+    shared1 = exchange(payload, SUMS_ORDER)
 
     payload, logits = call(
         third_table_body,
@@ -377,13 +401,16 @@
         flops=work,
         moved=4 * samples * half,
     )(near(shared1), near(coef), state, state_taken, near(picked), picked_taken, both)
-    shared2 = lax.all_to_all(payload, "rows", 0, 0, tiled=True)
+    shared2 = exchange(payload, LAST_ORDER)
 
     tables = []
-    for shared in (shared0, shared1, shared2):
-        parts = shared[:, :, :half].astype(f32).reshape(rows_count // 2, 2, class_share, half)
-        total = jnp.sum(parts, axis=0)
-        tables.append(jnp.concatenate([total[0], total[1]], axis=1))
+    for shared, order in ((shared0, SUMS_ORDER), (shared1, SUMS_ORDER), (shared2, LAST_ORDER)):
+        parts = shared[:, :, :half].astype(f32)
+        sides = [
+            sum(parts[place] for place, peer in enumerate(order) if peer % 2 == side)
+            for side in range(2)
+        ]
+        tables.append(jnp.concatenate(sides, axis=1))
     return (logits.T, jnp.stack(tables))
 
 

time: 102 us -> 102 us (level)
  waiting for transfers between devices: 54.7 us -> 52.4 us
  starting transfers between devices: 37.1 us -> 38.7 us
    all_to_all x4, waiting for transfers between devices: 53.5 us -> 51.2 us  [the longest x3 45.2 us: exchange(): lax.all_to_all(payload, 'rows', 0, 0, tiled=True, axis_index_groups=[list...]
    all_to_all x4, starting transfers between devices: 30.9 us -> 32.4 us  [the longest x3 20.7 us: exchange(): lax.all_to_all(payload, 'rows', 0, 0, tiled=True, axis_index_groups=[list...]
where the time goes in v12:
time: 102 us; the launch traced here: 101 us
  waiting for transfers between devices  52.4 us (51%)
  starting transfers between devices  38.7 us (38%)
  Pallas kernels  7.77 us (8%)
    all_to_all x3, waiting for transfers between devices, exchange(): lax.all_to_all(payload, 'rows', 0, 0, tiled=True, axis_index_groups=[list...  45.2 us
    all_to_all x3, starting transfers between devices, exchange(): lax.all_to_all(payload, 'rows', 0, 0, tiled=True, axis_index_groups=[list...  20.7 us
    all_to_all x1, starting transfers between devices, shards(): lax.all_to_all(sent, 'feat', 0, 0, tiled=True, axis_index_groups=[listed])  11.7 us
    all_to_all x1, waiting for transfers between devices, shards(): lax.all_to_all(sent, 'feat', 0, 0, tiled=True, axis_index_groups=[listed])  5.96 us
    ppermute x1, starting transfers between devices, shards(): picked_taken = near(lax.ppermute(far_picked, 'rows', partners))  2.4 us
    pallas_call x1, Pallas kernels, shards(): call(pick_body, (pltpu.VMEM((feat_count, ITERS * samples // LANES, LANES)...  2.06 us
  transfers between devices with their start and end apart: 7, of which 5 were waited for; matrix products, arithmetic and copies ran while one was open for 0% of the time, Pallas kernels for 4%

profile of v12, /device:TPU:32, one launch (start us, length us, event | category | flops | bytes accessed | tf_op | source)
XLA Modules:
  0.0 101.1 jit_solution(17598315434637710121)
XLA Ops:
  0.6 1.9 %collective-permute-start = (bf16[512,2048]{1,0:T(8,128)(2,1)}, bf16[512,2048]{1,0:T(8,128)(2,1)}, u32[]{:S(2)}, u32[]{:S(2)}) collective-permute-start(bf16[512,2048]{1,0:T(8,128)(2,1)} %geno_ref.3), channel_id=1, source_target_pairs={{0,64},{64,0},{128,192},{192,128},{256,320},{320,256},{384,448},{4... | collective-permute-start | bytes 6291464 | tf_op jit(solution)/shard_map/ppermute | solution.py:346
  2.6 0.0 copy-start
  2.6 0.7 copy-done
  3.2 2.1 %shard_map.59 = (bf16[64,8,128]{2,1,0:T(8,128)(2,1)}, f32[72,512]{1,0:T(8,128)S(1)}) custom-call(s32[2,64]{1,0:T(2,128)S(1)} %copy-done, bf16[512,2048]{1,0:T(8,128)(2,1)} %geno_ref.3, f32[64,512]{1,0:T(8,128)} %bitcast.21, s32[1,512]{1,0:T(1,128)} %bitcast.22), custom_call_target="tpu_custom_call" | custom-call | bytes 262144 | tf_op jit(solution)/shard_map/pallas_call | solution.py:329
  5.3 11.7 %all-to-all-start = ((bf16[64,8,128]{2,1,0:T(8,128)(2,1)}), bf16[64,8,128]{2,1,0:T(8,128)(2,1)S(1)}, u32[]{:S(2)}, u32[]{:S(2)}) async-start(bf16[64,8,128]{2,1,0:T(8,128)(2,1)} %get-tuple-element.14), calls=%async_computation | async-start | bytes 262144 | tf_op jit(solution)/shard_map/all_to_all | solution.py:344
  17.0 1.9 %collective-permute-start.1 = (f32[72,512]{1,0:T(8,128)S(1)}, f32[72,512]{1,0:T(8,128)S(1)}, u32[]{:S(2)}, u32[]{:S(2)}) collective-permute-start(f32[72,512]{1,0:T(8,128)S(1)} %get-tuple-element.15.state_ref), channel_id=1, source_target_pairs={{0,64},{64,0},{128,192},{192,128},{256,320},{320,256},{384,448},{4... | collective-permute-start | bytes 442376 | tf_op jit(solution)/shard_map/ppermute | solution.py:348
  18.9 0.0 collective-permute-done.far_taken_ref
  18.9 1.6 %shard_map.60 = (f32[64,1024]{1,0:T(8,128)S(1)}, bf16[1024,1024]{1,0:T(8,128)(2,1)S(1)}, bf16[2,64,64]{2,1,0:T(8,128)(2,1)S(1)}) custom-call(f32[72,512]{1,0:T(8,128)S(1)} %get-tuple-element.15.state_ref, bf16[512,2048]{1,0:T(8,128)(2,1)} %geno_ref.3, bf16[512,2048]{1,0:T(8,128)(2,1)} %collective-permute-done.far_taken_ref, s32[2,64]{1,0:T(2,128)} %far_win_ref.1), custom_call_target="tpu_custom_call" | custom-call | flops 67108864 | bytes 2097152 | tf_op jit(solution)/shard_map/pallas_call | solution.py:351
  20.5 0.0 collective-permute-done.1.state_taken_ref
  20.5 0.3 shard_map.61.table_ref
  20.9 6.0 %all-to-all-done.cols_ref = bf16[64,8,128]{2,1,0:T(8,128)(2,1)S(1)} async-done(((bf16[64,8,128]{2,1,0:T(8,128)(2,1)}), bf16[64,8,128]{2,1,0:T(8,128)(2,1)S(1)}, u32[]{:S(2)}, u32[]{:S(2)}) %all-to-all-start) | async-done | bytes 131104 | tf_op jit(solution)/shard_map/all_to_all | solution.py:344
  26.8 1.1 %shard_map.62 = (bf16[8,8,1152]{2,1,0:T(8,128)(2,1)}, bf16[2,64,512]{2,1,0:T(8,128)(2,1)S(1)}, bf16[2,64,512]{2,1,0:T(8,128)(2,1)}) custom-call(bf16[64,8,128]{2,1,0:T(8,128)(2,1)S(1)} %all-to-all-done.cols_ref, bf16[2,64,64]{2,1,0:T(8,128)(2,1)S(1)} %get-tuple-element.16.place_ref, f32[72,512]{1,0:T(8,128)S(1)} %get-tuple-element.15.state_ref, ...), custom_call_target="tpu_custom_call" | custom-call | bytes 2097152 | tf_op jit(solution)/shard_map/pallas_call | solution.py:372
  27.9 12.4 %all-to-all-start.1 = ((bf16[8,8,1152]{2,1,0:T(8,128)(2,1)}), bf16[8,8,1152]{2,1,0:T(8,128)(2,1)S(1)}, u32[]{:S(2)}, u32[]{:S(2)}) async-start(bf16[8,8,1152]{2,1,0:T(8,128)(2,1)} %get-tuple-element.19), calls=%async_computation.1 | async-start | bytes 294912 | tf_op jit(solution)/shard_map/all_to_all | solution.py:70
  40.3 2.4 %collective-permute-start.2 = (bf16[2,64,512]{2,1,0:T(8,128)(2,1)}, bf16[2,64,512]{2,1,0:T(8,128)(2,1)S(1)}, u32[]{:S(2)}, u32[]{:S(2)}) collective-permute-start(bf16[2,64,512]{2,1,0:T(8,128)(2,1)} %get-tuple-element.21), channel_id=1, source_target_pairs={{0,64},{64,0},{128,192},{192,128},{256,320},{320,256},{384,448},{4... | collective-permute-start | bytes 393224 | tf_op jit(solution)/shard_map/ppermute | solution.py:384
  42.7 1.2 %collective-permute-done.2.picked_taken_ref = bf16[2,64,512]{2,1,0:T(8,128)(2,1)S(1)} collective-permute-done((bf16[2,64,512]{2,1,0:T(8,128)(2,1)}, bf16[2,64,512]{2,1,0:T(8,128)(2,1)S(1)}, u32[]{:S(2)}, u32[]{:S(2)}) %collective-permute-start.2) | collective-permute-done | bytes 131104 | tf_op jit(solution)/shard_map/ppermute | solution.py:384
  43.9 12.1 %all-to-all-done.1.shared_ref = bf16[8,8,1152]{2,1,0:T(8,128)(2,1)S(1)} async-done(((bf16[8,8,1152]{2,1,0:T(8,128)(2,1)}), bf16[8,8,1152]{2,1,0:T(8,128)(2,1)S(1)}, u32[]{:S(2)}, u32[]{:S(2)}) %all-to-all-start.1) | async-done | bytes 147488 | tf_op jit(solution)/shard_map/all_to_all | solution.py:70
  56.0 1.4 %shard_map.63 = (bf16[8,8,1152]{2,1,0:T(8,128)(2,1)}, f32[64,128]{1,0:T(8,128)S(1)}) custom-call(bf16[8,8,1152]{2,1,0:T(8,128)(2,1)S(1)} %all-to-all-done.1.shared_ref, f32[72,512]{1,0:T(8,128)S(1)} %get-tuple-element.15.state_ref, f32[72,512]{1,0:T(8,128)S(1)} %collective-permute-done.1.state_taken_ref, ...), custom_call_target="tpu_custom_call" | custom-call | flops 134217728 | bytes 2097152 | tf_op jit(solution)/shard_map/pallas_call | solution.py:386
  57.5 4.1 %all-to-all-start.2 = ((bf16[8,8,1152]{2,1,0:T(8,128)(2,1)}), bf16[8,8,1152]{2,1,0:T(8,128)(2,1)S(1)}, u32[]{:S(2)}, u32[]{:S(2)}) async-start(bf16[8,8,1152]{2,1,0:T(8,128)(2,1)} %get-tuple-element.22), calls=%async_computation.2 | async-start | bytes 294912 | tf_op jit(solution)/shard_map/all_to_all | solution.py:70
  61.6 15.7 %all-to-all-done.2.shared_ref = bf16[8,8,1152]{2,1,0:T(8,128)(2,1)S(1)} async-done(((bf16[8,8,1152]{2,1,0:T(8,128)(2,1)}), bf16[8,8,1152]{2,1,0:T(8,128)(2,1)S(1)}, u32[]{:S(2)}, u32[]{:S(2)}) %all-to-all-start.2) | async-done | bytes 147488 | tf_op jit(solution)/shard_map/all_to_all | solution.py:70
  77.3 1.3 %shard_map.64 = (bf16[8,8,1024]{2,1,0:T(8,128)(2,1)}, f32[64,512]{1,0:T(8,128)}) custom-call(bf16[8,8,1152]{2,1,0:T(8,128)(2,1)S(1)} %all-to-all-done.2.shared_ref, f32[64,128]{1,0:T(8,128)S(1)} %get-tuple-element.23.coef_ref, f32[72,512]{1,0:T(8,128)S(1)} %get-tuple-element.15.state_ref, f32[72,512]{1,0:T(8,128)S(1)} %collective-permute-done.1.state_taken_ref, ...), custom_call_target="tpu_custom_call" | custom-call | flops 134217728 | bytes 2097152 | tf_op jit(solution)/shard_map/pallas_call | solution.py:396
  78.6 4.3 %all-to-all-start.3 = ((bf16[8,8,1024]{2,1,0:T(8,128)(2,1)}), bf16[8,8,1024]{2,1,0:T(8,128)(2,1)S(1)}, u32[]{:S(2)}, u32[]{:S(2)}) async-start(bf16[8,8,1024]{2,1,0:T(8,128)(2,1)} %get-tuple-element.25), calls=%async_computation.3 | async-start | bytes 262144 | tf_op jit(solution)/shard_map/all_to_all | solution.py:70
  82.9 17.4 %all-to-all-done.3 = bf16[8,8,1024]{2,1,0:T(8,128)(2,1)S(1)} async-done(((bf16[8,8,1024]{2,1,0:T(8,128)(2,1)}), bf16[8,8,1024]{2,1,0:T(8,128)(2,1)S(1)}, u32[]{:S(2)}, u32[]{:S(2)}) %all-to-all-start.3) | async-done | bytes 131104 | tf_op jit(solution)/shard_map/all_to_all | solution.py:70
  100.4 0.7 pad_maximum_fusion
  (8 shorter events, 0.1 us)
Async XLA Ops:
  0.6 18.3 %collective-permute-start = (bf16[512,2048]{1,0:T(8,128)(2,1)}, bf16[512,2048]{1,0:T(8,128)(2,1)}, u32[]{:S(2)}, u32[]{:S(2)}) collective-permute-start(bf16[512,2048]{1,0:T(8,128)(2,1)} %geno_ref.3), channel_id=1, source_target_pairs={{0,64},{64,0},{128,192},{192,128},{256,320},{320,256},{384,448},{4... | collective-permute-start | bytes 6291464 | tf_op jit(solution)/shard_map/ppermute | solution.py:346
  2.6 0.7 copy-start
  5.3 21.5 %all-to-all-start = ((bf16[64,8,128]{2,1,0:T(8,128)(2,1)}), bf16[64,8,128]{2,1,0:T(8,128)(2,1)S(1)}, u32[]{:S(2)}, u32[]{:S(2)}) async-start(bf16[64,8,128]{2,1,0:T(8,128)(2,1)} %get-tuple-element.14), calls=%async_computation | async-start | bytes 262144 | tf_op jit(solution)/shard_map/all_to_all | solution.py:344
  17.0 3.5 %collective-permute-start.1 = (f32[72,512]{1,0:T(8,128)S(1)}, f32[72,512]{1,0:T(8,128)S(1)}, u32[]{:S(2)}, u32[]{:S(2)}) collective-permute-start(f32[72,512]{1,0:T(8,128)S(1)} %get-tuple-element.15.state_ref), channel_id=1, source_target_pairs={{0,64},{64,0},{128,192},{192,128},{256,320},{320,256},{384,448},{4... | collective-permute-start | bytes 442376 | tf_op jit(solution)/shard_map/ppermute | solution.py:348
  27.9 28.1 %all-to-all-start.1 = ((bf16[8,8,1152]{2,1,0:T(8,128)(2,1)}), bf16[8,8,1152]{2,1,0:T(8,128)(2,1)S(1)}, u32[]{:S(2)}, u32[]{:S(2)}) async-start(bf16[8,8,1152]{2,1,0:T(8,128)(2,1)} %get-tuple-element.19), calls=%async_computation.1 | async-start | bytes 294912 | tf_op jit(solution)/shard_map/all_to_all | solution.py:70
  40.3 3.6 %collective-permute-start.2 = (bf16[2,64,512]{2,1,0:T(8,128)(2,1)}, bf16[2,64,512]{2,1,0:T(8,128)(2,1)S(1)}, u32[]{:S(2)}, u32[]{:S(2)}) collective-permute-start(bf16[2,64,512]{2,1,0:T(8,128)(2,1)} %get-tuple-element.21), channel_id=1, source_target_pairs={{0,64},{64,0},{128,192},{192,128},{256,320},{320,256},{384,448},{4... | collective-permute-start | bytes 393224 | tf_op jit(solution)/shard_map/ppermute | solution.py:384
  57.5 19.8 %all-to-all-start.2 = ((bf16[8,8,1152]{2,1,0:T(8,128)(2,1)}), bf16[8,8,1152]{2,1,0:T(8,128)(2,1)S(1)}, u32[]{:S(2)}, u32[]{:S(2)}) async-start(bf16[8,8,1152]{2,1,0:T(8,128)(2,1)} %get-tuple-element.22), calls=%async_computation.2 | async-start | bytes 294912 | tf_op jit(solution)/shard_map/all_to_all | solution.py:70
  78.6 21.7 %all-to-all-start.3 = ((bf16[8,8,1024]{2,1,0:T(8,128)(2,1)}), bf16[8,8,1024]{2,1,0:T(8,128)(2,1)S(1)}, u32[]{:S(2)}, u32[]{:S(2)}) async-start(bf16[8,8,1024]{2,1,0:T(8,128)(2,1)} %get-tuple-element.25), calls=%async_computation.3 | async-start | bytes 262144 | tf_op jit(solution)/shard_map/all_to_all | solution.py:70

commit v13 on v12

--- a/solution.py
+++ b/solution.py
@@ -9,7 +9,7 @@
 ITERS = 2
 LANES = 128
 SUMS_ORDER = (0, 4, 2, 6, 1, 5, 3, 7)
-LAST_ORDER = (0, 2, 6, 4, 1, 3, 7, 5)
+LAST_ORDER = (0, 4, 2, 6, 1, 5, 3, 7)
 
 
 shrink_rate = 0.5

time: 102 us -> 99.7 us (0.977)
  waiting for transfers between devices: 52.4 us -> 50.2 us
    all_to_all x3, waiting for transfers between devices: 45.2 us -> 43 us  [exchange(): lax.all_to_all(payload, 'rows', 0, 0, tiled=True, axis_index_groups=[list...]
where the time goes in v13:
time: 99.7 us; the launch traced here: 98.9 us
  waiting for transfers between devices  50.2 us (50%)
  starting transfers between devices  38.7 us (39%)
  Pallas kernels  7.77 us (8%)
    all_to_all x3, waiting for transfers between devices, exchange(): lax.all_to_all(payload, 'rows', 0, 0, tiled=True, axis_index_groups=[list...  43 us
    all_to_all x3, starting transfers between devices, exchange(): lax.all_to_all(payload, 'rows', 0, 0, tiled=True, axis_index_groups=[list...  20.7 us
    all_to_all x1, starting transfers between devices, shards(): lax.all_to_all(sent, 'feat', 0, 0, tiled=True, axis_index_groups=[listed])  11.7 us
    all_to_all x1, waiting for transfers between devices, shards(): lax.all_to_all(sent, 'feat', 0, 0, tiled=True, axis_index_groups=[listed])  5.96 us
    ppermute x1, starting transfers between devices, shards(): picked_taken = near(lax.ppermute(far_picked, 'rows', partners))  2.4 us
    pallas_call x1, Pallas kernels, shards(): call(pick_body, (pltpu.VMEM((feat_count, ITERS * samples // LANES, LANES)...  2.06 us
  transfers between devices with their start and end apart: 7, of which 5 were waited for; matrix products, arithmetic and copies ran while one was open for 0% of the time, Pallas kernels for 4%

profile of v13, /device:TPU:32, one launch (start us, length us, event | category | flops | bytes accessed | tf_op | source)
XLA Modules:
  0.0 98.9 jit_solution(908530244523376330)
XLA Ops:
  0.6 1.9 %collective-permute-start = (bf16[512,2048]{1,0:T(8,128)(2,1)}, bf16[512,2048]{1,0:T(8,128)(2,1)}, u32[]{:S(2)}, u32[]{:S(2)}) collective-permute-start(bf16[512,2048]{1,0:T(8,128)(2,1)} %geno_ref.3), channel_id=1, source_target_pairs={{0,64},{64,0},{128,192},{192,128},{256,320},{320,256},{384,448},{4... | collective-permute-start | bytes 6291464 | tf_op jit(solution)/shard_map/ppermute | solution.py:346
  2.6 0.0 copy-start
  2.6 0.7 copy-done
  3.2 2.1 %shard_map.59 = (bf16[64,8,128]{2,1,0:T(8,128)(2,1)}, f32[72,512]{1,0:T(8,128)S(1)}) custom-call(s32[2,64]{1,0:T(2,128)S(1)} %copy-done, bf16[512,2048]{1,0:T(8,128)(2,1)} %geno_ref.3, f32[64,512]{1,0:T(8,128)} %bitcast.21, s32[1,512]{1,0:T(1,128)} %bitcast.22), custom_call_target="tpu_custom_call" | custom-call | bytes 262144 | tf_op jit(solution)/shard_map/pallas_call | solution.py:329
  5.3 11.7 %all-to-all-start = ((bf16[64,8,128]{2,1,0:T(8,128)(2,1)}), bf16[64,8,128]{2,1,0:T(8,128)(2,1)S(1)}, u32[]{:S(2)}, u32[]{:S(2)}) async-start(bf16[64,8,128]{2,1,0:T(8,128)(2,1)} %get-tuple-element.14), calls=%async_computation | async-start | bytes 262144 | tf_op jit(solution)/shard_map/all_to_all | solution.py:344
  17.0 1.9 %collective-permute-start.1 = (f32[72,512]{1,0:T(8,128)S(1)}, f32[72,512]{1,0:T(8,128)S(1)}, u32[]{:S(2)}, u32[]{:S(2)}) collective-permute-start(f32[72,512]{1,0:T(8,128)S(1)} %get-tuple-element.15.state_ref), channel_id=1, source_target_pairs={{0,64},{64,0},{128,192},{192,128},{256,320},{320,256},{384,448},{4... | collective-permute-start | bytes 442376 | tf_op jit(solution)/shard_map/ppermute | solution.py:348
  18.9 0.0 collective-permute-done.far_taken_ref
  18.9 1.6 %shard_map.60 = (f32[64,1024]{1,0:T(8,128)S(1)}, bf16[1024,1024]{1,0:T(8,128)(2,1)S(1)}, bf16[2,64,64]{2,1,0:T(8,128)(2,1)S(1)}) custom-call(f32[72,512]{1,0:T(8,128)S(1)} %get-tuple-element.15.state_ref, bf16[512,2048]{1,0:T(8,128)(2,1)} %geno_ref.3, bf16[512,2048]{1,0:T(8,128)(2,1)} %collective-permute-done.far_taken_ref, s32[2,64]{1,0:T(2,128)} %far_win_ref.1), custom_call_target="tpu_custom_call" | custom-call | flops 67108864 | bytes 2097152 | tf_op jit(solution)/shard_map/pallas_call | solution.py:351
  20.5 0.0 collective-permute-done.1.state_taken_ref
  20.5 0.3 shard_map.61.table_ref
  20.9 6.0 %all-to-all-done.cols_ref = bf16[64,8,128]{2,1,0:T(8,128)(2,1)S(1)} async-done(((bf16[64,8,128]{2,1,0:T(8,128)(2,1)}), bf16[64,8,128]{2,1,0:T(8,128)(2,1)S(1)}, u32[]{:S(2)}, u32[]{:S(2)}) %all-to-all-start) | async-done | bytes 131104 | tf_op jit(solution)/shard_map/all_to_all | solution.py:344
  26.8 1.1 %shard_map.62 = (bf16[8,8,1152]{2,1,0:T(8,128)(2,1)}, bf16[2,64,512]{2,1,0:T(8,128)(2,1)S(1)}, bf16[2,64,512]{2,1,0:T(8,128)(2,1)}) custom-call(bf16[64,8,128]{2,1,0:T(8,128)(2,1)S(1)} %all-to-all-done.cols_ref, bf16[2,64,64]{2,1,0:T(8,128)(2,1)S(1)} %get-tuple-element.16.place_ref, f32[72,512]{1,0:T(8,128)S(1)} %get-tuple-element.15.state_ref, ...), custom_call_target="tpu_custom_call" | custom-call | bytes 2097152 | tf_op jit(solution)/shard_map/pallas_call | solution.py:372
  27.9 12.4 %all-to-all-start.1 = ((bf16[8,8,1152]{2,1,0:T(8,128)(2,1)}), bf16[8,8,1152]{2,1,0:T(8,128)(2,1)S(1)}, u32[]{:S(2)}, u32[]{:S(2)}) async-start(bf16[8,8,1152]{2,1,0:T(8,128)(2,1)} %get-tuple-element.19), calls=%async_computation.1 | async-start | bytes 294912 | tf_op jit(solution)/shard_map/all_to_all | solution.py:70
  40.3 2.4 %collective-permute-start.2 = (bf16[2,64,512]{2,1,0:T(8,128)(2,1)}, bf16[2,64,512]{2,1,0:T(8,128)(2,1)S(1)}, u32[]{:S(2)}, u32[]{:S(2)}) collective-permute-start(bf16[2,64,512]{2,1,0:T(8,128)(2,1)} %get-tuple-element.21), channel_id=1, source_target_pairs={{0,64},{64,0},{128,192},{192,128},{256,320},{320,256},{384,448},{4... | collective-permute-start | bytes 393224 | tf_op jit(solution)/shard_map/ppermute | solution.py:384
  42.7 1.2 %collective-permute-done.2.picked_taken_ref = bf16[2,64,512]{2,1,0:T(8,128)(2,1)S(1)} collective-permute-done((bf16[2,64,512]{2,1,0:T(8,128)(2,1)}, bf16[2,64,512]{2,1,0:T(8,128)(2,1)S(1)}, u32[]{:S(2)}, u32[]{:S(2)}) %collective-permute-start.2) | collective-permute-done | bytes 131104 | tf_op jit(solution)/shard_map/ppermute | solution.py:384
  43.9 12.1 %all-to-all-done.1.shared_ref = bf16[8,8,1152]{2,1,0:T(8,128)(2,1)S(1)} async-done(((bf16[8,8,1152]{2,1,0:T(8,128)(2,1)}), bf16[8,8,1152]{2,1,0:T(8,128)(2,1)S(1)}, u32[]{:S(2)}, u32[]{:S(2)}) %all-to-all-start.1) | async-done | bytes 147488 | tf_op jit(solution)/shard_map/all_to_all | solution.py:70
  56.0 1.4 %shard_map.63 = (bf16[8,8,1152]{2,1,0:T(8,128)(2,1)}, f32[64,128]{1,0:T(8,128)S(1)}) custom-call(bf16[8,8,1152]{2,1,0:T(8,128)(2,1)S(1)} %all-to-all-done.1.shared_ref, f32[72,512]{1,0:T(8,128)S(1)} %get-tuple-element.15.state_ref, f32[72,512]{1,0:T(8,128)S(1)} %collective-permute-done.1.state_taken_ref, ...), custom_call_target="tpu_custom_call" | custom-call | flops 134217728 | bytes 2097152 | tf_op jit(solution)/shard_map/pallas_call | solution.py:386
  57.5 4.1 %all-to-all-start.2 = ((bf16[8,8,1152]{2,1,0:T(8,128)(2,1)}), bf16[8,8,1152]{2,1,0:T(8,128)(2,1)S(1)}, u32[]{:S(2)}, u32[]{:S(2)}) async-start(bf16[8,8,1152]{2,1,0:T(8,128)(2,1)} %get-tuple-element.22), calls=%async_computation.2 | async-start | bytes 294912 | tf_op jit(solution)/shard_map/all_to_all | solution.py:70
  61.6 15.7 %all-to-all-done.2.shared_ref = bf16[8,8,1152]{2,1,0:T(8,128)(2,1)S(1)} async-done(((bf16[8,8,1152]{2,1,0:T(8,128)(2,1)}), bf16[8,8,1152]{2,1,0:T(8,128)(2,1)S(1)}, u32[]{:S(2)}, u32[]{:S(2)}) %all-to-all-start.2) | async-done | bytes 147488 | tf_op jit(solution)/shard_map/all_to_all | solution.py:70
  77.3 1.3 %shard_map.64 = (bf16[8,8,1024]{2,1,0:T(8,128)(2,1)}, f32[64,512]{1,0:T(8,128)}) custom-call(bf16[8,8,1152]{2,1,0:T(8,128)(2,1)S(1)} %all-to-all-done.2.shared_ref, f32[64,128]{1,0:T(8,128)S(1)} %get-tuple-element.23.coef_ref, f32[72,512]{1,0:T(8,128)S(1)} %get-tuple-element.15.state_ref, f32[72,512]{1,0:T(8,128)S(1)} %collective-permute-done.1.state_taken_ref, ...), custom_call_target="tpu_custom_call" | custom-call | flops 134217728 | bytes 2097152 | tf_op jit(solution)/shard_map/pallas_call | solution.py:396
  78.6 4.3 %all-to-all-start.3 = ((bf16[8,8,1024]{2,1,0:T(8,128)(2,1)}), bf16[8,8,1024]{2,1,0:T(8,128)(2,1)S(1)}, u32[]{:S(2)}, u32[]{:S(2)}) async-start(bf16[8,8,1024]{2,1,0:T(8,128)(2,1)} %get-tuple-element.25), calls=%async_computation.3 | async-start | bytes 262144 | tf_op jit(solution)/shard_map/all_to_all | solution.py:70
  82.9 15.2 %all-to-all-done.3 = bf16[8,8,1024]{2,1,0:T(8,128)(2,1)S(1)} async-done(((bf16[8,8,1024]{2,1,0:T(8,128)(2,1)}), bf16[8,8,1024]{2,1,0:T(8,128)(2,1)S(1)}, u32[]{:S(2)}, u32[]{:S(2)}) %all-to-all-start.3) | async-done | bytes 131104 | tf_op jit(solution)/shard_map/all_to_all | solution.py:70
  98.2 0.7 pad_maximum_fusion
  (8 shorter events, 0.1 us)
Async XLA Ops:
  0.6 18.3 %collective-permute-start = (bf16[512,2048]{1,0:T(8,128)(2,1)}, bf16[512,2048]{1,0:T(8,128)(2,1)}, u32[]{:S(2)}, u32[]{:S(2)}) collective-permute-start(bf16[512,2048]{1,0:T(8,128)(2,1)} %geno_ref.3), channel_id=1, source_target_pairs={{0,64},{64,0},{128,192},{192,128},{256,320},{320,256},{384,448},{4... | collective-permute-start | bytes 6291464 | tf_op jit(solution)/shard_map/ppermute | solution.py:346
  2.6 0.7 copy-start
  5.3 21.5 %all-to-all-start = ((bf16[64,8,128]{2,1,0:T(8,128)(2,1)}), bf16[64,8,128]{2,1,0:T(8,128)(2,1)S(1)}, u32[]{:S(2)}, u32[]{:S(2)}) async-start(bf16[64,8,128]{2,1,0:T(8,128)(2,1)} %get-tuple-element.14), calls=%async_computation | async-start | bytes 262144 | tf_op jit(solution)/shard_map/all_to_all | solution.py:344
  17.0 3.5 %collective-permute-start.1 = (f32[72,512]{1,0:T(8,128)S(1)}, f32[72,512]{1,0:T(8,128)S(1)}, u32[]{:S(2)}, u32[]{:S(2)}) collective-permute-start(f32[72,512]{1,0:T(8,128)S(1)} %get-tuple-element.15.state_ref), channel_id=1, source_target_pairs={{0,64},{64,0},{128,192},{192,128},{256,320},{320,256},{384,448},{4... | collective-permute-start | bytes 442376 | tf_op jit(solution)/shard_map/ppermute | solution.py:348
  27.9 28.1 %all-to-all-start.1 = ((bf16[8,8,1152]{2,1,0:T(8,128)(2,1)}), bf16[8,8,1152]{2,1,0:T(8,128)(2,1)S(1)}, u32[]{:S(2)}, u32[]{:S(2)}) async-start(bf16[8,8,1152]{2,1,0:T(8,128)(2,1)} %get-tuple-element.19), calls=%async_computation.1 | async-start | bytes 294912 | tf_op jit(solution)/shard_map/all_to_all | solution.py:70
  40.3 3.6 %collective-permute-start.2 = (bf16[2,64,512]{2,1,0:T(8,128)(2,1)}, bf16[2,64,512]{2,1,0:T(8,128)(2,1)S(1)}, u32[]{:S(2)}, u32[]{:S(2)}) collective-permute-start(bf16[2,64,512]{2,1,0:T(8,128)(2,1)} %get-tuple-element.21), channel_id=1, source_target_pairs={{0,64},{64,0},{128,192},{192,128},{256,320},{320,256},{384,448},{4... | collective-permute-start | bytes 393224 | tf_op jit(solution)/shard_map/ppermute | solution.py:384
  57.5 19.8 %all-to-all-start.2 = ((bf16[8,8,1152]{2,1,0:T(8,128)(2,1)}), bf16[8,8,1152]{2,1,0:T(8,128)(2,1)S(1)}, u32[]{:S(2)}, u32[]{:S(2)}) async-start(bf16[8,8,1152]{2,1,0:T(8,128)(2,1)} %get-tuple-element.22), calls=%async_computation.2 | async-start | bytes 294912 | tf_op jit(solution)/shard_map/all_to_all | solution.py:70
  78.6 19.5 %all-to-all-start.3 = ((bf16[8,8,1024]{2,1,0:T(8,128)(2,1)}), bf16[8,8,1024]{2,1,0:T(8,128)(2,1)S(1)}, u32[]{:S(2)}, u32[]{:S(2)}) async-start(bf16[8,8,1024]{2,1,0:T(8,128)(2,1)} %get-tuple-element.25), calls=%async_computation.3 | async-start | bytes 262144 | tf_op jit(solution)/shard_map/all_to_all | solution.py:70

commit v14 on v13

--- a/solution.py
+++ b/solution.py
@@ -195,7 +195,7 @@
     return copy
 
 
-def send_table(resid, resid_taken, both_ref, table_ref, out_ref, sem_ref, order, pieces=2):
+def send_table(resid, resid_taken, both_ref, table_ref, out_ref, sem_ref, order, pieces=1):
     width = table_ref.shape[2] // pieces
     copies = []
     for piece in range(pieces):

time: 99.7 us -> 99.8 us (level)
  no operation moved by 1% of the time
where the time goes in v14:
time: 99.8 us; the launch traced here: 98.9 us
  waiting for transfers between devices  50.2 us (50%)
  starting transfers between devices  38.7 us (39%)
  Pallas kernels  7.82 us (8%)
    all_to_all x3, waiting for transfers between devices, exchange(): lax.all_to_all(payload, 'rows', 0, 0, tiled=True, axis_index_groups=[list...  43 us
    all_to_all x3, starting transfers between devices, exchange(): lax.all_to_all(payload, 'rows', 0, 0, tiled=True, axis_index_groups=[list...  20.7 us
    all_to_all x1, starting transfers between devices, shards(): lax.all_to_all(sent, 'feat', 0, 0, tiled=True, axis_index_groups=[listed])  11.7 us
    all_to_all x1, waiting for transfers between devices, shards(): lax.all_to_all(sent, 'feat', 0, 0, tiled=True, axis_index_groups=[listed])  5.96 us
    ppermute x1, starting transfers between devices, shards(): picked_taken = near(lax.ppermute(far_picked, 'rows', partners))  2.4 us
    pallas_call x1, Pallas kernels, shards(): call(pick_body, (pltpu.VMEM((feat_count, ITERS * samples // LANES, LANES)...  2.06 us
  transfers between devices with their start and end apart: 7, of which 5 were waited for; matrix products, arithmetic and copies ran while one was open for 0% of the time, Pallas kernels for 4%

profile of v14, /device:TPU:32, one launch (start us, length us, event | category | flops | bytes accessed | tf_op | source)
XLA Modules:
  0.0 98.9 jit_solution(6639533511869763541)
XLA Ops:
  0.6 1.9 %collective-permute-start = (bf16[512,2048]{1,0:T(8,128)(2,1)}, bf16[512,2048]{1,0:T(8,128)(2,1)}, u32[]{:S(2)}, u32[]{:S(2)}) collective-permute-start(bf16[512,2048]{1,0:T(8,128)(2,1)} %geno_ref.3), channel_id=1, source_target_pairs={{0,64},{64,0},{128,192},{192,128},{256,320},{320,256},{384,448},{4... | collective-permute-start | bytes 6291464 | tf_op jit(solution)/shard_map/ppermute | solution.py:346
  2.6 0.0 copy-start
  2.6 0.7 copy-done
  3.2 2.1 %shard_map.59 = (bf16[64,8,128]{2,1,0:T(8,128)(2,1)}, f32[72,512]{1,0:T(8,128)S(1)}) custom-call(s32[2,64]{1,0:T(2,128)S(1)} %copy-done, bf16[512,2048]{1,0:T(8,128)(2,1)} %geno_ref.3, f32[64,512]{1,0:T(8,128)} %bitcast.21, s32[1,512]{1,0:T(1,128)} %bitcast.22), custom_call_target="tpu_custom_call" | custom-call | bytes 262144 | tf_op jit(solution)/shard_map/pallas_call | solution.py:329
  5.3 11.7 %all-to-all-start = ((bf16[64,8,128]{2,1,0:T(8,128)(2,1)}), bf16[64,8,128]{2,1,0:T(8,128)(2,1)S(1)}, u32[]{:S(2)}, u32[]{:S(2)}) async-start(bf16[64,8,128]{2,1,0:T(8,128)(2,1)} %get-tuple-element.14), calls=%async_computation | async-start | bytes 262144 | tf_op jit(solution)/shard_map/all_to_all | solution.py:344
  17.0 1.9 %collective-permute-start.1 = (f32[72,512]{1,0:T(8,128)S(1)}, f32[72,512]{1,0:T(8,128)S(1)}, u32[]{:S(2)}, u32[]{:S(2)}) collective-permute-start(f32[72,512]{1,0:T(8,128)S(1)} %get-tuple-element.15.state_ref), channel_id=1, source_target_pairs={{0,64},{64,0},{128,192},{192,128},{256,320},{320,256},{384,448},{4... | collective-permute-start | bytes 442376 | tf_op jit(solution)/shard_map/ppermute | solution.py:348
  18.9 0.0 collective-permute-done.far_taken_ref
  18.9 1.6 %shard_map.60 = (f32[64,1024]{1,0:T(8,128)S(1)}, bf16[1024,1024]{1,0:T(8,128)(2,1)S(1)}, bf16[2,64,64]{2,1,0:T(8,128)(2,1)S(1)}) custom-call(f32[72,512]{1,0:T(8,128)S(1)} %get-tuple-element.15.state_ref, bf16[512,2048]{1,0:T(8,128)(2,1)} %geno_ref.3, bf16[512,2048]{1,0:T(8,128)(2,1)} %collective-permute-done.far_taken_ref, s32[2,64]{1,0:T(2,128)} %far_win_ref.1), custom_call_target="tpu_custom_call" | custom-call | flops 67108864 | bytes 2097152 | tf_op jit(solution)/shard_map/pallas_call | solution.py:351
  20.5 0.0 collective-permute-done.1.state_taken_ref
  20.5 0.3 shard_map.61.table_ref
  20.9 6.0 %all-to-all-done.cols_ref = bf16[64,8,128]{2,1,0:T(8,128)(2,1)S(1)} async-done(((bf16[64,8,128]{2,1,0:T(8,128)(2,1)}), bf16[64,8,128]{2,1,0:T(8,128)(2,1)S(1)}, u32[]{:S(2)}, u32[]{:S(2)}) %all-to-all-start) | async-done | bytes 131104 | tf_op jit(solution)/shard_map/all_to_all | solution.py:344
  26.8 1.1 %shard_map.62 = (bf16[8,8,1152]{2,1,0:T(8,128)(2,1)}, bf16[2,64,512]{2,1,0:T(8,128)(2,1)S(1)}, bf16[2,64,512]{2,1,0:T(8,128)(2,1)}) custom-call(bf16[64,8,128]{2,1,0:T(8,128)(2,1)S(1)} %all-to-all-done.cols_ref, bf16[2,64,64]{2,1,0:T(8,128)(2,1)S(1)} %get-tuple-element.16.place_ref, f32[72,512]{1,0:T(8,128)S(1)} %get-tuple-element.15.state_ref, ...), custom_call_target="tpu_custom_call" | custom-call | bytes 2097152 | tf_op jit(solution)/shard_map/pallas_call | solution.py:372
  27.9 12.4 %all-to-all-start.1 = ((bf16[8,8,1152]{2,1,0:T(8,128)(2,1)}), bf16[8,8,1152]{2,1,0:T(8,128)(2,1)S(1)}, u32[]{:S(2)}, u32[]{:S(2)}) async-start(bf16[8,8,1152]{2,1,0:T(8,128)(2,1)} %get-tuple-element.19), calls=%async_computation.1 | async-start | bytes 294912 | tf_op jit(solution)/shard_map/all_to_all | solution.py:70
  40.3 2.4 %collective-permute-start.2 = (bf16[2,64,512]{2,1,0:T(8,128)(2,1)}, bf16[2,64,512]{2,1,0:T(8,128)(2,1)S(1)}, u32[]{:S(2)}, u32[]{:S(2)}) collective-permute-start(bf16[2,64,512]{2,1,0:T(8,128)(2,1)} %get-tuple-element.21), channel_id=1, source_target_pairs={{0,64},{64,0},{128,192},{192,128},{256,320},{320,256},{384,448},{4... | collective-permute-start | bytes 393224 | tf_op jit(solution)/shard_map/ppermute | solution.py:384
  42.7 1.2 %collective-permute-done.2.picked_taken_ref = bf16[2,64,512]{2,1,0:T(8,128)(2,1)S(1)} collective-permute-done((bf16[2,64,512]{2,1,0:T(8,128)(2,1)}, bf16[2,64,512]{2,1,0:T(8,128)(2,1)S(1)}, u32[]{:S(2)}, u32[]{:S(2)}) %collective-permute-start.2) | collective-permute-done | bytes 131104 | tf_op jit(solution)/shard_map/ppermute | solution.py:384
  43.9 12.1 %all-to-all-done.1.shared_ref = bf16[8,8,1152]{2,1,0:T(8,128)(2,1)S(1)} async-done(((bf16[8,8,1152]{2,1,0:T(8,128)(2,1)}), bf16[8,8,1152]{2,1,0:T(8,128)(2,1)S(1)}, u32[]{:S(2)}, u32[]{:S(2)}) %all-to-all-start.1) | async-done | bytes 147488 | tf_op jit(solution)/shard_map/all_to_all | solution.py:70
  56.0 1.4 %shard_map.63 = (bf16[8,8,1152]{2,1,0:T(8,128)(2,1)}, f32[64,128]{1,0:T(8,128)S(1)}) custom-call(bf16[8,8,1152]{2,1,0:T(8,128)(2,1)S(1)} %all-to-all-done.1.shared_ref, f32[72,512]{1,0:T(8,128)S(1)} %get-tuple-element.15.state_ref, f32[72,512]{1,0:T(8,128)S(1)} %collective-permute-done.1.state_taken_ref, ...), custom_call_target="tpu_custom_call" | custom-call | flops 134217728 | bytes 2097152 | tf_op jit(solution)/shard_map/pallas_call | solution.py:386
  57.5 4.1 %all-to-all-start.2 = ((bf16[8,8,1152]{2,1,0:T(8,128)(2,1)}), bf16[8,8,1152]{2,1,0:T(8,128)(2,1)S(1)}, u32[]{:S(2)}, u32[]{:S(2)}) async-start(bf16[8,8,1152]{2,1,0:T(8,128)(2,1)} %get-tuple-element.22), calls=%async_computation.2 | async-start | bytes 294912 | tf_op jit(solution)/shard_map/all_to_all | solution.py:70
  61.6 15.7 %all-to-all-done.2.shared_ref = bf16[8,8,1152]{2,1,0:T(8,128)(2,1)S(1)} async-done(((bf16[8,8,1152]{2,1,0:T(8,128)(2,1)}), bf16[8,8,1152]{2,1,0:T(8,128)(2,1)S(1)}, u32[]{:S(2)}, u32[]{:S(2)}) %all-to-all-start.2) | async-done | bytes 147488 | tf_op jit(solution)/shard_map/all_to_all | solution.py:70
  77.3 1.3 %shard_map.64 = (bf16[8,8,1024]{2,1,0:T(8,128)(2,1)}, f32[64,512]{1,0:T(8,128)}) custom-call(bf16[8,8,1152]{2,1,0:T(8,128)(2,1)S(1)} %all-to-all-done.2.shared_ref, f32[64,128]{1,0:T(8,128)S(1)} %get-tuple-element.23.coef_ref, f32[72,512]{1,0:T(8,128)S(1)} %get-tuple-element.15.state_ref, f32[72,512]{1,0:T(8,128)S(1)} %collective-permute-done.1.state_taken_ref, ...), custom_call_target="tpu_custom_call" | custom-call | flops 134217728 | bytes 2097152 | tf_op jit(solution)/shard_map/pallas_call | solution.py:396
  78.7 4.3 %all-to-all-start.3 = ((bf16[8,8,1024]{2,1,0:T(8,128)(2,1)}), bf16[8,8,1024]{2,1,0:T(8,128)(2,1)S(1)}, u32[]{:S(2)}, u32[]{:S(2)}) async-start(bf16[8,8,1024]{2,1,0:T(8,128)(2,1)} %get-tuple-element.25), calls=%async_computation.3 | async-start | bytes 262144 | tf_op jit(solution)/shard_map/all_to_all | solution.py:70
  83.0 15.2 %all-to-all-done.3 = bf16[8,8,1024]{2,1,0:T(8,128)(2,1)S(1)} async-done(((bf16[8,8,1024]{2,1,0:T(8,128)(2,1)}), bf16[8,8,1024]{2,1,0:T(8,128)(2,1)S(1)}, u32[]{:S(2)}, u32[]{:S(2)}) %all-to-all-start.3) | async-done | bytes 131104 | tf_op jit(solution)/shard_map/all_to_all | solution.py:70
  98.2 0.7 pad_maximum_fusion
  (8 shorter events, 0.1 us)
Async XLA Ops:
  0.6 18.3 %collective-permute-start = (bf16[512,2048]{1,0:T(8,128)(2,1)}, bf16[512,2048]{1,0:T(8,128)(2,1)}, u32[]{:S(2)}, u32[]{:S(2)}) collective-permute-start(bf16[512,2048]{1,0:T(8,128)(2,1)} %geno_ref.3), channel_id=1, source_target_pairs={{0,64},{64,0},{128,192},{192,128},{256,320},{320,256},{384,448},{4... | collective-permute-start | bytes 6291464 | tf_op jit(solution)/shard_map/ppermute | solution.py:346
  2.6 0.7 copy-start
  5.3 21.5 %all-to-all-start = ((bf16[64,8,128]{2,1,0:T(8,128)(2,1)}), bf16[64,8,128]{2,1,0:T(8,128)(2,1)S(1)}, u32[]{:S(2)}, u32[]{:S(2)}) async-start(bf16[64,8,128]{2,1,0:T(8,128)(2,1)} %get-tuple-element.14), calls=%async_computation | async-start | bytes 262144 | tf_op jit(solution)/shard_map/all_to_all | solution.py:344
  17.0 3.5 %collective-permute-start.1 = (f32[72,512]{1,0:T(8,128)S(1)}, f32[72,512]{1,0:T(8,128)S(1)}, u32[]{:S(2)}, u32[]{:S(2)}) collective-permute-start(f32[72,512]{1,0:T(8,128)S(1)} %get-tuple-element.15.state_ref), channel_id=1, source_target_pairs={{0,64},{64,0},{128,192},{192,128},{256,320},{320,256},{384,448},{4... | collective-permute-start | bytes 442376 | tf_op jit(solution)/shard_map/ppermute | solution.py:348
  27.9 28.1 %all-to-all-start.1 = ((bf16[8,8,1152]{2,1,0:T(8,128)(2,1)}), bf16[8,8,1152]{2,1,0:T(8,128)(2,1)S(1)}, u32[]{:S(2)}, u32[]{:S(2)}) async-start(bf16[8,8,1152]{2,1,0:T(8,128)(2,1)} %get-tuple-element.19), calls=%async_computation.1 | async-start | bytes 294912 | tf_op jit(solution)/shard_map/all_to_all | solution.py:70
  40.3 3.6 %collective-permute-start.2 = (bf16[2,64,512]{2,1,0:T(8,128)(2,1)}, bf16[2,64,512]{2,1,0:T(8,128)(2,1)S(1)}, u32[]{:S(2)}, u32[]{:S(2)}) collective-permute-start(bf16[2,64,512]{2,1,0:T(8,128)(2,1)} %get-tuple-element.21), channel_id=1, source_target_pairs={{0,64},{64,0},{128,192},{192,128},{256,320},{320,256},{384,448},{4... | collective-permute-start | bytes 393224 | tf_op jit(solution)/shard_map/ppermute | solution.py:384
  57.5 19.8 %all-to-all-start.2 = ((bf16[8,8,1152]{2,1,0:T(8,128)(2,1)}), bf16[8,8,1152]{2,1,0:T(8,128)(2,1)S(1)}, u32[]{:S(2)}, u32[]{:S(2)}) async-start(bf16[8,8,1152]{2,1,0:T(8,128)(2,1)} %get-tuple-element.22), calls=%async_computation.2 | async-start | bytes 294912 | tf_op jit(solution)/shard_map/all_to_all | solution.py:70
  78.7 19.5 %all-to-all-start.3 = ((bf16[8,8,1024]{2,1,0:T(8,128)(2,1)}), bf16[8,8,1024]{2,1,0:T(8,128)(2,1)S(1)}, u32[]{:S(2)}, u32[]{:S(2)}) async-start(bf16[8,8,1024]{2,1,0:T(8,128)(2,1)} %get-tuple-element.25), calls=%async_computation.3 | async-start | bytes 262144 | tf_op jit(solution)/shard_map/all_to_all | solution.py:70
